TPU v7x, 32 devices: a whole 2x2x4 slice. The times are simulated.
32 devices in a mesh: pairs: 8 (over y, x, core), rep: 4 (over z).
Axes of the slice: x: 2, y: 2, z: 4, core: 2. Of those that a mesh axis runs over, the one named last changes fastest.
Arguments:
- mat_val: bfloat16 [8192, 2048], P('pairs', 'rep'), may hold values from -6 to 6
- mat_cond: bfloat16 [1024, 2048], P('pairs', 'rep'), may hold values from -0.25 to 0.25
- screening: float32 [2048], P('rep'), may hold values from 0.2 to 2
- trial_cols: bfloat16 [1024, 256], P('pairs', 'rep'), may hold values from -0.09375 to 0.09375
- trial_rows: bfloat16 [8192, 256], P('pairs', 'rep'), may hold values from -6 to 6
- row_map: int32 [8192], replicated, may hold values from 0 to 8191, as said below
- val_index: int32 [8192], P('pairs'), may hold values from 0 to 127
- cond_index: int32 [8192], P('pairs'), may hold values from 0 to 255
- val_energy: float32 [128], replicated, may hold values from -1.5 to -0.25
- cond_energy: float32 [256], replicated, may hold values from 0.25 to 1.5
Outputs:
- response: bfloat16 [8192, 256], P('pairs', 'rep')
- kernel_tiles: bfloat16 [4, 8192, 1024], P('rep', 'pairs')
Inputs may be any that keep to these rules, and one draw needn't show every extreme that they name: row_map is a permutation of the rows; of the 1024 rows of each aligned block, exactly 128 have values in each aligned block of 1024 values.
All inputs are finite; a program needn't handle non-finite values.
Results may differ from a plain program's by a relative error of at most 0.005.
Values may be sent and summed in bfloat16 or wider, within the bound.
No kernel may reach another device: no remote copies, remote signals or barrier semaphores. Data moves between devices by JAX's collectives and lax.ppermute only.
A program may use at most 64 MiB of HBM per device.

v0:
```python
import jax
import jax.numpy as jnp
from jax import lax
from jax.experimental import pallas as pl
from jax.experimental.pallas import tpu as pltpu
from jax.sharding import PartitionSpec as P

F32 = jnp.float32
BF16 = jnp.bfloat16
SCALAR = pl.BlockSpec(memory_space=pltpu.SMEM)
WHOLE = pl.BlockSpec(memory_space=pltpu.VMEM)


def roomy(mib):
    return pltpu.CompilerParams(vmem_limit_bytes=mib << 20)


def exchange(x, axis, mask):
    size = lax.axis_size(axis)
    return lax.ppermute(x, axis, [(i, i ^ mask) for i in range(size)])


def split_exchange(x, even_mask, odd_mask):
    size = lax.axis_size("pairs")
    return lax.ppermute(x, "pairs", [(i, i ^ (odd_mask if i & 1 else even_mask)) for i in range(size)])


def in_order(odd, own, partner):
    return jnp.where(odd, jnp.stack([partner, own]), jnp.stack([own, partner]))


def lane_cumsum(x):
    width = x.shape[1]
    lane = lax.broadcasted_iota(jnp.int32, x.shape, 1)
    step = 1
    while step < width:
        x = x + jnp.where(lane >= step, pltpu.roll(x, step, 1), 0)
        step *= 2
    return x


def lookup(table_ref, index):
    value = jnp.zeros(index.shape, F32)
    for part in range(table_ref.shape[0]):
        row = jnp.broadcast_to(table_ref[part : part + 1, :], index.shape)
        near = jnp.clip(index - 128 * part, 0, 127)
        found = jnp.take_along_axis(row, near, axis=1)
        value = jnp.where(index // 128 == part, found, value)
    return value


def load_kernel(n, me_ref, map_hbm, val_hbm, screen_hbm, scaled_ref, order_ref, map_ref, val_ref, screen_ref, sems):
    rows = val_ref.shape[0]
    per_peer = rows // n
    lanes = rows // 128
    tall = rows // 4
    first = pl.multiple_of(me_ref[0] * lanes, lanes)
    head = [
        pltpu.make_async_copy(screen_hbm, screen_ref, sems.at[0]),
        pltpu.make_async_copy(map_hbm.at[pl.ds(first, lanes), :], map_ref, sems.at[1]),
    ]
    body = [
        pltpu.make_async_copy(
            val_hbm.at[pl.ds(k * tall, tall), :], val_ref.at[pl.ds(k * tall, tall), :], sems.at[2 + k])
        for k in range(4)
    ]
    for copy in head + body:
        copy.start()
    for copy in head:
        copy.wait()
    own = jnp.concatenate([map_ref[c : c + 1, :] for c in range(lanes)], axis=1)
    own = jnp.broadcast_to(own, (n, rows))
    block = lax.broadcasted_iota(jnp.int32, (n, rows), 0)
    goes = (own >= block * rows) & (own < (block + 1) * rows)
    rank = lane_cumsum(goes.astype(jnp.int32)) - 1
    order_ref[...] = jnp.sum(jnp.where(goes, rank + block * per_peer, 0), axis=0, keepdims=True)
    for k, copy in enumerate(body):
        copy.wait()
        part = slice(k * tall, (k + 1) * tall)
        scaled_ref[part, :] = (val_ref[part, :].astype(F32) * screen_ref[...]).astype(BF16)


def sent_kernel(first, order_ref, scaled_ref, sent_ref):
    rows = scaled_ref.shape[0]
    chunk = 128
    for c in range(sent_ref.shape[0] // chunk):
        ids = lax.broadcasted_iota(jnp.int32, (chunk, rows), 0) + (first + c * chunk)
        pick = jnp.where(ids == order_ref[...], 1.0, 0.0).astype(BF16)
        sent_ref[c * chunk : (c + 1) * chunk, :] = jnp.dot(
            pick, scaled_ref[...], preferred_element_type=F32
        ).astype(BF16)


def place_kernel(n, rows, me_ref, map_ref, ci_ref, vi_ref, ce_ref, ve_ref, place_ref, gap_ref):
    per_peer = rows // n
    lanes = rows // 128
    gap_ref[...] = lookup(ce_ref, ci_ref[...]) - lookup(ve_ref, vi_ref[...])
    grid = jnp.concatenate([map_ref[pl.ds(c, n, stride=lanes), :] for c in range(lanes)], axis=1)
    slots = grid - me_ref[0] * rows
    lands = (slots >= 0) & (slots < rows)
    arrival = jnp.where(lands, lane_cumsum(lands.astype(jnp.int32)) - 1, -1)
    slots = slots.astype(F32)
    ids = lax.broadcasted_iota(jnp.int32, (per_peer, rows), 0)
    lane = lax.broadcasted_iota(jnp.int32, (per_peer, rows), 1).astype(F32)
    for q in range(n):
        hit = ids == arrival[q : q + 1, :]
        slot = jnp.sum(jnp.where(hit, slots[q : q + 1, :], 0.0), axis=1, keepdims=True)
        place_ref[q * per_peer : (q + 1) * per_peer, :] = jnp.where(slot == lane, 1.0, 0.0).astype(BF16)


def tile_kernel(me_ref, scaled_ref, cond_ref, out_ref):
    chips, _, cols, depth = cond_ref.shape
    chip = me_ref[0] // 2
    for k in range(chips):
        tile = lax.dot_general(
            scaled_ref[...],
            cond_ref[k].reshape(2 * cols, depth),
            (((1,), (1,)), ((), ())),
            preferred_element_type=F32,
        )
        start = pl.multiple_of((chip ^ k) * (2 * cols), 128)
        out_ref[0, :, pl.ds(start, 2 * cols)] = tile.astype(BF16)


def apply_kernel(m, n, me_ref, mixed_ref, *refs):
    shares = (len(refs) - 1) // 2
    out_ref = refs[-1]
    half, width = out_ref.shape[1:]
    per_peer = width // 2
    odd = (me_ref[0] & 1) == 1
    for share in range(shares):
        own, other = (
            lax.dot_general(
                mixed_ref[...], ref[...], (((1,), (1,)), ((), ())), preferred_element_type=F32
            ).astype(BF16)
            for ref in (refs[share], refs[shares + share])
        )
        first, second = jnp.where(odd, other, own), jnp.where(odd, own, other)
        for d in range(n // shares):
            part = slice(d * per_peer, (d + 1) * per_peer)
            for k in range(m):
                to = ((share * n) // shares + d) * m + k
                out_ref[to, :, :per_peer] = first[k * half : (k + 1) * half, part]
                out_ref[to, :, per_peer:] = second[k * half : (k + 1) * half, part]


def final_kernel(n, m, arrived_ref, place_ref, gap_ref, trial_ref, out_ref, row_ref):
    width = out_ref.shape[1]
    half, pair = arrived_ref.shape[1:]
    for q in range(n):
        total = arrived_ref[q * m].astype(F32)
        for k in range(1, m):
            total = total + arrived_ref[q * m + k].astype(F32)
        at = (q & 1) * half
        row_ref[at : at + half, (q // 2) * pair : (q // 2 + 1) * pair] = total.astype(BF16)
    moved = jnp.dot(row_ref[...], place_ref[...], preferred_element_type=F32)
    for c in range(width // 128):
        part = slice(c * 128, (c + 1) * 128)
        gap = gap_ref[c : c + 1, :]
        out_ref[:, part] = (gap * trial_ref[:, part].astype(F32) + moved[:, part]).astype(BF16)


def cond_gather(both, odd):
    n = lax.axis_size("pairs")
    if n != 8:
        every = both[None]
        mask = 2
        while mask < n:
            every = jnp.concatenate([every, exchange(every, "pairs", mask)])
            mask *= 2
        return every
    far = split_exchange(both, 2, 4)
    corner = split_exchange(jnp.where(odd, far[1], far[0]), 4, 2)
    mine = jnp.concatenate([far, corner[None]])
    other = exchange(mine, "pairs", 1)
    first, second = jnp.where(odd, other, mine), jnp.where(odd, mine, other)
    return jnp.stack([both, first[:2], second[:2], jnp.stack([first[2], second[2]])])


def per_device(
    mat_val,
    mat_cond,
    screening,
    trial_cols,
    trial_rows,
    row_map,
    val_index,
    cond_index,
    val_energy,
    cond_energy,
):
    n = lax.axis_size("pairs")
    m = lax.axis_size("rep")
    rows, depth = mat_val.shape
    cols = mat_cond.shape[0]
    vecs = trial_cols.shape[1]
    half = vecs // 2
    per_peer = rows // n
    own = lax.axis_index("pairs").astype(jnp.int32)
    layer = lax.axis_index("rep").astype(jnp.int32)
    odd = (own & 1) == 1
    me = own.reshape(1)
    screen = screening.reshape(1, depth)
    map_lanes = row_map.reshape(-1, 128)

    trial = trial_cols.T
    low, high = trial[:half], trial[half:]
    got = exchange(jnp.where(odd, low, high), "pairs", 1)
    vec = in_order(odd, jnp.where(odd, high, low), got)
    vec = vec.transpose(1, 0, 2).reshape(half, 2 * cols)
    turns = [vec]
    for k in range(1, m):
        turns.append(lax.ppermute(vec, "rep", [(i, (i + k) % m) for i in range(m)]))
    vec_all = []
    for k in range(m):
        block = turns[0]
        for t in range(1, m):
            block = jnp.where(lax.rem(layer - t + m, m) == k, turns[t], block)
        vec_all.append(block)
    vec_all = jnp.concatenate(vec_all)

    both = in_order(odd, mat_cond, exchange(mat_cond, "pairs", 1))

    shares = 2
    far_away = pl.BlockSpec(memory_space=pltpu.HBM)
    scaled, order = pl.pallas_call(
        lambda *refs: load_kernel(n, *refs),
        in_specs=[SCALAR, far_away, far_away, far_away],
        out_specs=(WHOLE, WHOLE),
        out_shape=(
            jax.ShapeDtypeStruct((rows, depth), BF16),
            jax.ShapeDtypeStruct((1, rows), jnp.int32),
        ),
        scratch_shapes=[
            pltpu.VMEM((rows // 128, 128), jnp.int32),
            pltpu.VMEM((rows, depth), BF16),
            pltpu.VMEM((1, depth), F32),
            pltpu.SemaphoreType.DMA((6,)),
        ],
        cost_estimate=pl.CostEstimate(flops=rows * depth, bytes_accessed=4 * rows * depth, transcendentals=0),
        compiler_params=roomy(12),
        name="load",
    )(me, *(pltpu.with_memory_space_constraint(x, pltpu.HBM) for x in (map_lanes, mat_val, screen)))
    shares = 1
    sent = [pl.pallas_call(
        lambda *refs, share=share: sent_kernel(share * (rows // shares), *refs),
        in_specs=[WHOLE, WHOLE],
        out_specs=WHOLE,
        out_shape=jax.ShapeDtypeStruct((rows // shares, depth), BF16),
        cost_estimate=pl.CostEstimate(
            flops=2 * rows * rows * depth // shares, bytes_accessed=4 * rows * depth, transcendentals=0),
        compiler_params=roomy(12),
    )(order, scaled) for share in range(shares)]
    sent_other = [exchange(part, "pairs", 1) for part in sent]

    mixed = jnp.dot(vec_all, both.reshape(2 * cols, depth), preferred_element_type=F32)
    masks = [2**b for b in range(1, n.bit_length() - 1)]
    for even_mask, odd_mask in zip(masks, masks[::-1]):
        mixed = mixed + split_exchange(mixed.astype(BF16), even_mask, odd_mask).astype(F32)
    mixed = mixed.astype(BF16)
    if per_peer % 128 == 0:
        outgoing = pl.pallas_call(
            lambda *refs: apply_kernel(m, n, *refs),
            in_specs=[SCALAR] + [WHOLE] * (1 + 2 * shares),
            out_specs=WHOLE,
            compiler_params=roomy(12),
            out_shape=jax.ShapeDtypeStruct((n * m, half, 2 * per_peer), BF16),
            cost_estimate=pl.CostEstimate(
                flops=4 * rows * depth * m * half, bytes_accessed=4 * rows * depth, transcendentals=0),
            name="apply",
        )(me, mixed, *sent, *sent_other)
    else:
        rows_both = in_order(odd, jnp.concatenate(sent), jnp.concatenate(sent_other))
        rows_both = rows_both.reshape(2, n, per_peer, depth).transpose(1, 0, 2, 3).reshape(2 * rows, depth)
        partial = lax.dot_general(
            mixed, rows_both, (((1,), (1,)), ((), ())), preferred_element_type=F32
        ).astype(BF16)
        outgoing = partial.reshape(m, half, n, 2 * per_peer).transpose(2, 0, 1, 3)
        outgoing = outgoing.reshape(n * m, half, 2 * per_peer)
    arrived = lax.all_to_all(outgoing, ("pairs", "rep"), split_axis=0, concat_axis=0, tiled=True)

    cond_all = cond_gather(both, odd)
    tall = min(rows, 256)
    tiles = pl.pallas_call(
        tile_kernel,
        grid_spec=pltpu.PrefetchScalarGridSpec(
            num_scalar_prefetch=1,
            grid=(rows // tall,),
            in_specs=[
                pl.BlockSpec((tall, depth), lambda d, me: (d, 0)),
                pl.BlockSpec((n // 2, 2, cols, depth), lambda d, me: (0, 0, 0, 0)),
            ],
            out_specs=pl.BlockSpec((1, tall, n * cols), lambda d, me: (0, d, 0)),
        ),
        out_shape=jax.ShapeDtypeStruct((1, rows, n * cols), BF16),
        cost_estimate=pl.CostEstimate(
            flops=2 * rows * depth * n * cols, bytes_accessed=2 * rows * (depth + n * cols), transcendentals=0),
        compiler_params=roomy(16),
        name="tiles",
    )(me, scaled, cond_all)

    place, gap = pl.pallas_call(
        lambda *refs: place_kernel(n, rows, *refs),
        in_specs=[SCALAR] + [WHOLE] * 5,
        out_specs=(WHOLE, WHOLE),
        out_shape=(
            jax.ShapeDtypeStruct((rows, rows), BF16),
            jax.ShapeDtypeStruct((rows // 128, 128), F32),
        ),
        cost_estimate=pl.CostEstimate(
            flops=8 * rows * rows, bytes_accessed=2 * rows * rows, transcendentals=0),
        compiler_params=roomy(12),
        name="place",
    )(
        me,
        map_lanes,
        cond_index.reshape(-1, 128),
        val_index.reshape(-1, 128),
        cond_energy.reshape(-1, 128),
        val_energy.reshape(-1, 128),
    )

    if per_peer % 128 != 0:
        arrived = jnp.sum(arrived.reshape(n // 2, 2, m, half, 2 * per_peer).astype(F32), axis=2).astype(BF16)
        arrived = arrived.transpose(1, 2, 0, 3).reshape(2, half, rows)
    parts, layers = (n, m) if per_peer % 128 == 0 else (2, 1)
    response = pl.pallas_call(
        lambda *refs: final_kernel(parts, layers, *refs),
        in_specs=[WHOLE] * 4,
        out_specs=WHOLE,
        compiler_params=roomy(12),
        out_shape=jax.ShapeDtypeStruct((vecs, rows), BF16),
        scratch_shapes=[pltpu.VMEM((vecs, rows), BF16)],
        cost_estimate=pl.CostEstimate(
            flops=2 * rows * rows * vecs, bytes_accessed=2 * rows * rows, transcendentals=0),
        name="final",
    )(arrived, place, gap, trial_rows.T)
    return (response.T, tiles)


def solution(mesh):
    in_specs = (
        P("pairs", "rep"),
        P("pairs", "rep"),
        P("rep"),
        P("pairs", "rep"),
        P("pairs", "rep"),
        P(),
        P("pairs"),
        P("pairs"),
        P(),
        P(),
    )
    out_specs = (P("pairs", "rep"), P("rep", "pairs", None))

    return jax.shard_map(per_device, mesh=mesh, in_specs=in_specs, out_specs=out_specs, check_vma=False)
```

profile of v0, /device:TPU:1, one launch (start us, length us, event | category | flops | bytes accessed | tf_op | source)
XLA Modules:
  0.0 48.7 jit_solution(7469342522160842666)
XLA Ops:
  0.7 0.7 %broadcast_select_fusion.2 = (bf16[32,128]{1,0:T(8,128)(2,1)S(1)}, bf16[1,32,128]{2,1,0:T(8,128)(2,1)S(1)}) fusion(pred[]{:T(512)S(6)} %eq.40, bf16[64,128]{1,0:T(8,128)(2,1)} %bitcast.60), kind=kLoop, calls=%fused_computation.30 | loop fusion | flops 8192 | bytes 32769 | tf_op jit(solution)/shard_map/jit(_where)/select_n | solution.py:208
  1.4 0.5 collective-permute-start
  1.9 1.5 %load.1 = (bf16[1024,512]{1,0:T(8,128)(2,1)S(1)}, s32[1,1024]{1,0:T(1,128)S(1)}) custom-call(s32[1]{0:T(128)} %bitcast.refs_0_.me_ref, s32[64,128]{1,0:T(8,128)} %bitcast.44, bf16[1024,512]{1,0:T(8,128)(2,1)} %refs_2_.1, f32[1,512]{1,0:T(1,128)} %bitcast.61), custom_call_target="tpu_custom_call" | custom-call | flops 524288 | bytes 2097152 | tf_op jit(solution)/shard_map/load/pallas_call | solution.py:226
  3.4 1.3 %shard_map.113.refs_2_ = bf16[1024,512]{1,0:T(8,128)(2,1)S(1)} custom-call(s32[1,1024]{1,0:T(1,128)S(1)} %get-tuple-element.6.refs_0_, bf16[1024,512]{1,0:T(8,128)(2,1)S(1)} %get-tuple-element.7.refs_1_.scaled_ref), custom_call_target="tpu_custom_call" | custom-call | flops 1073741824 | bytes 2097152 | tf_op jit(solution)/shard_map/pallas_call | solution.py:245
  4.7 1.0 %copy-done = bf16[1024,512]{1,0:T(8,128)(2,1)} copy-done((bf16[1024,512]{1,0:T(8,128)(2,1)}, bf16[1024,512]{1,0:T(8,128)(2,1)S(1)}, u32[]{:S(2)}) %copy-start) | copy-done | bytes 1048600
  5.7 4.8 %collective-permute-start.1 = (bf16[32,256]{1,0:T(8,128)(2,1)S(1)}, bf16[32,256]{1,0:T(8,128)(2,1)S(1)}, u32[]{:S(2)}, u32[]{:S(2)}) collective-permute-start(bf16[32,256]{1,0:T(8,128)(2,1)S(1)} %copy_bitcast_fusion), channel_id=1, source_target_pairs={{0,3},{1,0},{2,1},{3,2},{4,7},{5,4},{6,5},{7,6},{8,11},{9,8},{10,9... | collective-permute-start | bytes 49160 | tf_op jit(solution)/shard_map/ppermute | solution.py:213
  11.0 1.3 %collective-permute-start.8 = (bf16[2,128,512]{2,1,0:T(8,128)(2,1)S(1)}, bf16[2,128,512]{2,1,0:T(8,128)(2,1)S(1)}, u32[]{:S(2)}, u32[]{:S(2)}) collective-permute-start(bf16[2,128,512]{2,1,0:T(8,128)(2,1)S(1)} %maximum_select_fusion), channel_id=1, source_target_pairs={{0,8},{4,20},{8,0},{12,28},{16,24},{20,4},{24,16},{28,12},{1,9},{5... | collective-permute-start | bytes 786440 | tf_op jit(solution)/shard_map/ppermute | solution.py:25
  12.3 1.7 %collective-permute-done.2 = bf16[32,256]{1,0:T(8,128)(2,1)S(1)} collective-permute-done((bf16[32,256]{1,0:T(8,128)(2,1)S(1)}, bf16[32,256]{1,0:T(8,128)(2,1)S(1)}, u32[]{:S(2)}, u32[]{:S(2)}) %collective-permute-start.2) | collective-permute-done | bytes 16416 | tf_op jit(solution)/shard_map/ppermute | solution.py:213
  14.0 0.9 %collective-permute-done.3 = bf16[32,256]{1,0:T(8,128)(2,1)S(1)} collective-permute-done((bf16[32,256]{1,0:T(8,128)(2,1)S(1)}, bf16[32,256]{1,0:T(8,128)(2,1)S(1)}, u32[]{:S(2)}, u32[]{:S(2)}) %collective-permute-start.3) | collective-permute-done | bytes 16416 | tf_op jit(solution)/shard_map/ppermute | solution.py:213
  15.2 1.3 %collective-permute-start.5 = (bf16[128,512]{1,0:T(8,128)(2,1)S(1)}, bf16[128,512]{1,0:T(8,128)(2,1)S(1)}, u32[]{:S(2)}, u32[]{:S(2)}) collective-permute-start(bf16[128,512]{1,0:T(8,128)(2,1)S(1)} %get-tuple-element.18), channel_id=1, source_target_pairs={{0,8},{4,20},{8,0},{12,28},{16,24},{20,4},{24,16},{28,12},{1,9},{5... | collective-permute-start | bytes 393224 | tf_op jit(solution)/shard_map/ppermute | solution.py:25
  16.6 1.3 %collective-permute-start.9 = (bf16[128,512]{1,0:T(8,128)(2,1)S(1)}, bf16[128,512]{1,0:T(8,128)(2,1)S(1)}, u32[]{:S(2)}, u32[]{:S(2)}) collective-permute-start(bf16[128,512]{1,0:T(8,128)(2,1)S(1)} %fusion.1), channel_id=1, source_target_pairs={{0,16},{4,12},{8,24},{12,4},{16,0},{20,28},{24,8},{28,20},{1,17},{... | collective-permute-start | bytes 393224 | tf_op jit(solution)/shard_map/ppermute | solution.py:25
  17.9 1.2 %collective-permute-done.5 = bf16[128,512]{1,0:T(8,128)(2,1)S(1)} collective-permute-done((bf16[128,512]{1,0:T(8,128)(2,1)S(1)}, bf16[128,512]{1,0:T(8,128)(2,1)S(1)}, u32[]{:S(2)}, u32[]{:S(2)}) %collective-permute-start.5) | collective-permute-done | bytes 131104 | tf_op jit(solution)/shard_map/ppermute | solution.py:25
  19.1 1.3 %collective-permute-start.6 = (bf16[128,512]{1,0:T(8,128)(2,1)S(1)}, bf16[128,512]{1,0:T(8,128)(2,1)S(1)}, u32[]{:S(2)}, u32[]{:S(2)}) collective-permute-start(bf16[128,512]{1,0:T(8,128)(2,1)S(1)} %fusion), channel_id=1, source_target_pairs={{0,16},{4,12},{8,24},{12,4},{16,0},{20,28},{24,8},{28,20},{1,17},{... | collective-permute-start | bytes 393224 | tf_op jit(solution)/shard_map/ppermute | solution.py:25
  20.4 1.4 %collective-permute-done.9 = bf16[128,512]{1,0:T(8,128)(2,1)S(1)} collective-permute-done((bf16[128,512]{1,0:T(8,128)(2,1)S(1)}, bf16[128,512]{1,0:T(8,128)(2,1)S(1)}, u32[]{:S(2)}, u32[]{:S(2)}) %collective-permute-start.9) | collective-permute-done | bytes 131104 | tf_op jit(solution)/shard_map/ppermute | solution.py:25
  21.8 0.8 %pad_maximum_fusion.1 = bf16[3,128,512]{2,1,0:T(8,128)(2,1)} fusion(bf16[1,128,512]{2,1,0:T(8,128)(2,1)S(1)} %bitcast.55, bf16[2,128,512]{2,1,0:T(8,128)(2,1)S(1)} %collective-permute-done.8), kind=kLoop, calls=%fused_computation.1 | loop fusion | flops 196608 | bytes 786432 | tf_op jit(solution)/shard_map/concatenate | solution.py:174
  22.6 2.8 %collective-permute-start.10 = (bf16[3,128,512]{2,1,0:T(8,128)(2,1)}, bf16[3,128,512]{2,1,0:T(8,128)(2,1)}, u32[]{:S(2)}, u32[]{:S(2)}) collective-permute-start(bf16[3,128,512]{2,1,0:T(8,128)(2,1)} %pad_maximum_fusion.1), channel_id=1, source_target_pairs={{0,4},{4,0},{8,12},{12,8},{16,20},{20,16},{24,28},{28,24},{1,5},{5... | collective-permute-start | bytes 1179656 | tf_op jit(solution)/shard_map/ppermute | solution.py:20
  25.5 1.6 %apply.1 = bf16[32,32,256]{2,1,0:T(8,128)(2,1)} custom-call(s32[1]{0:T(128)} %bitcast.refs_0_.me_ref, bf16[128,512]{1,0:T(8,128)(2,1)S(1)} %add_convert_fusion.refs_1_, bf16[1024,512]{1,0:T(8,128)(2,1)S(1)} %shard_map.113.refs_2_, bf16[1024,512]{1,0:T(8,128)(2,1)S(1)} %collective-permute-done.7.refs_3_), custom_call_target="tpu_custom_call" | custom-call | flops 268435456 | bytes 2097152 | tf_op jit(solution)/shard_map/apply/pallas_call | solution.py:262
  27.1 5.2 %all-to-all-start = ((bf16[32,32,256]{2,1,0:T(8,128)(2,1)}), bf16[32,32,256]{2,1,0:T(8,128)(2,1)S(1)}, u32[]{:S(2)}, u32[]{:S(2)}) async-start(bf16[32,32,256]{2,1,0:T(8,128)(2,1)} %apply.1), calls=%async_computation | async-start | bytes 1048576 | tf_op jit(solution)/shard_map/all_to_all | solution.py:280
  32.4 1.4 %place.1 = (bf16[1024,1024]{1,0:T(8,128)(2,1)S(1)}, f32[8,128]{1,0:T(8,128)S(1)}) custom-call(s32[1]{0:T(128)} %bitcast.refs_0_.me_ref, s32[64,128]{1,0:T(8,128)S(1)} %bitcast.45, s32[8,128]{1,0:T(8,128)S(1)} %bitcast.46, s32[8,128]{1,0:T(8,128)S(1)} %bitcast.47, f32[2,128]{1,0:T(2,128)S(1)} %bitcast.48, f32[1,128]{1,0:T(1,128)S(1)} %bitcast.49), custom_call_target="tpu_custom_call" | custom-call | flops 8388608 | bytes 2097152 | tf_op jit(solution)/shard_map/place/pallas_call | solution.py:302
  33.8 1.1 %broadcast_select_fusion.1 = (bf16[3,128,512]{2,1,0:T(8,128)(2,1)S(1)}, bf16[3,128,512]{2,1,0:T(8,128)(2,1)S(1)}) fusion(bf16[3,128,512]{2,1,0:T(8,128)(2,1)} %collective-permute-done.10, pred[]{:T(512)S(6)} %eq.40, bf16[1,128,512]{2,1,0:T(8,128)(2,1)S(1)} %bitcast.56, bf16[2,128,512]{2,1,0:T(8,128)(2,1)S(1)} %collective-permute-done.8), kind=kLoop, calls=%fused_computation.3 | loop fusion | flops 589824 | bytes 1572865 | tf_op jit(solution)/shard_map/jit(_where)/select_n | solution.py:176
  35.2 1.0 %copy-done.1 = bf16[1024,512]{1,0:T(8,128)(2,1)S(1)} copy-done((bf16[1024,512]{1,0:T(8,128)(2,1)S(1)}, bf16[1024,512]{1,0:T(8,128)(2,1)}, u32[]{:S(2)}) %copy-start.1) | copy-done | bytes 1048600
  36.1 3.1 %tiles.1 = bf16[1,1024,1024]{2,1,0:T(8,128)(2,1)} custom-call(s32[1]{0:T(128)} %bitcast.refs_0_.me_ref, bf16[1024,512]{1,0:T(8,128)(2,1)S(1)} %copy-done.1, bf16[4,2,128,512]{3,2,1,0:T(8,128)(2,1)S(1)} %pad_maximum_fusion.cond_ref), custom_call_target="tpu_custom_call" | custom-call | flops 1073741824 | bytes 3145728 | tf_op jit(solution)/shard_map/tiles/pallas_call | solution.py:284
  39.2 8.4 %all-to-all-done.refs_0_ = bf16[32,32,256]{2,1,0:T(8,128)(2,1)S(1)} async-done(((bf16[32,32,256]{2,1,0:T(8,128)(2,1)}), bf16[32,32,256]{2,1,0:T(8,128)(2,1)S(1)}, u32[]{:S(2)}, u32[]{:S(2)}) %all-to-all-start) | async-done | bytes 524320 | tf_op jit(solution)/shard_map/all_to_all | solution.py:280
  47.6 1.1 %final.1 = bf16[64,1024]{1,0:T(8,128)(2,1)} custom-call(bf16[32,32,256]{2,1,0:T(8,128)(2,1)S(1)} %all-to-all-done.refs_0_, bf16[1024,1024]{1,0:T(8,128)(2,1)S(1)} %get-tuple-element.8.refs_1_, f32[8,128]{1,0:T(8,128)S(1)} %get-tuple-element.9.refs_2_, bf16[64,1024]{1,0:T(8,128)(2,1)S(1)} %bitcast.43), custom_call_target="tpu_custom_call" | custom-call | flops 134217728 | bytes 2097152 | tf_op jit(solution)/shard_map/final/pallas_call | solution.py:327
  (40 shorter events, 1.3 us)
Async XLA Ops:
  0.6 10.4 %collective-permute-start.4 = (bf16[128,512]{1,0:T(8,128)(2,1)}, bf16[128,512]{1,0:T(8,128)(2,1)S(1)}, u32[]{:S(2)}, u32[]{:S(2)}) collective-permute-start(bf16[128,512]{1,0:T(8,128)(2,1)} %param.11), channel_id=1, source_target_pairs={{0,4},{4,0},{8,12},{12,8},{16,20},{20,16},{24,28},{28,24},{1,5},{5... | collective-permute-start | bytes 393224 | tf_op jit(solution)/shard_map/ppermute | solution.py:20
  1.4 4.3 %collective-permute-start = (bf16[32,128]{1,0:T(8,128)(2,1)S(1)}, bf16[32,128]{1,0:T(8,128)(2,1)S(1)}, u32[]{:S(2)}, u32[]{:S(2)}) collective-permute-start(bf16[32,128]{1,0:T(8,128)(2,1)S(1)} %get-tuple-element.16), channel_id=1, source_target_pairs={{0,4},{4,0},{8,12},{12,8},{16,20},{20,16},{24,28},{28,24},{1,5},{5... | collective-permute-start | bytes 24584 | tf_op jit(solution)/shard_map/ppermute | solution.py:20
  3.4 7.6 %copy-start.8 = (bf16[128,512]{1,0:T(8,128)(2,1)S(1)}, bf16[128,512]{1,0:T(8,128)(2,1)}, u32[]{:S(2)}) copy-start(bf16[128,512]{1,0:T(8,128)(2,1)} %param.11) | copy-start | bytes 393220
  4.7 1.0 %copy-start = (bf16[1024,512]{1,0:T(8,128)(2,1)}, bf16[1024,512]{1,0:T(8,128)(2,1)S(1)}, u32[]{:S(2)}) copy-start(bf16[1024,512]{1,0:T(8,128)(2,1)S(1)} %get-tuple-element.7.refs_1_.scaled_ref) | copy-start | bytes 3145732
  5.7 19.8 %collective-permute-start.7 = (bf16[1024,512]{1,0:T(8,128)(2,1)S(1)}, bf16[1024,512]{1,0:T(8,128)(2,1)S(1)}, u32[]{:S(2)}, u32[]{:S(2)}) collective-permute-start(bf16[1024,512]{1,0:T(8,128)(2,1)S(1)} %shard_map.113.refs_2_), channel_id=1, source_target_pairs={{0,4},{4,0},{8,12},{12,8},{16,20},{20,16},{24,28},{28,24},{1,5},{5... | collective-permute-start | bytes 3145736 | tf_op jit(solution)/shard_map/ppermute | solution.py:20
  5.7 6.6 %collective-permute-start.1 = (bf16[32,256]{1,0:T(8,128)(2,1)S(1)}, bf16[32,256]{1,0:T(8,128)(2,1)S(1)}, u32[]{:S(2)}, u32[]{:S(2)}) collective-permute-start(bf16[32,256]{1,0:T(8,128)(2,1)S(1)} %copy_bitcast_fusion), channel_id=1, source_target_pairs={{0,3},{1,0},{2,1},{3,2},{4,7},{5,4},{6,5},{7,6},{8,11},{9,8},{10,9... | collective-permute-start | bytes 49160 | tf_op jit(solution)/shard_map/ppermute | solution.py:213
  10.5 3.5 %collective-permute-start.2 = (bf16[32,256]{1,0:T(8,128)(2,1)S(1)}, bf16[32,256]{1,0:T(8,128)(2,1)S(1)}, u32[]{:S(2)}, u32[]{:S(2)}) collective-permute-start(bf16[32,256]{1,0:T(8,128)(2,1)S(1)} %copy_bitcast_fusion), channel_id=1, source_target_pairs={{0,2},{1,3},{2,0},{3,1},{4,6},{5,7},{6,4},{7,5},{8,10},{9,11},{10,... | collective-permute-start | bytes 49160 | tf_op jit(solution)/shard_map/ppermute | solution.py:213
  10.6 4.4 %collective-permute-start.3 = (bf16[32,256]{1,0:T(8,128)(2,1)S(1)}, bf16[32,256]{1,0:T(8,128)(2,1)S(1)}, u32[]{:S(2)}, u32[]{:S(2)}) collective-permute-start(bf16[32,256]{1,0:T(8,128)(2,1)S(1)} %copy_bitcast_fusion), channel_id=1, source_target_pairs={{0,1},{1,2},{2,3},{3,0},{4,5},{5,6},{6,7},{7,4},{8,9},{9,10},{10,1... | collective-permute-start | bytes 49160 | tf_op jit(solution)/shard_map/ppermute | solution.py:213
  11.0 5.6 %collective-permute-start.8 = (bf16[2,128,512]{2,1,0:T(8,128)(2,1)S(1)}, bf16[2,128,512]{2,1,0:T(8,128)(2,1)S(1)}, u32[]{:S(2)}, u32[]{:S(2)}) collective-permute-start(bf16[2,128,512]{2,1,0:T(8,128)(2,1)S(1)} %maximum_select_fusion), channel_id=1, source_target_pairs={{0,8},{4,20},{8,0},{12,28},{16,24},{20,4},{24,16},{28,12},{1,9},{5... | collective-permute-start | bytes 786440 | tf_op jit(solution)/shard_map/ppermute | solution.py:25
  15.2 3.9 %collective-permute-start.5 = (bf16[128,512]{1,0:T(8,128)(2,1)S(1)}, bf16[128,512]{1,0:T(8,128)(2,1)S(1)}, u32[]{:S(2)}, u32[]{:S(2)}) collective-permute-start(bf16[128,512]{1,0:T(8,128)(2,1)S(1)} %get-tuple-element.18), channel_id=1, source_target_pairs={{0,8},{4,20},{8,0},{12,28},{16,24},{20,4},{24,16},{28,12},{1,9},{5... | collective-permute-start | bytes 393224 | tf_op jit(solution)/shard_map/ppermute | solution.py:25
  16.6 5.1 %collective-permute-start.9 = (bf16[128,512]{1,0:T(8,128)(2,1)S(1)}, bf16[128,512]{1,0:T(8,128)(2,1)S(1)}, u32[]{:S(2)}, u32[]{:S(2)}) collective-permute-start(bf16[128,512]{1,0:T(8,128)(2,1)S(1)} %fusion.1), channel_id=1, source_target_pairs={{0,16},{4,12},{8,24},{12,4},{16,0},{20,28},{24,8},{28,20},{1,17},{... | collective-permute-start | bytes 393224 | tf_op jit(solution)/shard_map/ppermute | solution.py:25
  19.1 6.3 %collective-permute-start.6 = (bf16[128,512]{1,0:T(8,128)(2,1)S(1)}, bf16[128,512]{1,0:T(8,128)(2,1)S(1)}, u32[]{:S(2)}, u32[]{:S(2)}) collective-permute-start(bf16[128,512]{1,0:T(8,128)(2,1)S(1)} %fusion), channel_id=1, source_target_pairs={{0,16},{4,12},{8,24},{12,4},{16,0},{20,28},{24,8},{28,20},{1,17},{... | collective-permute-start | bytes 393224 | tf_op jit(solution)/shard_map/ppermute | solution.py:25
  22.6 9.7 %copy-start.3 = (s32[8192]{0:T(1024)S(1)}, s32[8192]{0:T(1024)}, u32[]{:S(2)}) copy-start(s32[8192]{0:T(1024)} %param.15) | copy-start | bytes 98308
  22.6 9.8 %copy-start.4 = (s32[1024]{0:T(1024)S(1)}, s32[1024]{0:T(1024)}, u32[]{:S(2)}) copy-start(s32[1024]{0:T(1024)} %param.17) | copy-start | bytes 12292
  22.6 9.8 %copy-start.5 = (s32[1024]{0:T(1024)S(1)}, s32[1024]{0:T(1024)}, u32[]{:S(2)}) copy-start(s32[1024]{0:T(1024)} %param.16) | copy-start | bytes 12292
  22.6 9.8 %copy-start.6 = (f32[256]{0:T(256)S(1)}, f32[256]{0:T(256)}, u32[]{:S(2)}) copy-start(f32[256]{0:T(256)} %param.19) | copy-start | bytes 3076
  22.6 9.8 %copy-start.7 = (f32[128]{0:T(128)S(1)}, f32[128]{0:T(128)}, u32[]{:S(2)}) copy-start(f32[128]{0:T(128)} %param.18) | copy-start | bytes 1540
  22.6 11.2 %collective-permute-start.10 = (bf16[3,128,512]{2,1,0:T(8,128)(2,1)}, bf16[3,128,512]{2,1,0:T(8,128)(2,1)}, u32[]{:S(2)}, u32[]{:S(2)}) collective-permute-start(bf16[3,128,512]{2,1,0:T(8,128)(2,1)} %pad_maximum_fusion.1), channel_id=1, source_target_pairs={{0,4},{4,0},{8,12},{12,8},{16,20},{20,16},{24,28},{28,24},{1,5},{5... | collective-permute-start | bytes 1179656 | tf_op jit(solution)/shard_map/ppermute | solution.py:20
  27.1 20.4 %all-to-all-start = ((bf16[32,32,256]{2,1,0:T(8,128)(2,1)}), bf16[32,32,256]{2,1,0:T(8,128)(2,1)S(1)}, u32[]{:S(2)}, u32[]{:S(2)}) async-start(bf16[32,32,256]{2,1,0:T(8,128)(2,1)} %apply.1), calls=%async_computation | async-start | bytes 1048576 | tf_op jit(solution)/shard_map/all_to_all | solution.py:280
  34.9 1.2 %copy-start.1 = (bf16[1024,512]{1,0:T(8,128)(2,1)S(1)}, bf16[1024,512]{1,0:T(8,128)(2,1)}, u32[]{:S(2)}) copy-start(bf16[1024,512]{1,0:T(8,128)(2,1)} %copy-done) | copy-start | bytes 3145732
  36.1 11.5 %copy-start.2 = (bf16[1024,64]{0,1:T(8,128)(2,1)S(1)}, bf16[1024,64]{0,1:T(8,128)(2,1)}, u32[]{:S(2)}) copy-start(bf16[1024,64]{0,1:T(8,128)(2,1)} %param.14) | copy-start | bytes 393220
where the time goes:
time: 49.1 us; the launch traced here: 48.7 us
  starting transfers between devices  19.1 us (39%)
  waiting for transfers between devices  13.7 us (28%)
  Pallas kernels  10 us (20%)
  other arithmetic  2.91 us (6%)
  local copies, waits for them, and re-layouts  2.01 us (4%)
  between operations  0.85 us (2%)
    all_to_all x1, waiting for transfers between devices, per_device(): lax.all_to_all(outgoing, ('pairs', 'rep'), split_axis=0, concat_axis=0, t...  8.39 us
    ppermute x3, starting transfers between devices, per_device(): turns.append(lax.ppermute(vec, 'rep', [(i, (i + k) % m) for i in range(m)]))  5.29 us
    all_to_all x1, starting transfers between devices, per_device(): lax.all_to_all(outgoing, ('pairs', 'rep'), split_axis=0, concat_axis=0, t...  5.17 us
    ppermute x4, starting transfers between devices, split_exchange(): lax.ppermute(x, 'pairs', [(i, i ^ (odd_mask if i & 1 else even_mask)) for...  5.16 us
    ppermute x4, starting transfers between devices, exchange(): return lax.ppermute(x, axis, [(i, i ^ mask) for i in range(size)])  3.44 us
    pallas_call x1, Pallas kernels, per_device(): pl.pallas_call(tile_kernel, grid_spec=pltpu.PrefetchScalarGridSpec(num_sc...  3.06 us
    ppermute x4, waiting for transfers between devices, split_exchange(): lax.ppermute(x, 'pairs', [(i, i ^ (odd_mask if i & 1 else even_mask)) for...  2.66 us
    ppermute x3, waiting for transfers between devices, per_device(): turns.append(lax.ppermute(vec, 'rep', [(i, (i + k) % m) for i in range(m)]))  2.63 us
  transfers between devices with their start and end apart: 12, of which 6 were waited for; matrix products, arithmetic and copies ran while one was open for 6% of the time, Pallas kernels for 18%

commit v1 on v0

--- a/solution.py
+++ b/solution.py
@@ -49,7 +49,10 @@
     return value
 
 
-def load_kernel(n, me_ref, map_hbm, val_hbm, screen_hbm, scaled_ref, order_ref, map_ref, val_ref, screen_ref, sems):
+def load_kernel(
+    n, me_ref, map_hbm, val_hbm, screen_hbm, cond_hbm, trial_hbm,
+    scaled_ref, order_ref, cond_ref, trial_ref, map_ref, val_ref, screen_ref, sems,
+):
     rows = val_ref.shape[0]
     per_peer = rows // n
     lanes = rows // 128
@@ -59,12 +62,16 @@
         pltpu.make_async_copy(screen_hbm, screen_ref, sems.at[0]),
         pltpu.make_async_copy(map_hbm.at[pl.ds(first, lanes), :], map_ref, sems.at[1]),
     ]
+    tail = [
+        pltpu.make_async_copy(cond_hbm, cond_ref, sems.at[6]),
+        pltpu.make_async_copy(trial_hbm, trial_ref, sems.at[7]),
+    ]
     body = [
         pltpu.make_async_copy(
             val_hbm.at[pl.ds(k * tall, tall), :], val_ref.at[pl.ds(k * tall, tall), :], sems.at[2 + k])
         for k in range(4)
     ]
-    for copy in head + body:
+    for copy in head + body + tail:
         copy.start()
     for copy in head:
         copy.wait()
@@ -78,6 +85,8 @@
         copy.wait()
         part = slice(k * tall, (k + 1) * tall)
         scaled_ref[part, :] = (val_ref[part, :].astype(F32) * screen_ref[...]).astype(BF16)
+    for copy in tail:
+        copy.wait()
 
 
 def sent_kernel(first, order_ref, scaled_ref, sent_ref):
@@ -203,44 +212,46 @@
     screen = screening.reshape(1, depth)
     map_lanes = row_map.reshape(-1, 128)
 
-    trial = trial_cols.T
-    low, high = trial[:half], trial[half:]
-    got = exchange(jnp.where(odd, low, high), "pairs", 1)
-    vec = in_order(odd, jnp.where(odd, high, low), got)
-    vec = vec.transpose(1, 0, 2).reshape(half, 2 * cols)
-    turns = [vec]
+    turns = [None]
     for k in range(1, m):
-        turns.append(lax.ppermute(vec, "rep", [(i, (i + k) % m) for i in range(m)]))
-    vec_all = []
-    for k in range(m):
-        block = turns[0]
-        for t in range(1, m):
-            block = jnp.where(lax.rem(layer - t + m, m) == k, turns[t], block)
-        vec_all.append(block)
-    vec_all = jnp.concatenate(vec_all)
-
-    both = in_order(odd, mat_cond, exchange(mat_cond, "pairs", 1))
+        turns.append(lax.ppermute(trial_cols.T, "rep", [(i, (i + k) % m) for i in range(m)]))
+    cond_other = exchange(mat_cond, "pairs", 1)
 
     shares = 2
     far_away = pl.BlockSpec(memory_space=pltpu.HBM)
-    scaled, order = pl.pallas_call(
+    scaled, order, cond_own, turns[0] = pl.pallas_call(
         lambda *refs: load_kernel(n, *refs),
-        in_specs=[SCALAR, far_away, far_away, far_away],
-        out_specs=(WHOLE, WHOLE),
+        in_specs=[SCALAR] + [far_away] * 5,
+        out_specs=(WHOLE,) * 4,
         out_shape=(
             jax.ShapeDtypeStruct((rows, depth), BF16),
             jax.ShapeDtypeStruct((1, rows), jnp.int32),
+            jax.ShapeDtypeStruct((cols, depth), BF16),
+            jax.ShapeDtypeStruct((vecs, cols), BF16),
         ),
         scratch_shapes=[
             pltpu.VMEM((rows // 128, 128), jnp.int32),
             pltpu.VMEM((rows, depth), BF16),
             pltpu.VMEM((1, depth), F32),
-            pltpu.SemaphoreType.DMA((6,)),
+            pltpu.SemaphoreType.DMA((8,)),
         ],
         cost_estimate=pl.CostEstimate(flops=rows * depth, bytes_accessed=4 * rows * depth, transcendentals=0),
-        compiler_params=roomy(12),
+        compiler_params=roomy(8),
         name="load",
-    )(me, *(pltpu.with_memory_space_constraint(x, pltpu.HBM) for x in (map_lanes, mat_val, screen)))
+    )(me, *(pltpu.with_memory_space_constraint(x, pltpu.HBM) for x in (map_lanes, mat_val, screen, mat_cond, trial_cols.T)))
+    both = in_order(odd, cond_own, cond_other)
+    wide = []
+    for k in range(m):
+        block = turns[0]
+        for t in range(1, m):
+            block = jnp.where(lax.rem(layer - t + m, m) == k, turns[t], block)
+        wide.append(block)
+    wide = jnp.stack(wide)
+    low, high = wide[:, :half], wide[:, half:]
+    got = exchange(jnp.where(odd, low, high), "pairs", 1)
+    kept = jnp.where(odd, high, low)
+    vec_all = jnp.where(odd, jnp.concatenate([got, kept], axis=2), jnp.concatenate([kept, got], axis=2))
+    vec_all = vec_all.reshape(m * half, 2 * cols)
     shares = 1
     sent = [pl.pallas_call(
         lambda *refs, share=share: sent_kernel(share * (rows // shares), *refs),
@@ -249,7 +260,7 @@
         out_shape=jax.ShapeDtypeStruct((rows // shares, depth), BF16),
         cost_estimate=pl.CostEstimate(
             flops=2 * rows * rows * depth // shares, bytes_accessed=4 * rows * depth, transcendentals=0),
-        compiler_params=roomy(12),
+        compiler_params=roomy(8),
     )(order, scaled) for share in range(shares)]
     sent_other = [exchange(part, "pairs", 1) for part in sent]
 
@@ -263,7 +274,7 @@
             lambda *refs: apply_kernel(m, n, *refs),
             in_specs=[SCALAR] + [WHOLE] * (1 + 2 * shares),
             out_specs=WHOLE,
-            compiler_params=roomy(12),
+            compiler_params=roomy(8),
             out_shape=jax.ShapeDtypeStruct((n * m, half, 2 * per_peer), BF16),
             cost_estimate=pl.CostEstimate(
                 flops=4 * rows * depth * m * half, bytes_accessed=4 * rows * depth, transcendentals=0),
@@ -295,7 +306,7 @@
         out_shape=jax.ShapeDtypeStruct((1, rows, n * cols), BF16),
         cost_estimate=pl.CostEstimate(
             flops=2 * rows * depth * n * cols, bytes_accessed=2 * rows * (depth + n * cols), transcendentals=0),
-        compiler_params=roomy(16),
+        compiler_params=roomy(8),
         name="tiles",
     )(me, scaled, cond_all)
 
@@ -309,7 +320,7 @@
         ),
         cost_estimate=pl.CostEstimate(
             flops=8 * rows * rows, bytes_accessed=2 * rows * rows, transcendentals=0),
-        compiler_params=roomy(12),
+        compiler_params=roomy(8),
         name="place",
     )(
         me,
@@ -328,7 +339,7 @@
         lambda *refs: final_kernel(parts, layers, *refs),
         in_specs=[WHOLE] * 4,
         out_specs=WHOLE,
-        compiler_params=roomy(12),
+        compiler_params=roomy(8),
         out_shape=jax.ShapeDtypeStruct((vecs, rows), BF16),
         scratch_shapes=[pltpu.VMEM((vecs, rows), BF16)],
         cost_estimate=pl.CostEstimate(

time: 49.1 us -> 46.2 us (0.941)
  waiting for transfers between devices: 13.7 us -> 12.5 us
  local copies, waits for them, and re-layouts: 2.01 us -> 1.05 us
  other arithmetic: 2.91 us -> 2.19 us
    ppermute x4, starting transfers between devices: 3.44 us -> 5.83 us  [exchange(): return lax.ppermute(x, axis, [(i, i ^ mask) for i in range(size)])]
    all_to_all x1, starting transfers between devices: 5.17 us -> 3.64 us  [per_device(): lax.all_to_all(outgoing, ('pairs', 'rep'), split_axis=0, concat_axis=0, t...]
    ppermute x3, waiting for transfers between devices: 2.63 us -> 1.11 us  [per_device(): lax.ppermute(trial_cols.T, 'rep', [(i, (i + k) % m) for i in range(m)])]
    unnamed x18 -> x16, local copies, waits for them, and re-layouts: 1.96 us -> 0.99 us
    select_n x1, other arithmetic: 0.72 us -> 0.01 us  [per_device(): got = exchange(jnp.where(odd, low, high), 'pairs', 1)]
    ppermute x3, starting transfers between devices: 5.29 us -> 4.65 us  [per_device(): lax.ppermute(trial_cols.T, 'rep', [(i, (i + k) % m) for i in range(m)])]
  transfers between devices with their start and end apart: 12 -> 12, of which waited for: 6 -> 6; matrix products, arithmetic and copies ran while one was open for 6% -> 5% of each run, Pallas kernels for 18% -> 19%
where the time goes in v1:
time: 46.2 us; the launch traced here: 45.9 us
  starting transfers between devices  19 us (41%)
  waiting for transfers between devices  12.5 us (27%)
  Pallas kernels  10 us (22%)
  other arithmetic  2.19 us (5%)
  local copies, waits for them, and re-layouts  1.05 us (2%)
  between operations  0.87 us (2%)
    all_to_all x1, waiting for transfers between devices, per_device(): lax.all_to_all(outgoing, ('pairs', 'rep'), split_axis=0, concat_axis=0, t...  8.39 us
    ppermute x4, starting transfers between devices, exchange(): return lax.ppermute(x, axis, [(i, i ^ mask) for i in range(size)])  5.83 us
    ppermute x4, starting transfers between devices, split_exchange(): lax.ppermute(x, 'pairs', [(i, i ^ (odd_mask if i & 1 else even_mask)) for...  4.91 us
    ppermute x3, starting transfers between devices, per_device(): lax.ppermute(trial_cols.T, 'rep', [(i, (i + k) % m) for i in range(m)])  4.65 us
    all_to_all x1, starting transfers between devices, per_device(): lax.all_to_all(outgoing, ('pairs', 'rep'), split_axis=0, concat_axis=0, t...  3.64 us
    pallas_call x1, Pallas kernels, per_device(): pl.pallas_call(tile_kernel, grid_spec=pltpu.PrefetchScalarGridSpec(num_sc...  3.06 us
    ppermute x4, waiting for transfers between devices, split_exchange(): lax.ppermute(x, 'pairs', [(i, i ^ (odd_mask if i & 1 else even_mask)) for...  3 us
    pallas_call x1, Pallas kernels, per_device(): pl.pallas_call(lambda *refs: apply_kernel(m, n, *refs), in_specs=[SCALAR]...  1.64 us
  transfers between devices with their start and end apart: 12, of which 6 were waited for; matrix products, arithmetic and copies ran while one was open for 5% of the time, Pallas kernels for 19%

profile of v1, /device:TPU:1, one launch (start us, length us, event | category | flops | bytes accessed | tf_op | source)
XLA Modules:
  0.0 45.9 jit_solution(4243536997766609557)
XLA Ops:
  0.6 4.2 %collective-permute-start = (bf16[64,128]{1,0:T(8,128)(2,1)}, bf16[64,128]{1,0:T(8,128)(2,1)S(1)}, u32[]{:S(2)}, u32[]{:S(2)}) collective-permute-start(bf16[64,128]{1,0:T(8,128)(2,1)} %bitcast.52), channel_id=1, source_target_pairs={{0,3},{1,0},{2,1},{3,2},{4,7},{5,4},{6,5},{7,6},{8,11},{9,8},{10,9... | collective-permute-start | bytes 49160 | tf_op jit(solution)/shard_map/ppermute | solution.py:217
  4.8 0.5 collective-permute-start.2
  5.3 1.5 %collective-permute-start.4 = (bf16[128,512]{1,0:T(8,128)(2,1)}, bf16[128,512]{1,0:T(8,128)(2,1)S(1)}, u32[]{:S(2)}, u32[]{:S(2)}) collective-permute-start(bf16[128,512]{1,0:T(8,128)(2,1)} %refs_4_.1), channel_id=1, source_target_pairs={{0,4},{4,0},{8,12},{12,8},{16,20},{20,16},{24,28},{28,24},{1,5},{5... | collective-permute-start | bytes 393224 | tf_op jit(solution)/shard_map/ppermute | solution.py:20
  6.8 1.5 %load.1 = (bf16[1024,512]{1,0:T(8,128)(2,1)S(1)}, s32[1,1024]{1,0:T(1,128)S(1)}, bf16[128,512]{1,0:T(8,128)(2,1)S(1)}, bf16[64,128]{1,0:T(8,128)(2,1)S(1)}) custom-call(s32[1]{0:T(128)} %bitcast.refs_0_.me_ref, s32[64,128]{1,0:T(8,128)} %bitcast.38, bf16[1024,512]{1,0:T(8,128)(2,1)} %refs_2_.1, f32[1,512]{1,0:T(1,128)} %bitcast.56, ...), custom_call_target="tpu_custom_call" | custom-call | flops 524288 | bytes 2097152 | tf_op jit(solution)/shard_map/load/pallas_call | solution.py:222
  8.5 0.9 %collective-permute-done.2 = bf16[64,128]{1,0:T(8,128)(2,1)S(1)} collective-permute-done((bf16[64,128]{1,0:T(8,128)(2,1)}, bf16[64,128]{1,0:T(8,128)(2,1)S(1)}, u32[]{:S(2)}, u32[]{:S(2)}) %collective-permute-start.2) | collective-permute-done | bytes 16416 | tf_op jit(solution)/shard_map/ppermute | solution.py:217
  9.5 2.2 %collective-permute-start.3 = (bf16[4,32,128]{2,1,0:T(8,128)(2,1)S(1)}, bf16[4,32,128]{2,1,0:T(8,128)(2,1)S(1)}, u32[]{:S(2)}, u32[]{:S(2)}) collective-permute-start(bf16[4,32,128]{2,1,0:T(8,128)(2,1)S(1)} %get-tuple-element.16), channel_id=1, source_target_pairs={{0,4},{4,0},{8,12},{12,8},{16,20},{20,16},{24,28},{28,24},{1,5},{5... | collective-permute-start | bytes 98312 | tf_op jit(solution)/shard_map/ppermute | solution.py:20
  11.7 1.3 %collective-permute-start.8 = (bf16[2,128,512]{2,1,0:T(8,128)(2,1)S(1)}, bf16[2,128,512]{2,1,0:T(8,128)(2,1)S(1)}, u32[]{:S(2)}, u32[]{:S(2)}) collective-permute-start(bf16[2,128,512]{2,1,0:T(8,128)(2,1)S(1)} %maximum_select_fusion), channel_id=1, source_target_pairs={{0,8},{4,20},{8,0},{12,28},{16,24},{20,4},{24,16},{28,12},{1,9},{5... | collective-permute-start | bytes 786440 | tf_op jit(solution)/shard_map/ppermute | solution.py:25
  13.0 1.3 %shard_map.113.refs_2_ = bf16[1024,512]{1,0:T(8,128)(2,1)S(1)} custom-call(s32[1,1024]{1,0:T(1,128)S(1)} %get-tuple-element.10.refs_0_, bf16[1024,512]{1,0:T(8,128)(2,1)S(1)} %get-tuple-element.11.refs_1_.scaled_ref), custom_call_target="tpu_custom_call" | custom-call | flops 1073741824 | bytes 2097152 | tf_op jit(solution)/shard_map/pallas_call | solution.py:256
  14.8 1.3 %collective-permute-start.5 = (bf16[128,512]{1,0:T(8,128)(2,1)S(1)}, bf16[128,512]{1,0:T(8,128)(2,1)S(1)}, u32[]{:S(2)}, u32[]{:S(2)}) collective-permute-start(bf16[128,512]{1,0:T(8,128)(2,1)S(1)} %get-tuple-element.22), channel_id=1, source_target_pairs={{0,8},{4,20},{8,0},{12,28},{16,24},{20,4},{24,16},{28,12},{1,9},{5... | collective-permute-start | bytes 393224 | tf_op jit(solution)/shard_map/ppermute | solution.py:25
  16.1 1.2 %collective-permute-done.8 = bf16[2,128,512]{2,1,0:T(8,128)(2,1)S(1)} collective-permute-done((bf16[2,128,512]{2,1,0:T(8,128)(2,1)S(1)}, bf16[2,128,512]{2,1,0:T(8,128)(2,1)S(1)}, u32[]{:S(2)}, u32[]{:S(2)}) %collective-permute-start.8) | collective-permute-done | bytes 262176 | tf_op jit(solution)/shard_map/ppermute | solution.py:25
  17.3 1.3 %collective-permute-start.9 = (bf16[128,512]{1,0:T(8,128)(2,1)S(1)}, bf16[128,512]{1,0:T(8,128)(2,1)S(1)}, u32[]{:S(2)}, u32[]{:S(2)}) collective-permute-start(bf16[128,512]{1,0:T(8,128)(2,1)S(1)} %fusion.1), channel_id=1, source_target_pairs={{0,16},{4,12},{8,24},{12,4},{16,0},{20,28},{24,8},{28,20},{1,17},{... | collective-permute-start | bytes 393224 | tf_op jit(solution)/shard_map/ppermute | solution.py:25
  18.6 0.4 collective-permute-done.5
  19.0 1.0 %collective-permute-start.6 = (bf16[128,512]{1,0:T(8,128)(2,1)S(1)}, bf16[128,512]{1,0:T(8,128)(2,1)S(1)}, u32[]{:S(2)}, u32[]{:S(2)}) collective-permute-start(bf16[128,512]{1,0:T(8,128)(2,1)S(1)} %fusion), channel_id=1, source_target_pairs={{0,16},{4,12},{8,24},{12,4},{16,0},{20,28},{24,8},{28,20},{1,17},{... | collective-permute-start | bytes 393224 | tf_op jit(solution)/shard_map/ppermute | solution.py:25
  20.0 1.4 %collective-permute-done.9 = bf16[128,512]{1,0:T(8,128)(2,1)S(1)} collective-permute-done((bf16[128,512]{1,0:T(8,128)(2,1)S(1)}, bf16[128,512]{1,0:T(8,128)(2,1)S(1)}, u32[]{:S(2)}, u32[]{:S(2)}) %collective-permute-start.9) | collective-permute-done | bytes 131104 | tf_op jit(solution)/shard_map/ppermute | solution.py:25
  21.5 0.8 %pad_maximum_fusion.1 = bf16[3,128,512]{2,1,0:T(8,128)(2,1)} fusion(bf16[1,128,512]{2,1,0:T(8,128)(2,1)S(1)} %bitcast.47, bf16[2,128,512]{2,1,0:T(8,128)(2,1)S(1)} %collective-permute-done.8), kind=kLoop, calls=%fused_computation.1 | loop fusion | flops 196608 | bytes 786432 | tf_op jit(solution)/shard_map/concatenate | solution.py:183
  22.3 1.8 %collective-permute-start.10 = (bf16[3,128,512]{2,1,0:T(8,128)(2,1)}, bf16[3,128,512]{2,1,0:T(8,128)(2,1)}, u32[]{:S(2)}, u32[]{:S(2)}) collective-permute-start(bf16[3,128,512]{2,1,0:T(8,128)(2,1)} %pad_maximum_fusion.1), channel_id=1, source_target_pairs={{0,4},{4,0},{8,12},{12,8},{16,20},{20,16},{24,28},{28,24},{1,5},{5... | collective-permute-start | bytes 1179656 | tf_op jit(solution)/shard_map/ppermute | solution.py:20
  24.1 1.6 %apply.1 = bf16[32,32,256]{2,1,0:T(8,128)(2,1)} custom-call(s32[1]{0:T(128)} %bitcast.refs_0_.me_ref, bf16[128,512]{1,0:T(8,128)(2,1)S(1)} %add_convert_fusion.refs_1_, bf16[1024,512]{1,0:T(8,128)(2,1)S(1)} %shard_map.113.refs_2_, bf16[1024,512]{1,0:T(8,128)(2,1)S(1)} %collective-permute-done.7.refs_3_), custom_call_target="tpu_custom_call" | custom-call | flops 268435456 | bytes 2097152 | tf_op jit(solution)/shard_map/apply/pallas_call | solution.py:273
  25.8 3.6 %all-to-all-start = ((bf16[32,32,256]{2,1,0:T(8,128)(2,1)}), bf16[32,32,256]{2,1,0:T(8,128)(2,1)S(1)}, u32[]{:S(2)}, u32[]{:S(2)}) async-start(bf16[32,32,256]{2,1,0:T(8,128)(2,1)} %apply.1), calls=%async_computation | async-start | bytes 1048576 | tf_op jit(solution)/shard_map/all_to_all | solution.py:291
  29.5 1.4 %place.1 = (bf16[1024,1024]{1,0:T(8,128)(2,1)S(1)}, f32[8,128]{1,0:T(8,128)S(1)}) custom-call(s32[1]{0:T(128)} %bitcast.refs_0_.me_ref, s32[64,128]{1,0:T(8,128)S(1)} %bitcast.39, s32[8,128]{1,0:T(8,128)S(1)} %bitcast.40, s32[8,128]{1,0:T(8,128)S(1)} %bitcast.41, f32[2,128]{1,0:T(2,128)S(1)} %bitcast.42, f32[1,128]{1,0:T(1,128)S(1)} %bitcast.43), custom_call_target="tpu_custom_call" | custom-call | flops 8388608 | bytes 2097152 | tf_op jit(solution)/shard_map/place/pallas_call | solution.py:313
  31.0 1.1 %broadcast_select_fusion.1 = (bf16[3,128,512]{2,1,0:T(8,128)(2,1)S(1)}, bf16[3,128,512]{2,1,0:T(8,128)(2,1)S(1)}) fusion(bf16[3,128,512]{2,1,0:T(8,128)(2,1)} %collective-permute-done.10, pred[]{:T(512)S(6)} %eq.39, bf16[1,128,512]{2,1,0:T(8,128)(2,1)S(1)} %bitcast.48, bf16[2,128,512]{2,1,0:T(8,128)(2,1)S(1)} %collective-permute-done.8), kind=kLoop, calls=%fused_computation.3 | loop fusion | flops 589824 | bytes 1572865 | tf_op jit(solution)/shard_map/jit(_where)/select_n | solution.py:185
  32.3 1.0 %copy-done.1 = bf16[1024,512]{1,0:T(8,128)(2,1)S(1)} copy-done((bf16[1024,512]{1,0:T(8,128)(2,1)S(1)}, bf16[1024,512]{1,0:T(8,128)(2,1)}, u32[]{:S(2)}) %copy-start.1) | copy-done | bytes 1048600
  33.2 3.1 %tiles.1 = bf16[1,1024,1024]{2,1,0:T(8,128)(2,1)} custom-call(s32[1]{0:T(128)} %bitcast.refs_0_.me_ref, bf16[1024,512]{1,0:T(8,128)(2,1)S(1)} %copy-done.1, bf16[4,2,128,512]{3,2,1,0:T(8,128)(2,1)S(1)} %pad_maximum_fusion.cond_ref), custom_call_target="tpu_custom_call" | custom-call | flops 1073741824 | bytes 3145728 | tf_op jit(solution)/shard_map/tiles/pallas_call | solution.py:295
  36.3 8.4 %all-to-all-done.refs_0_ = bf16[32,32,256]{2,1,0:T(8,128)(2,1)S(1)} async-done(((bf16[32,32,256]{2,1,0:T(8,128)(2,1)}), bf16[32,32,256]{2,1,0:T(8,128)(2,1)S(1)}, u32[]{:S(2)}, u32[]{:S(2)}) %all-to-all-start) | async-done | bytes 524320 | tf_op jit(solution)/shard_map/all_to_all | solution.py:291
  44.7 1.1 %final.1 = bf16[64,1024]{1,0:T(8,128)(2,1)} custom-call(bf16[32,32,256]{2,1,0:T(8,128)(2,1)S(1)} %all-to-all-done.refs_0_, bf16[1024,1024]{1,0:T(8,128)(2,1)S(1)} %get-tuple-element.12.refs_1_, f32[8,128]{1,0:T(8,128)S(1)} %get-tuple-element.13.refs_2_, bf16[64,1024]{1,0:T(8,128)(2,1)S(1)} %bitcast.37), custom_call_target="tpu_custom_call" | custom-call | flops 134217728 | bytes 2097152 | tf_op jit(solution)/shard_map/final/pallas_call | solution.py:338
  (38 shorter events, 1.2 us)
Async XLA Ops:
  0.6 7.7 %collective-permute-start = (bf16[64,128]{1,0:T(8,128)(2,1)}, bf16[64,128]{1,0:T(8,128)(2,1)S(1)}, u32[]{:S(2)}, u32[]{:S(2)}) collective-permute-start(bf16[64,128]{1,0:T(8,128)(2,1)} %bitcast.52), channel_id=1, source_target_pairs={{0,3},{1,0},{2,1},{3,2},{4,7},{5,4},{6,5},{7,6},{8,11},{9,8},{10,9... | collective-permute-start | bytes 49160 | tf_op jit(solution)/shard_map/ppermute | solution.py:217
  4.8 3.7 %collective-permute-start.1 = (bf16[64,128]{1,0:T(8,128)(2,1)}, bf16[64,128]{1,0:T(8,128)(2,1)S(1)}, u32[]{:S(2)}, u32[]{:S(2)}) collective-permute-start(bf16[64,128]{1,0:T(8,128)(2,1)} %bitcast.53), channel_id=1, source_target_pairs={{0,2},{1,3},{2,0},{3,1},{4,6},{5,7},{6,4},{7,5},{8,10},{9,11},{10,... | collective-permute-start | bytes 49160 | tf_op jit(solution)/shard_map/ppermute | solution.py:217
  4.8 4.6 %collective-permute-start.2 = (bf16[64,128]{1,0:T(8,128)(2,1)}, bf16[64,128]{1,0:T(8,128)(2,1)S(1)}, u32[]{:S(2)}, u32[]{:S(2)}) collective-permute-start(bf16[64,128]{1,0:T(8,128)(2,1)} %bitcast.54), channel_id=1, source_target_pairs={{0,1},{1,2},{2,3},{3,0},{4,5},{5,6},{6,7},{7,4},{8,9},{9,10},{10,1... | collective-permute-start | bytes 49160 | tf_op jit(solution)/shard_map/ppermute | solution.py:217
  5.3 6.4 %collective-permute-start.4 = (bf16[128,512]{1,0:T(8,128)(2,1)}, bf16[128,512]{1,0:T(8,128)(2,1)S(1)}, u32[]{:S(2)}, u32[]{:S(2)}) collective-permute-start(bf16[128,512]{1,0:T(8,128)(2,1)} %refs_4_.1), channel_id=1, source_target_pairs={{0,4},{4,0},{8,12},{12,8},{16,20},{20,16},{24,28},{28,24},{1,5},{5... | collective-permute-start | bytes 393224 | tf_op jit(solution)/shard_map/ppermute | solution.py:20
  8.3 6.0 %copy-start = (bf16[1024,512]{1,0:T(8,128)(2,1)}, bf16[1024,512]{1,0:T(8,128)(2,1)S(1)}, u32[]{:S(2)}) copy-start(bf16[1024,512]{1,0:T(8,128)(2,1)S(1)} %get-tuple-element.11.refs_1_.scaled_ref) | copy-start | bytes 3145732
  9.5 5.1 %collective-permute-start.3 = (bf16[4,32,128]{2,1,0:T(8,128)(2,1)S(1)}, bf16[4,32,128]{2,1,0:T(8,128)(2,1)S(1)}, u32[]{:S(2)}, u32[]{:S(2)}) collective-permute-start(bf16[4,32,128]{2,1,0:T(8,128)(2,1)S(1)} %get-tuple-element.16), channel_id=1, source_target_pairs={{0,4},{4,0},{8,12},{12,8},{16,20},{20,16},{24,28},{28,24},{1,5},{5... | collective-permute-start | bytes 98312 | tf_op jit(solution)/shard_map/ppermute | solution.py:20
  11.7 5.6 %collective-permute-start.8 = (bf16[2,128,512]{2,1,0:T(8,128)(2,1)S(1)}, bf16[2,128,512]{2,1,0:T(8,128)(2,1)S(1)}, u32[]{:S(2)}, u32[]{:S(2)}) collective-permute-start(bf16[2,128,512]{2,1,0:T(8,128)(2,1)S(1)} %maximum_select_fusion), channel_id=1, source_target_pairs={{0,8},{4,20},{8,0},{12,28},{16,24},{20,4},{24,16},{28,12},{1,9},{5... | collective-permute-start | bytes 786440 | tf_op jit(solution)/shard_map/ppermute | solution.py:25
  14.3 9.9 %collective-permute-start.7 = (bf16[1024,512]{1,0:T(8,128)(2,1)S(1)}, bf16[1024,512]{1,0:T(8,128)(2,1)S(1)}, u32[]{:S(2)}, u32[]{:S(2)}) collective-permute-start(bf16[1024,512]{1,0:T(8,128)(2,1)S(1)} %shard_map.113.refs_2_), channel_id=1, source_target_pairs={{0,4},{4,0},{8,12},{12,8},{16,20},{20,16},{24,28},{28,24},{1,5},{5... | collective-permute-start | bytes 3145736 | tf_op jit(solution)/shard_map/ppermute | solution.py:20
  14.8 4.2 %collective-permute-start.5 = (bf16[128,512]{1,0:T(8,128)(2,1)S(1)}, bf16[128,512]{1,0:T(8,128)(2,1)S(1)}, u32[]{:S(2)}, u32[]{:S(2)}) collective-permute-start(bf16[128,512]{1,0:T(8,128)(2,1)S(1)} %get-tuple-element.22), channel_id=1, source_target_pairs={{0,8},{4,20},{8,0},{12,28},{16,24},{20,4},{24,16},{28,12},{1,9},{5... | collective-permute-start | bytes 393224 | tf_op jit(solution)/shard_map/ppermute | solution.py:25
  17.3 4.2 %collective-permute-start.9 = (bf16[128,512]{1,0:T(8,128)(2,1)S(1)}, bf16[128,512]{1,0:T(8,128)(2,1)S(1)}, u32[]{:S(2)}, u32[]{:S(2)}) collective-permute-start(bf16[128,512]{1,0:T(8,128)(2,1)S(1)} %fusion.1), channel_id=1, source_target_pairs={{0,16},{4,12},{8,24},{12,4},{16,0},{20,28},{24,8},{28,20},{1,17},{... | collective-permute-start | bytes 393224 | tf_op jit(solution)/shard_map/ppermute | solution.py:25
  19.0 5.1 %collective-permute-start.6 = (bf16[128,512]{1,0:T(8,128)(2,1)S(1)}, bf16[128,512]{1,0:T(8,128)(2,1)S(1)}, u32[]{:S(2)}, u32[]{:S(2)}) collective-permute-start(bf16[128,512]{1,0:T(8,128)(2,1)S(1)} %fusion), channel_id=1, source_target_pairs={{0,16},{4,12},{8,24},{12,4},{16,0},{20,28},{24,8},{28,20},{1,17},{... | collective-permute-start | bytes 393224 | tf_op jit(solution)/shard_map/ppermute | solution.py:25
  22.3 7.2 %copy-start.3 = (s32[8192]{0:T(1024)S(1)}, s32[8192]{0:T(1024)}, u32[]{:S(2)}) copy-start(s32[8192]{0:T(1024)} %param.15) | copy-start | bytes 98308
  22.3 7.2 %copy-start.4 = (s32[1024]{0:T(1024)S(1)}, s32[1024]{0:T(1024)}, u32[]{:S(2)}) copy-start(s32[1024]{0:T(1024)} %param.17) | copy-start | bytes 12292
  22.3 7.2 %copy-start.5 = (s32[1024]{0:T(1024)S(1)}, s32[1024]{0:T(1024)}, u32[]{:S(2)}) copy-start(s32[1024]{0:T(1024)} %param.16) | copy-start | bytes 12292
  22.3 7.2 %copy-start.6 = (f32[256]{0:T(256)S(1)}, f32[256]{0:T(256)}, u32[]{:S(2)}) copy-start(f32[256]{0:T(256)} %param.19) | copy-start | bytes 3076
  22.3 7.2 %copy-start.7 = (f32[128]{0:T(128)S(1)}, f32[128]{0:T(128)}, u32[]{:S(2)}) copy-start(f32[128]{0:T(128)} %param.18) | copy-start | bytes 1540
  22.3 8.7 %collective-permute-start.10 = (bf16[3,128,512]{2,1,0:T(8,128)(2,1)}, bf16[3,128,512]{2,1,0:T(8,128)(2,1)}, u32[]{:S(2)}, u32[]{:S(2)}) collective-permute-start(bf16[3,128,512]{2,1,0:T(8,128)(2,1)} %pad_maximum_fusion.1), channel_id=1, source_target_pairs={{0,4},{4,0},{8,12},{12,8},{16,20},{20,16},{24,28},{28,24},{1,5},{5... | collective-permute-start | bytes 1179656 | tf_op jit(solution)/shard_map/ppermute | solution.py:20
  25.8 18.9 %all-to-all-start = ((bf16[32,32,256]{2,1,0:T(8,128)(2,1)}), bf16[32,32,256]{2,1,0:T(8,128)(2,1)S(1)}, u32[]{:S(2)}, u32[]{:S(2)}) async-start(bf16[32,32,256]{2,1,0:T(8,128)(2,1)} %apply.1), calls=%async_computation | async-start | bytes 1048576 | tf_op jit(solution)/shard_map/all_to_all | solution.py:291
  32.0 1.2 %copy-start.1 = (bf16[1024,512]{1,0:T(8,128)(2,1)S(1)}, bf16[1024,512]{1,0:T(8,128)(2,1)}, u32[]{:S(2)}) copy-start(bf16[1024,512]{1,0:T(8,128)(2,1)} %copy-done) | copy-start | bytes 3145732
  33.2 11.5 %copy-start.2 = (bf16[1024,64]{0,1:T(8,128)(2,1)S(1)}, bf16[1024,64]{0,1:T(8,128)(2,1)}, u32[]{:S(2)}) copy-start(bf16[1024,64]{0,1:T(8,128)(2,1)} %param.14) | copy-start | bytes 393220

commit v2 on v0

v2 whole, which is shorter than its diff:
```python
import jax
import jax.numpy as jnp
from jax import lax
from jax.experimental import pallas as pl
from jax.experimental.pallas import tpu as pltpu
from jax.sharding import PartitionSpec as P

F32 = jnp.float32
BF16 = jnp.bfloat16
SCALAR = pl.BlockSpec(memory_space=pltpu.SMEM)
WHOLE = pl.BlockSpec(memory_space=pltpu.VMEM)


def roomy(mib):
    return pltpu.CompilerParams(vmem_limit_bytes=mib << 20)


def exchange(x, mask):
    size = lax.axis_size("pairs")
    return lax.ppermute(x, "pairs", [(i, i ^ mask) for i in range(size)])


def in_order(odd, own, partner):
    return jnp.where(odd, jnp.stack([partner, own]), jnp.stack([own, partner]))


def lane_cumsum(x):
    width = x.shape[1]
    lane = lax.broadcasted_iota(jnp.int32, x.shape, 1)
    step = 1
    while step < width:
        x = x + jnp.where(lane >= step, pltpu.roll(x, step, 1), 0)
        step *= 2
    return x


def lookup(table_ref, index):
    value = jnp.zeros(index.shape, F32)
    for part in range(table_ref.shape[0]):
        row = jnp.broadcast_to(table_ref[part : part + 1, :], index.shape)
        near = jnp.clip(index - 128 * part, 0, 127)
        found = jnp.take_along_axis(row, near, axis=1)
        value = jnp.where(index // 128 == part, found, value)
    return value


def load_kernel(n, me_ref, map_hbm, val_hbm, screen_hbm, scaled_ref, order_ref, screen_ref, map_ref, val_ref, sems):
    rows = val_ref.shape[0]
    per_peer = rows // n
    lanes = rows // 128
    parts = 4
    tall = rows // parts
    first = pl.multiple_of((me_ref[0] // 2) * (2 * lanes), lanes)
    head = [
        pltpu.make_async_copy(screen_hbm, screen_ref, sems.at[0]),
        pltpu.make_async_copy(map_hbm.at[pl.ds(first, 2 * lanes), :], map_ref, sems.at[1]),
    ]
    body = [
        pltpu.make_async_copy(
            val_hbm.at[pl.ds(k * tall, tall), :], val_ref.at[pl.ds(k * tall, tall), :], sems.at[2 + k])
        for k in range(parts)
    ]
    for copy in head + body:
        copy.start()
    for copy in head:
        copy.wait()
    block = lax.broadcasted_iota(jnp.int32, (n, rows), 0)
    for flip in range(2):
        at = pl.multiple_of(((me_ref[0] & 1) ^ flip) * lanes, lanes)
        own = map_ref[pl.ds(at, lanes), :]
        own = jnp.concatenate([own[c : c + 1, :] for c in range(lanes)], axis=1)
        own = jnp.broadcast_to(own, (n, rows))
        goes = (own >= block * rows) & (own < (block + 1) * rows)
        rank = lane_cumsum(goes.astype(jnp.int32)) - 1
        order_ref[flip : flip + 1, :] = jnp.sum(
            jnp.where(goes, rank + block * per_peer, 0), axis=0, keepdims=True)
    for k, copy in enumerate(body):
        copy.wait()
        part = slice(k * tall, (k + 1) * tall)
        scaled_ref[part, :] = (val_ref[part, :].astype(F32) * screen_ref[...]).astype(BF16)


def fetch_kernel(trial_hbm, cond_hbm, trial_ref, cond_ref, sems):
    copies = [
        pltpu.make_async_copy(trial_hbm, trial_ref, sems.at[0]),
        pltpu.make_async_copy(cond_hbm, cond_ref, sems.at[1]),
    ]
    for copy in copies:
        copy.start()
    for copy in copies:
        copy.wait()


def send_order(order, scaled, sent_ref):
    rows = sent_ref.shape[0]
    chunk = 128
    for c in range(rows // chunk):
        ids = lax.broadcasted_iota(jnp.int32, (chunk, rows), 0) + c * chunk
        pick = jnp.where(ids == order, 1.0, 0.0).astype(BF16)
        sent_ref[c * chunk : (c + 1) * chunk, :] = jnp.dot(
            pick, scaled, preferred_element_type=F32
        ).astype(BF16)


def sent_kernel(order_ref, scaled_ref, sent_ref):
    send_order(order_ref[0:1, :], scaled_ref[...], sent_ref)


def other_kernel(order_ref, screen_ref, val_ref, sent_ref):
    scaled = (val_ref[...].astype(F32) * screen_ref[...]).astype(BF16)
    send_order(order_ref[1:2, :], scaled, sent_ref)


def place_kernel(n, rows, me_ref, map_ref, ci_ref, vi_ref, ce_ref, ve_ref, slot_ref, gap_ref):
    per_peer = rows // n
    lanes = rows // 128
    gap_ref[...] = lookup(ce_ref, ci_ref[...]) - lookup(ve_ref, vi_ref[...])
    grid = jnp.concatenate([map_ref[pl.ds(c, n, stride=lanes), :] for c in range(lanes)], axis=1)
    slots = grid - me_ref[0] * rows
    lands = (slots >= 0) & (slots < rows)
    arrival = jnp.where(lands, lane_cumsum(lands.astype(jnp.int32)) - 1, -1)
    slots = slots.astype(F32)
    ids = lax.broadcasted_iota(jnp.int32, (per_peer, rows), 0)
    for q in range(n):
        hit = ids == arrival[q : q + 1, :]
        slot = jnp.sum(jnp.where(hit, slots[q : q + 1, :], 0.0), axis=1, keepdims=True)
        slot_ref[q * per_peer : (q + 1) * per_peer, :] = jnp.broadcast_to(slot, (per_peer, 128))


def tile_kernel(me_ref, val_ref, screen_ref, mine_ref, theirs_ref, out_ref):
    scaled = (val_ref[...].astype(F32) * screen_ref[...]).astype(BF16)
    chips, cols, _ = mine_ref.shape
    me = me_ref[0]
    for k in range(chips):
        for flip, cond_ref in enumerate((mine_ref, theirs_ref)):
            tile = lax.dot_general(
                scaled, cond_ref[k], (((1,), (1,)), ((), ())), preferred_element_type=F32
            )
            start = pl.multiple_of((me ^ (2 * k + flip)) * cols, 128)
            out_ref[0, :, pl.ds(start, cols)] = tile.astype(BF16)


def mixed_kernel(m, me_ref, vec_ref, cond_ref, keep_ref, give_ref):
    chips, vecs, cols = vec_ref.shape
    depth = cond_ref.shape[-1]
    odd = (me_ref[0] & 1) == 1
    vec = jnp.concatenate([vec_ref[k] for k in range(chips)], axis=1)
    total = jnp.dot(vec, cond_ref[...].reshape(chips * cols, depth), preferred_element_type=F32)
    half = vecs // (2 * m)
    for k in range(m):
        low = total[2 * k * half : (2 * k + 1) * half]
        high = total[(2 * k + 1) * half : (2 * k + 2) * half]
        keep_ref[k * half : (k + 1) * half, :] = jnp.where(odd, high, low)
        give_ref[k * half : (k + 1) * half, :] = jnp.where(odd, low, high).astype(BF16)


def apply_kernel(m, n, me_ref, keep_ref, take_ref, own_ref, other_ref, out_ref):
    half, width = out_ref.shape[1:]
    per_peer = width // 2
    odd = (me_ref[0] & 1) == 1
    mixed = (keep_ref[...] + take_ref[...].astype(F32)).astype(BF16)
    rows_last = (((1,), (1,)), ((), ()))
    own, other = (
        lax.dot_general(mixed, ref[...], rows_last, preferred_element_type=F32).astype(BF16)
        for ref in (own_ref, other_ref)
    )
    first, second = jnp.where(odd, other, own), jnp.where(odd, own, other)
    for d in range(n):
        at = slice(d * per_peer, (d + 1) * per_peer)
        for k in range(m):
            out_ref[d * m + k, :, :per_peer] = first[k * half : (k + 1) * half, at]
            out_ref[d * m + k, :, per_peer:] = second[k * half : (k + 1) * half, at]


def final_kernel(n, m, arrived_ref, slot_ref, gap_ref, trial_ref, out_ref, row_ref):
    width = out_ref.shape[1]
    half, pair = arrived_ref.shape[1:]
    for q in range(n):
        total = arrived_ref[q * m].astype(F32)
        for k in range(1, m):
            total = total + arrived_ref[q * m + k].astype(F32)
        at = (q & 1) * half
        row_ref[at : at + half, (q // 2) * pair : (q // 2 + 1) * pair] = total.astype(BF16)
    slot = slot_ref[...]
    lane = lax.broadcasted_iota(jnp.int32, slot.shape, 1).astype(F32)
    for c in range(0, width // 128, 2):
        lands = jnp.concatenate(
            [jnp.where(slot == lane + 128.0 * (c + k), 1.0, 0.0).astype(BF16) for k in range(2)], axis=1)
        moved = jnp.dot(row_ref[...], lands, preferred_element_type=F32)
        for k in range(2):
            part = slice((c + k) * 128, (c + k + 1) * 128)
            gap = gap_ref[c + k : c + k + 1, :]
            out_ref[:, part] = (
                gap * trial_ref[:, part].astype(F32) + moved[:, k * 128 : (k + 1) * 128]
            ).astype(BF16)


def per_device(
    mat_val,
    mat_cond,
    screening,
    trial_cols,
    trial_rows,
    row_map,
    val_index,
    cond_index,
    val_energy,
    cond_energy,
):
    n = lax.axis_size("pairs")
    m = lax.axis_size("rep")
    rows, depth = mat_val.shape
    cols = mat_cond.shape[0]
    vecs = trial_cols.shape[1]
    half = vecs // 2
    per_peer = rows // n
    own = lax.axis_index("pairs").astype(jnp.int32)
    layer = lax.axis_index("rep").astype(jnp.int32)
    odd = (own & 1) == 1
    me = own.reshape(1)
    screen = screening.reshape(1, depth)
    map_lanes = row_map.reshape(-1, 128)

    far_away = pl.BlockSpec(memory_space=pltpu.HBM)

    def in_hbm(x):
        return pltpu.with_memory_space_constraint(x, pltpu.HBM)

    val_other = exchange(mat_val, 1)
    trial, cond_own = pl.pallas_call(
        fetch_kernel,
        in_specs=[far_away, far_away],
        out_specs=(WHOLE, WHOLE),
        out_shape=(
            jax.ShapeDtypeStruct((vecs, cols), BF16),
            jax.ShapeDtypeStruct((cols, depth), BF16),
        ),
        scratch_shapes=[pltpu.SemaphoreType.DMA((2,))],
        cost_estimate=pl.CostEstimate(flops=0, bytes_accessed=4 * cols * depth, transcendentals=0),
        compiler_params=roomy(4),
        name="fetch",
    )(in_hbm(trial_cols.T), in_hbm(mat_cond))
    turns = [trial]
    for k in range(1, m):
        turns.append(lax.ppermute(trial_cols.T, "rep", [(i, (i + k) % m) for i in range(m)]))
    wide = []
    for k in range(m):
        block = turns[0]
        for t in range(1, m):
            block = jnp.where(lax.rem(layer - t + m, m) == k, turns[t], block)
        wide.append(block)
    wide = jnp.concatenate(wide)
    vec_all = jnp.stack([wide] + [exchange(wide, k) for k in range(2, n, 2)])
    mine = jnp.stack([cond_own] + [exchange(mat_cond, k) for k in range(2, n, 2)])
    theirs = exchange(mine, 1)
    scaled, order, screen_near = pl.pallas_call(
        lambda *refs: load_kernel(n, *refs),
        in_specs=[SCALAR] + [far_away] * 3,
        out_specs=(WHOLE, WHOLE, WHOLE),
        out_shape=(
            jax.ShapeDtypeStruct((rows, depth), BF16),
            jax.ShapeDtypeStruct((2, rows), jnp.int32),
            jax.ShapeDtypeStruct((1, depth), F32),
        ),
        scratch_shapes=[
            pltpu.VMEM((2 * rows // 128, 128), jnp.int32),
            pltpu.VMEM((rows, depth), BF16),
            pltpu.SemaphoreType.DMA((6,)),
        ],
        cost_estimate=pl.CostEstimate(flops=rows * depth, bytes_accessed=4 * rows * depth, transcendentals=0),
        compiler_params=roomy(8),
        name="load",
    )(me, in_hbm(map_lanes), in_hbm(mat_val), in_hbm(screen))
    sent_cost = pl.CostEstimate(
        flops=2 * rows * rows * depth, bytes_accessed=4 * rows * depth, transcendentals=0)
    sent = [
        pl.pallas_call(
            body,
            in_specs=[WHOLE] * len(given),
            out_specs=WHOLE,
            out_shape=jax.ShapeDtypeStruct((rows, depth), BF16),
            cost_estimate=sent_cost,
            compiler_params=roomy(6),
        )(*given)
        for body, given in ((sent_kernel, (order, scaled)), (other_kernel, (order, screen_near, val_other)))
    ]
    keep, give = pl.pallas_call(
        lambda *refs: mixed_kernel(m, *refs),
        in_specs=[SCALAR, WHOLE, WHOLE],
        out_specs=(WHOLE, WHOLE),
        out_shape=(
            jax.ShapeDtypeStruct((m * half, depth), F32),
            jax.ShapeDtypeStruct((m * half, depth), BF16),
        ),
        cost_estimate=pl.CostEstimate(
            flops=2 * m * vecs * n * cols * depth // 2, bytes_accessed=n * cols * depth, transcendentals=0),
        compiler_params=roomy(8),
        name="mixed",
    )(me, vec_all, mine)
    take = exchange(give, 1)

    if per_peer % 128 == 0:
        outgoing = pl.pallas_call(
            lambda *refs: apply_kernel(m, n, *refs),
            in_specs=[SCALAR] + [WHOLE] * 4,
            out_specs=WHOLE,
            compiler_params=roomy(8),
            out_shape=jax.ShapeDtypeStruct((n * m, half, 2 * per_peer), BF16),
            cost_estimate=pl.CostEstimate(
                flops=4 * rows * depth * m * half, bytes_accessed=4 * rows * depth, transcendentals=0),
            name="apply",
        )(me, keep, take, *sent)
    else:
        mixed = (keep + take.astype(F32)).astype(BF16)
        partial = jnp.einsum("vg,srg->svr", mixed, jnp.stack(sent), preferred_element_type=F32).astype(BF16)
        partial = in_order(odd, partial[0], partial[1]).reshape(2, m, half, n, per_peer)
        outgoing = partial.transpose(3, 1, 2, 0, 4).reshape(n * m, half, 2 * per_peer)
    arrived = lax.all_to_all(outgoing, ("pairs", "rep"), split_axis=0, concat_axis=0, tiled=True)

    tall = min(rows, 256)
    tiles = pl.pallas_call(
        tile_kernel,
        grid_spec=pltpu.PrefetchScalarGridSpec(
            num_scalar_prefetch=1,
            grid=(rows // tall,),
            in_specs=[
                pl.BlockSpec((tall, depth), lambda d, me: (d, 0)),
                pl.BlockSpec((1, depth), lambda d, me: (0, 0)),
                pl.BlockSpec((n // 2, cols, depth), lambda d, me: (0, 0, 0)),
                pl.BlockSpec((n // 2, cols, depth), lambda d, me: (0, 0, 0)),
            ],
            out_specs=pl.BlockSpec((1, tall, n * cols), lambda d, me: (0, d, 0)),
        ),
        out_shape=jax.ShapeDtypeStruct((1, rows, n * cols), BF16),
        cost_estimate=pl.CostEstimate(
            flops=2 * rows * depth * n * cols, bytes_accessed=2 * rows * (depth + n * cols), transcendentals=0),
        compiler_params=roomy(8),
        name="tiles",
    )(me, mat_val, screen, mine, theirs)

    slot, gap = pl.pallas_call(
        lambda *refs: place_kernel(n, rows, *refs),
        in_specs=[SCALAR] + [WHOLE] * 5,
        out_specs=(WHOLE, WHOLE),
        out_shape=(
            jax.ShapeDtypeStruct((rows, 128), F32),
            jax.ShapeDtypeStruct((rows // 128, 128), F32),
        ),
        cost_estimate=pl.CostEstimate(
            flops=8 * rows * rows, bytes_accessed=2 * rows * rows, transcendentals=0),
        compiler_params=roomy(8),
        name="place",
    )(
        me,
        map_lanes,
        cond_index.reshape(-1, 128),
        val_index.reshape(-1, 128),
        cond_energy.reshape(-1, 128),
        val_energy.reshape(-1, 128),
    )

    if per_peer % 128 != 0:
        arrived = jnp.sum(arrived.reshape(n // 2, 2, m, half, 2 * per_peer).astype(F32), axis=2).astype(BF16)
        arrived = arrived.transpose(1, 2, 0, 3).reshape(2, half, rows)
    parts, layers = (n, m) if per_peer % 128 == 0 else (2, 1)
    response = pl.pallas_call(
        lambda *refs: final_kernel(parts, layers, *refs),
        in_specs=[WHOLE] * 4,
        out_specs=WHOLE,
        compiler_params=roomy(8),
        out_shape=jax.ShapeDtypeStruct((vecs, rows), BF16),
        scratch_shapes=[pltpu.VMEM((vecs, rows), BF16)],
        cost_estimate=pl.CostEstimate(
            flops=2 * rows * rows * vecs, bytes_accessed=2 * rows * rows, transcendentals=0),
        name="final",
    )(arrived, slot, gap, trial_rows.T)
    return (response.T, tiles)


def solution(mesh):
    in_specs = (
        P("pairs", "rep"),
        P("pairs", "rep"),
        P("rep"),
        P("pairs", "rep"),
        P("pairs", "rep"),
        P(),
        P("pairs"),
        P("pairs"),
        P(),
        P(),
    )
    out_specs = (P("pairs", "rep"), P("rep", "pairs", None))

    return jax.shard_map(per_device, mesh=mesh, in_specs=in_specs, out_specs=out_specs, check_vma=False)
```

time: 49.1 us -> 49.7 us (1.012)
  waiting for transfers between devices: 13.7 us -> 17.3 us
  Pallas kernels: 10 us -> 13.2 us
  other arithmetic: 2.91 us -> 0.13 us
  local copies, waits for them, and re-layouts: 2.01 us -> 0.05 us
  starting transfers between devices: 19.1 us -> 17.9 us
    all_to_all x1, starting transfers between devices: 5.17 us -> 2.35 us  [per_device(): lax.all_to_all(outgoing, ('pairs', 'rep'), split_axis=0, concat_axis=0, t...]
    pallas_call x2 -> x5, Pallas kernels: 2.74 us -> 5.36 us  [the longest x2 2.59 us: per_device(): pl.pallas_call(body, in_specs=[WHOLE] * len(given), out_specs=WHOLE, out_...]
    ppermute x11 -> x12, waiting for transfers between devices: 5.3 us -> 7.82 us  [the longest x9 4.55 us: exchange(): return lax.ppermute(x, 'pairs', [(i, i ^ mask) for i in range(size)])]
    unnamed x18 -> x16, local copies, waits for them, and re-layouts: 1.96 us -> 0.05 us
    select_n x5 -> x0, other arithmetic: 1.84 us -> none  [the longest x1 1.05 us: cond_gather(): first, second = (jnp.where(odd, other, mine), jnp.where(odd, mine, other))]
    ppermute x11 -> x12, starting transfers between devices: 13.9 us -> 15.5 us  [the longest x9 10.3 us: exchange(): return lax.ppermute(x, 'pairs', [(i, i ^ mask) for i in range(size)])]
    all_to_all x1, waiting for transfers between devices: 8.39 us -> 9.45 us  [per_device(): lax.all_to_all(outgoing, ('pairs', 'rep'), split_axis=0, concat_axis=0, t...]
    pallas_call x1, Pallas kernels: 3.06 us -> 3.87 us  [per_device(): pl.pallas_call(tile_kernel, grid_spec=pltpu.PrefetchScalarGridSpec(num_sc...]
  transfers between devices with their start and end apart: 12 -> 13, of which waited for: 6 -> 6; matrix products, arithmetic and copies ran while one was open for 6% -> 0% of each run, Pallas kernels for 18% -> 21%
where the time goes in v2:
time: 49.7 us; the launch traced here: 49.3 us
  starting transfers between devices  17.9 us (36%)
  waiting for transfers between devices  17.3 us (35%)
  Pallas kernels  13.2 us (27%)
  between operations  0.82 us (2%)
    ppermute x9, starting transfers between devices, exchange(): return lax.ppermute(x, 'pairs', [(i, i ^ mask) for i in range(size)])  10.3 us
    all_to_all x1, waiting for transfers between devices, per_device(): lax.all_to_all(outgoing, ('pairs', 'rep'), split_axis=0, concat_axis=0, t...  9.45 us
    ppermute x3, starting transfers between devices, per_device(): lax.ppermute(trial_cols.T, 'rep', [(i, (i + k) % m) for i in range(m)])  5.25 us
    ppermute x9, waiting for transfers between devices, exchange(): return lax.ppermute(x, 'pairs', [(i, i ^ mask) for i in range(size)])  4.55 us
    pallas_call x1, Pallas kernels, per_device(): pl.pallas_call(tile_kernel, grid_spec=pltpu.PrefetchScalarGridSpec(num_sc...  3.87 us
    ppermute x3, waiting for transfers between devices, per_device(): lax.ppermute(trial_cols.T, 'rep', [(i, (i + k) % m) for i in range(m)])  3.27 us
    pallas_call x2, Pallas kernels, per_device(): pl.pallas_call(body, in_specs=[WHOLE] * len(given), out_specs=WHOLE, out_...  2.59 us
    all_to_all x1, starting transfers between devices, per_device(): lax.all_to_all(outgoing, ('pairs', 'rep'), split_axis=0, concat_axis=0, t...  2.35 us
  transfers between devices with their start and end apart: 13, of which 6 were waited for; matrix products, arithmetic and copies ran while one was open for 0% of the time, Pallas kernels for 21%

profile of v2, /device:TPU:1, one launch (start us, length us, event | category | flops | bytes accessed | tf_op | source)
XLA Modules:
  0.0 49.3 jit_solution(7475269356698882447)
XLA Ops:
  0.7 4.8 %collective-permute-start = (bf16[64,128]{1,0:T(8,128)(2,1)}, bf16[64,128]{1,0:T(8,128)(2,1)S(1)}, u32[]{:S(2)}, u32[]{:S(2)}) collective-permute-start(bf16[64,128]{1,0:T(8,128)(2,1)} %bitcast.36), channel_id=1, source_target_pairs={{0,3},{1,0},{2,1},{3,2},{4,7},{5,4},{6,5},{7,6},{8,11},{9,8},{10,9... | collective-permute-start | bytes 49160 | tf_op jit(solution)/shard_map/ppermute | solution.py:245
  5.5 0.5 collective-permute-start.2
  6.0 0.9 %fetch.1 = (bf16[64,128]{1,0:T(8,128)(2,1)S(1)}, bf16[128,512]{1,0:T(8,128)(2,1)S(1)}) custom-call(bf16[64,128]{1,0:T(8,128)(2,1)} %bitcast.39, bf16[128,512]{1,0:T(8,128)(2,1)} %cond_hbm.1), custom_call_target="tpu_custom_call" | custom-call | bytes 262144 | tf_op jit(solution)/shard_map/fetch/pallas_call | solution.py:230
  6.9 2.3 %collective-permute-done.1 = bf16[64,128]{1,0:T(8,128)(2,1)S(1)} collective-permute-done((bf16[64,128]{1,0:T(8,128)(2,1)}, bf16[64,128]{1,0:T(8,128)(2,1)S(1)}, u32[]{:S(2)}, u32[]{:S(2)}) %collective-permute-start.1) | collective-permute-done | bytes 16416 | tf_op jit(solution)/shard_map/ppermute | solution.py:245
  9.2 1.0 %collective-permute-done.2 = bf16[64,128]{1,0:T(8,128)(2,1)S(1)} collective-permute-done((bf16[64,128]{1,0:T(8,128)(2,1)}, bf16[64,128]{1,0:T(8,128)(2,1)S(1)}, u32[]{:S(2)}, u32[]{:S(2)}) %collective-permute-start.2) | collective-permute-done | bytes 16416 | tf_op jit(solution)/shard_map/ppermute | solution.py:245
  10.2 2.2 %collective-permute-start.5 = (bf16[256,128]{1,0:T(8,128)(2,1)S(1)}, bf16[256,128]{1,0:T(8,128)(2,1)S(1)}, u32[]{:S(2)}, u32[]{:S(2)}) collective-permute-start(bf16[256,128]{1,0:T(8,128)(2,1)S(1)} %get-tuple-element.21), channel_id=1, source_target_pairs={{0,24},{4,28},{8,16},{12,20},{16,8},{20,12},{24,0},{28,4},{1,25},{... | collective-permute-start | bytes 196616 | tf_op jit(solution)/shard_map/ppermute | solution.py:20
  12.9 2.2 %collective-permute-start.8 = (bf16[128,512]{1,0:T(8,128)(2,1)}, bf16[128,512]{1,0:T(8,128)(2,1)S(1)}, u32[]{:S(2)}, u32[]{:S(2)}) collective-permute-start(bf16[128,512]{1,0:T(8,128)(2,1)} %cond_hbm.1), channel_id=1, source_target_pairs={{0,24},{4,28},{8,16},{12,20},{16,8},{20,12},{24,0},{28,4},{1,25},{... | collective-permute-start | bytes 393224 | tf_op jit(solution)/shard_map/ppermute | solution.py:20
  15.1 0.5 collective-permute-start.7
  15.6 0.3 collective-permute-done.4
  15.9 0.9 %collective-permute-start.6 = (bf16[128,512]{1,0:T(8,128)(2,1)}, bf16[128,512]{1,0:T(8,128)(2,1)S(1)}, u32[]{:S(2)}, u32[]{:S(2)}) collective-permute-start(bf16[128,512]{1,0:T(8,128)(2,1)} %cond_hbm.1), channel_id=1, source_target_pairs={{0,8},{4,12},{8,0},{12,4},{16,24},{20,28},{24,16},{28,20},{1,9},{5... | collective-permute-start | bytes 393224 | tf_op jit(solution)/shard_map/ppermute | solution.py:20
  16.8 1.5 %load.1 = (bf16[1024,512]{1,0:T(8,128)(2,1)S(1)}, s32[2,1024]{1,0:T(2,128)S(1)}, f32[1,512]{1,0:T(1,128)S(1)}) custom-call(s32[1]{0:T(128)} %bitcast.refs_0_.me_ref, s32[64,128]{1,0:T(8,128)} %bitcast.20, bf16[1024,512]{1,0:T(8,128)(2,1)} %val_ref.1, f32[1,512]{1,0:T(1,128)} %bitcast.23), custom_call_target="tpu_custom_call" | custom-call | flops 524288 | bytes 2097152 | tf_op jit(solution)/shard_map/load/pallas_call | solution.py:256
  18.4 3.7 %collective-permute-done.7 = bf16[128,512]{1,0:T(8,128)(2,1)S(1)} collective-permute-done((bf16[128,512]{1,0:T(8,128)(2,1)}, bf16[128,512]{1,0:T(8,128)(2,1)S(1)}, u32[]{:S(2)}, u32[]{:S(2)}) %collective-permute-start.7) | collective-permute-done | bytes 131104 | tf_op jit(solution)/shard_map/ppermute | solution.py:20
  22.2 0.3 mixed.1
  22.5 3.6 %collective-permute-start.9 = (bf16[128,512]{1,0:T(8,128)(2,1)S(1)}, bf16[128,512]{1,0:T(8,128)(2,1)S(1)}, u32[]{:S(2)}, u32[]{:S(2)}) collective-permute-start(bf16[128,512]{1,0:T(8,128)(2,1)S(1)} %get-tuple-element.14), channel_id=1, source_target_pairs={{0,4},{4,0},{8,12},{12,8},{16,20},{20,16},{24,28},{28,24},{1,5},{5... | collective-permute-start | bytes 393224 | tf_op jit(solution)/shard_map/ppermute | solution.py:20
  26.1 1.3 %shard_map.113.refs_3_ = bf16[1024,512]{1,0:T(8,128)(2,1)S(1)} custom-call(s32[2,1024]{1,0:T(2,128)S(1)} %get-tuple-element.15.order_ref, bf16[1024,512]{1,0:T(8,128)(2,1)S(1)} %get-tuple-element.16.scaled_ref), custom_call_target="tpu_custom_call" | custom-call | flops 1073741824 | bytes 2097152 | tf_op jit(solution)/shard_map/pallas_call | solution.py:277
  27.4 1.3 %shard_map.114.refs_4_ = bf16[1024,512]{1,0:T(8,128)(2,1)S(1)} custom-call(s32[2,1024]{1,0:T(2,128)S(1)} %get-tuple-element.15.order_ref, f32[1,512]{1,0:T(1,128)S(1)} %get-tuple-element.17.screen_ref, bf16[1024,512]{1,0:T(8,128)(2,1)S(1)} %collective-permute-done.10.val_ref), custom_call_target="tpu_custom_call" | custom-call | flops 1073741824 | bytes 2097152 | tf_op jit(solution)/shard_map/pallas_call | solution.py:277
  28.8 1.6 %apply.1 = bf16[32,32,256]{2,1,0:T(8,128)(2,1)} custom-call(s32[1]{0:T(128)} %bitcast.refs_0_.me_ref, f32[128,512]{1,0:T(8,128)S(1)} %get-tuple-element.13.refs_1_, bf16[128,512]{1,0:T(8,128)(2,1)S(1)} %collective-permute-done.9.refs_2_, bf16[1024,512]{1,0:T(8,128)(2,1)S(1)} %shard_map.113.refs_3_, bf16[1024,512]{1,0:T(8,128)(2,1)S(1)} %shard_map.114.refs_4_), custom_call_target="tpu_custom_call" | custom-call | flops 268435456 | bytes 2097152 | tf_op jit(solution)/shard_map/apply/pallas_call | solution.py:303
  30.5 2.3 %all-to-all-start = ((bf16[32,32,256]{2,1,0:T(8,128)(2,1)}), bf16[32,32,256]{2,1,0:T(8,128)(2,1)S(1)}, u32[]{:S(2)}, u32[]{:S(2)}) async-start(bf16[32,32,256]{2,1,0:T(8,128)(2,1)} %apply.1), calls=%async_computation | async-start | bytes 1048576 | tf_op jit(solution)/shard_map/all_to_all | solution.py:318
  32.8 0.4 collective-permute-start.11
  33.2 1.1 %place.1 = (f32[1024,128]{1,0:T(8,128)S(1)}, f32[8,128]{1,0:T(8,128)S(1)}) custom-call(s32[1]{0:T(128)} %bitcast.refs_0_.me_ref, s32[64,128]{1,0:T(8,128)S(1)} %bitcast.21, s32[8,128]{1,0:T(8,128)S(1)} %bitcast.25, s32[8,128]{1,0:T(8,128)S(1)} %bitcast.26, f32[2,128]{1,0:T(2,128)S(1)} %bitcast.27, f32[1,128]{1,0:T(1,128)S(1)} %bitcast.28), custom_call_target="tpu_custom_call" | custom-call | flops 8388608 | bytes 2097152 | tf_op jit(solution)/shard_map/place/pallas_call | solution.py:341
  34.3 0.5 collective-permute-done.11.theirs_ref
  34.8 3.9 %tiles.1 = bf16[1,1024,1024]{2,1,0:T(8,128)(2,1)} custom-call(s32[1]{0:T(128)} %bitcast.refs_0_.me_ref, bf16[1024,512]{1,0:T(8,128)(2,1)S(1)} %copy-done, f32[1,512]{1,0:T(1,128)S(1)} %bitcast.24, bf16[4,128,512]{2,1,0:T(8,128)(2,1)S(1)} %pad_maximum_fusion.refs_2_.mine_ref, bf16[4,128,512]{2,1,0:T(8,128)(2,1)S(1)} %collective-permute-done.11.theirs_ref), custom_call_target="tpu_custom_call" | custom-call | flops 1073741824 | bytes 3145728 | tf_op jit(solution)/shard_map/tiles/pallas_call | solution.py:321
  38.7 9.4 %all-to-all-done.refs_0_ = bf16[32,32,256]{2,1,0:T(8,128)(2,1)S(1)} async-done(((bf16[32,32,256]{2,1,0:T(8,128)(2,1)}), bf16[32,32,256]{2,1,0:T(8,128)(2,1)S(1)}, u32[]{:S(2)}, u32[]{:S(2)}) %all-to-all-start) | async-done | bytes 524320 | tf_op jit(solution)/shard_map/all_to_all | solution.py:318
  48.1 1.2 %final.1 = bf16[64,1024]{1,0:T(8,128)(2,1)} custom-call(bf16[32,32,256]{2,1,0:T(8,128)(2,1)S(1)} %all-to-all-done.refs_0_, f32[1024,128]{1,0:T(8,128)S(1)} %get-tuple-element.18.refs_1_, f32[8,128]{1,0:T(8,128)S(1)} %get-tuple-element.19.refs_2_, bf16[64,1024]{1,0:T(8,128)(2,1)S(1)} %bitcast.19), custom_call_target="tpu_custom_call" | custom-call | flops 134217728 | bytes 2097152 | tf_op jit(solution)/shard_map/final/pallas_call | solution.py:366
  (31 shorter events, 0.8 us)
Async XLA Ops:
  0.6 26.8 %collective-permute-start.10 = (bf16[1024,512]{1,0:T(8,128)(2,1)}, bf16[1024,512]{1,0:T(8,128)(2,1)S(1)}, u32[]{:S(2)}, u32[]{:S(2)}) collective-permute-start(bf16[1024,512]{1,0:T(8,128)(2,1)} %val_ref.1), channel_id=1, source_target_pairs={{0,4},{4,0},{8,12},{12,8},{16,20},{20,16},{24,28},{28,24},{1,5},{5... | collective-permute-start | bytes 3145736 | tf_op jit(solution)/shard_map/ppermute | solution.py:20
  0.7 6.2 %collective-permute-start = (bf16[64,128]{1,0:T(8,128)(2,1)}, bf16[64,128]{1,0:T(8,128)(2,1)S(1)}, u32[]{:S(2)}, u32[]{:S(2)}) collective-permute-start(bf16[64,128]{1,0:T(8,128)(2,1)} %bitcast.36), channel_id=1, source_target_pairs={{0,3},{1,0},{2,1},{3,2},{4,7},{5,4},{6,5},{7,6},{8,11},{9,8},{10,9... | collective-permute-start | bytes 49160 | tf_op jit(solution)/shard_map/ppermute | solution.py:245
  5.5 3.7 %collective-permute-start.1 = (bf16[64,128]{1,0:T(8,128)(2,1)}, bf16[64,128]{1,0:T(8,128)(2,1)S(1)}, u32[]{:S(2)}, u32[]{:S(2)}) collective-permute-start(bf16[64,128]{1,0:T(8,128)(2,1)} %bitcast.37), channel_id=1, source_target_pairs={{0,2},{1,3},{2,0},{3,1},{4,6},{5,7},{6,4},{7,5},{8,10},{9,11},{10,... | collective-permute-start | bytes 49160 | tf_op jit(solution)/shard_map/ppermute | solution.py:245
  5.5 4.7 %collective-permute-start.2 = (bf16[64,128]{1,0:T(8,128)(2,1)}, bf16[64,128]{1,0:T(8,128)(2,1)S(1)}, u32[]{:S(2)}, u32[]{:S(2)}) collective-permute-start(bf16[64,128]{1,0:T(8,128)(2,1)} %bitcast.38), channel_id=1, source_target_pairs={{0,1},{1,2},{2,3},{3,0},{4,5},{5,6},{6,7},{7,4},{8,9},{9,10},{10,1... | collective-permute-start | bytes 49160 | tf_op jit(solution)/shard_map/ppermute | solution.py:245
  10.2 4.9 %collective-permute-start.5 = (bf16[256,128]{1,0:T(8,128)(2,1)S(1)}, bf16[256,128]{1,0:T(8,128)(2,1)S(1)}, u32[]{:S(2)}, u32[]{:S(2)}) collective-permute-start(bf16[256,128]{1,0:T(8,128)(2,1)S(1)} %get-tuple-element.21), channel_id=1, source_target_pairs={{0,24},{4,28},{8,16},{12,20},{16,8},{20,12},{24,0},{28,4},{1,25},{... | collective-permute-start | bytes 196616 | tf_op jit(solution)/shard_map/ppermute | solution.py:20
  12.5 3.4 %collective-permute-start.4 = (bf16[256,128]{1,0:T(8,128)(2,1)S(1)}, bf16[256,128]{1,0:T(8,128)(2,1)S(1)}, u32[]{:S(2)}, u32[]{:S(2)}) collective-permute-start(bf16[256,128]{1,0:T(8,128)(2,1)S(1)} %get-tuple-element.21), channel_id=1, source_target_pairs={{0,16},{4,20},{8,24},{12,28},{16,0},{20,4},{24,8},{28,12},{1,17},{... | collective-permute-start | bytes 196616 | tf_op jit(solution)/shard_map/ppermute | solution.py:20
  12.7 5.6 %collective-permute-start.3 = (bf16[256,128]{1,0:T(8,128)(2,1)S(1)}, bf16[256,128]{1,0:T(8,128)(2,1)S(1)}, u32[]{:S(2)}, u32[]{:S(2)}) collective-permute-start(bf16[256,128]{1,0:T(8,128)(2,1)S(1)} %get-tuple-element.21), channel_id=1, source_target_pairs={{0,8},{4,12},{8,0},{12,4},{16,24},{20,28},{24,16},{28,20},{1,9},{5... | collective-permute-start | bytes 196616 | tf_op jit(solution)/shard_map/ppermute | solution.py:20
  12.9 5.4 %collective-permute-start.8 = (bf16[128,512]{1,0:T(8,128)(2,1)}, bf16[128,512]{1,0:T(8,128)(2,1)S(1)}, u32[]{:S(2)}, u32[]{:S(2)}) collective-permute-start(bf16[128,512]{1,0:T(8,128)(2,1)} %cond_hbm.1), channel_id=1, source_target_pairs={{0,24},{4,28},{8,16},{12,20},{16,8},{20,12},{24,0},{28,4},{1,25},{... | collective-permute-start | bytes 393224 | tf_op jit(solution)/shard_map/ppermute | solution.py:20
  15.1 7.0 %collective-permute-start.7 = (bf16[128,512]{1,0:T(8,128)(2,1)}, bf16[128,512]{1,0:T(8,128)(2,1)S(1)}, u32[]{:S(2)}, u32[]{:S(2)}) collective-permute-start(bf16[128,512]{1,0:T(8,128)(2,1)} %cond_hbm.1), channel_id=1, source_target_pairs={{0,16},{4,20},{8,24},{12,28},{16,0},{20,4},{24,8},{28,12},{1,17},{... | collective-permute-start | bytes 393224 | tf_op jit(solution)/shard_map/ppermute | solution.py:20
  15.9 6.2 %collective-permute-start.6 = (bf16[128,512]{1,0:T(8,128)(2,1)}, bf16[128,512]{1,0:T(8,128)(2,1)S(1)}, u32[]{:S(2)}, u32[]{:S(2)}) collective-permute-start(bf16[128,512]{1,0:T(8,128)(2,1)} %cond_hbm.1), channel_id=1, source_target_pairs={{0,8},{4,12},{8,0},{12,4},{16,24},{20,28},{24,16},{28,20},{1,9},{5... | collective-permute-start | bytes 393224 | tf_op jit(solution)/shard_map/ppermute | solution.py:20
  22.5 6.3 %collective-permute-start.9 = (bf16[128,512]{1,0:T(8,128)(2,1)S(1)}, bf16[128,512]{1,0:T(8,128)(2,1)S(1)}, u32[]{:S(2)}, u32[]{:S(2)}) collective-permute-start(bf16[128,512]{1,0:T(8,128)(2,1)S(1)} %get-tuple-element.14), channel_id=1, source_target_pairs={{0,4},{4,0},{8,12},{12,8},{16,20},{20,16},{24,28},{28,24},{1,5},{5... | collective-permute-start | bytes 393224 | tf_op jit(solution)/shard_map/ppermute | solution.py:20
  28.7 4.5 %copy-start.2 = (s32[8192]{0:T(1024)S(1)}, s32[8192]{0:T(1024)}, u32[]{:S(2)}) copy-start(s32[8192]{0:T(1024)} %param.15) | copy-start | bytes 98308
  28.7 4.4 %copy-start.4 = (s32[1024]{0:T(1024)S(1)}, s32[1024]{0:T(1024)}, u32[]{:S(2)}) copy-start(s32[1024]{0:T(1024)} %param.17) | copy-start | bytes 12292
  28.8 4.4 %copy-start.5 = (s32[1024]{0:T(1024)S(1)}, s32[1024]{0:T(1024)}, u32[]{:S(2)}) copy-start(s32[1024]{0:T(1024)} %param.16) | copy-start | bytes 12292
  28.8 4.4 %copy-start.6 = (f32[256]{0:T(256)S(1)}, f32[256]{0:T(256)}, u32[]{:S(2)}) copy-start(f32[256]{0:T(256)} %param.19) | copy-start | bytes 3076
  28.8 4.4 %copy-start.7 = (f32[128]{0:T(128)S(1)}, f32[128]{0:T(128)}, u32[]{:S(2)}) copy-start(f32[128]{0:T(128)} %param.18) | copy-start | bytes 1540
  28.8 6.0 %copy-start = (bf16[1024,512]{1,0:T(8,128)(2,1)S(1)}, bf16[1024,512]{1,0:T(8,128)(2,1)}, u32[]{:S(2)}) copy-start(bf16[1024,512]{1,0:T(8,128)(2,1)} %val_ref.1) | copy-start | bytes 3145732
  28.8 6.0 %copy-start.3 = (f32[512]{0:T(512)S(1)}, f32[512]{0:T(512)}, u32[]{:S(2)}) copy-start(f32[512]{0:T(512)} %param.12) | copy-start | bytes 6148
  30.5 17.7 %all-to-all-start = ((bf16[32,32,256]{2,1,0:T(8,128)(2,1)}), bf16[32,32,256]{2,1,0:T(8,128)(2,1)S(1)}, u32[]{:S(2)}, u32[]{:S(2)}) async-start(bf16[32,32,256]{2,1,0:T(8,128)(2,1)} %apply.1), calls=%async_computation | async-start | bytes 1048576 | tf_op jit(solution)/shard_map/all_to_all | solution.py:318
  32.8 2.0 %collective-permute-start.11 = (bf16[4,128,512]{2,1,0:T(8,128)(2,1)S(1)}, bf16[4,128,512]{2,1,0:T(8,128)(2,1)S(1)}, u32[]{:S(2)}, u32[]{:S(2)}) collective-permute-start(bf16[4,128,512]{2,1,0:T(8,128)(2,1)S(1)} %pad_maximum_fusion.refs_2_.mine_ref), channel_id=1, source_target_pairs={{0,4},{4,0},{8,12},{12,8},{16,20},{20,16},{24,28},{28,24},{1,5},{5... | collective-permute-start | bytes 1572872 | tf_op jit(solution)/shard_map/ppermute | solution.py:20
  34.3 13.8 %copy-start.1 = (bf16[1024,64]{0,1:T(8,128)(2,1)S(1)}, bf16[1024,64]{0,1:T(8,128)(2,1)}, u32[]{:S(2)}) copy-start(bf16[1024,64]{0,1:T(8,128)(2,1)} %param.14) | copy-start | bytes 393220

commit v3 on v2

--- a/solution.py
+++ b/solution.py
@@ -106,9 +106,11 @@
     send_order(order_ref[0:1, :], scaled_ref[...], sent_ref)
 
 
-def other_kernel(order_ref, screen_ref, val_ref, sent_ref):
-    scaled = (val_ref[...].astype(F32) * screen_ref[...]).astype(BF16)
-    send_order(order_ref[1:2, :], scaled, sent_ref)
+def other_kernel(parity, me_ref, order_ref, screen_ref, val_ref, *refs):
+    @pl.when((me_ref[0] & 1) == parity)
+    def _():
+        scaled = (val_ref[...].astype(F32) * screen_ref[...]).astype(BF16)
+        send_order(order_ref[1:2, :], scaled, refs[-1])
 
 
 def place_kernel(n, rows, me_ref, map_ref, ci_ref, vi_ref, ce_ref, ve_ref, slot_ref, gap_ref):
@@ -154,22 +156,35 @@
         give_ref[k * half : (k + 1) * half, :] = jnp.where(odd, low, high).astype(BF16)
 
 
-def apply_kernel(m, n, me_ref, keep_ref, take_ref, own_ref, other_ref, out_ref):
+def apply_kernel(m, n, me_ref, keep_ref, take_ref, own_ref, other_ref, out_hbm, out_ref, sems):
     half, width = out_ref.shape[1:]
     per_peer = width // 2
     odd = (me_ref[0] & 1) == 1
     mixed = (keep_ref[...] + take_ref[...].astype(F32)).astype(BF16)
-    rows_last = (((1,), (1,)), ((), ()))
-    own, other = (
-        lax.dot_general(mixed, ref[...], rows_last, preferred_element_type=F32).astype(BF16)
-        for ref in (own_ref, other_ref)
-    )
-    first, second = jnp.where(odd, other, own), jnp.where(odd, own, other)
-    for d in range(n):
-        at = slice(d * per_peer, (d + 1) * per_peer)
-        for k in range(m):
-            out_ref[d * m + k, :, :per_peer] = first[k * half : (k + 1) * half, at]
-            out_ref[d * m + k, :, per_peer:] = second[k * half : (k + 1) * half, at]
+    shares = sems.shape[0]
+    tall = own_ref.shape[0] // shares
+    blocks = (n // shares) * m
+    copies = []
+    for share in range(shares):
+        part = slice(share * tall, (share + 1) * tall)
+        own, other = (
+            lax.dot_general(
+                mixed, ref[part, :], (((1,), (1,)), ((), ())), preferred_element_type=F32
+            ).astype(BF16)
+            for ref in (own_ref, other_ref)
+        )
+        first, second = jnp.where(odd, other, own), jnp.where(odd, own, other)
+        for d in range(n // shares):
+            at = slice(d * per_peer, (d + 1) * per_peer)
+            for k in range(m):
+                to = share * blocks + d * m + k
+                out_ref[to, :, :per_peer] = first[k * half : (k + 1) * half, at]
+                out_ref[to, :, per_peer:] = second[k * half : (k + 1) * half, at]
+        some = pl.ds(share * blocks, blocks)
+        copies.append(pltpu.make_async_copy(out_ref.at[some], out_hbm.at[some], sems.at[share]))
+        copies[-1].start()
+    for copy in copies:
+        copy.wait()
 
 
 def final_kernel(n, m, arrived_ref, slot_ref, gap_ref, trial_ref, out_ref, row_ref):
@@ -273,17 +288,28 @@
     )(me, in_hbm(map_lanes), in_hbm(mat_val), in_hbm(screen))
     sent_cost = pl.CostEstimate(
         flops=2 * rows * rows * depth, bytes_accessed=4 * rows * depth, transcendentals=0)
-    sent = [
-        pl.pallas_call(
-            body,
-            in_specs=[WHOLE] * len(given),
+    sent_shape = jax.ShapeDtypeStruct((rows, depth), BF16)
+    sent = pl.pallas_call(
+        sent_kernel,
+        in_specs=[WHOLE] * 2,
+        out_specs=WHOLE,
+        out_shape=sent_shape,
+        cost_estimate=sent_cost,
+        compiler_params=roomy(6),
+        name="sent0",
+    )(order, scaled)
+    sent_other = ()
+    for parity in (1, 0):
+        sent_other = (pl.pallas_call(
+            lambda *refs, parity=parity: other_kernel(parity, *refs),
+            in_specs=[SCALAR] + [WHOLE] * (3 + len(sent_other)),
             out_specs=WHOLE,
-            out_shape=jax.ShapeDtypeStruct((rows, depth), BF16),
+            out_shape=sent_shape,
+            input_output_aliases={4: 0} if sent_other else {},
             cost_estimate=sent_cost,
             compiler_params=roomy(6),
-        )(*given)
-        for body, given in ((sent_kernel, (order, scaled)), (other_kernel, (order, screen_near, val_other)))
-    ]
+        )(me, order, screen_near, val_other, *sent_other),)
+    sent = (sent, *sent_other)
     keep, give = pl.pallas_call(
         lambda *refs: mixed_kernel(m, *refs),
         in_specs=[SCALAR, WHOLE, WHOLE],
@@ -303,7 +329,11 @@
         outgoing = pl.pallas_call(
             lambda *refs: apply_kernel(m, n, *refs),
             in_specs=[SCALAR] + [WHOLE] * 4,
-            out_specs=WHOLE,
+            out_specs=pl.BlockSpec(memory_space=pltpu.HBM),
+            scratch_shapes=[
+                pltpu.VMEM((n * m, half, 2 * per_peer), BF16),
+                pltpu.SemaphoreType.DMA((2,)),
+            ],
             compiler_params=roomy(8),
             out_shape=jax.ShapeDtypeStruct((n * m, half, 2 * per_peer), BF16),
             cost_estimate=pl.CostEstimate(

time: 49.7 us -> 48 us (0.966)
  starting transfers between devices: 17.9 us -> 16.2 us
    ppermute x9, starting transfers between devices: 10.3 us -> 8.54 us  [exchange(): return lax.ppermute(x, 'pairs', [(i, i ^ mask) for i in range(size)])]
    pallas_call x2 -> x3, Pallas kernels: 2.59 us -> 2.6 us  [the longest x2 1.34 us: per_device(): pl.pallas_call(lambda *refs, parity=parity: other_kernel(parity, *refs),...]
  transfers between devices with their start and end apart: 13 -> 13, of which waited for: 6 -> 5; matrix products, arithmetic and copies ran while one was open for 0% -> 0% of each run, Pallas kernels for 21% -> 22%
where the time goes in v3:
time: 48 us; the launch traced here: 47.6 us
  waiting for transfers between devices  17.3 us (36%)
  starting transfers between devices  16.2 us (34%)
  Pallas kernels  13.1 us (27%)
  between operations  0.84 us (2%)
    all_to_all x1, waiting for transfers between devices, per_device(): lax.all_to_all(outgoing, ('pairs', 'rep'), split_axis=0, concat_axis=0, t...  9.42 us
    ppermute x9, starting transfers between devices, exchange(): return lax.ppermute(x, 'pairs', [(i, i ^ mask) for i in range(size)])  8.54 us
    ppermute x3, starting transfers between devices, per_device(): lax.ppermute(trial_cols.T, 'rep', [(i, (i + k) % m) for i in range(m)])  5.25 us
    ppermute x9, waiting for transfers between devices, exchange(): return lax.ppermute(x, 'pairs', [(i, i ^ mask) for i in range(size)])  4.56 us
    pallas_call x1, Pallas kernels, per_device(): pl.pallas_call(tile_kernel, grid_spec=pltpu.PrefetchScalarGridSpec(num_sc...  3.87 us
    ppermute x3, waiting for transfers between devices, per_device(): lax.ppermute(trial_cols.T, 'rep', [(i, (i + k) % m) for i in range(m)])  3.27 us
    all_to_all x1, starting transfers between devices, per_device(): lax.all_to_all(outgoing, ('pairs', 'rep'), split_axis=0, concat_axis=0, t...  2.4 us
    pallas_call x1, Pallas kernels, per_device(): pl.pallas_call(lambda *refs: apply_kernel(m, n, *refs), in_specs=[SCALAR]...  1.54 us
  transfers between devices with their start and end apart: 13, of which 5 were waited for; matrix products, arithmetic and copies ran while one was open for 0% of the time, Pallas kernels for 22%

profile of v3, /device:TPU:1, one launch (start us, length us, event | category | flops | bytes accessed | tf_op | source)
XLA Modules:
  0.0 47.6 jit_solution(2808931323061892429)
XLA Ops:
  0.7 4.8 %collective-permute-start = (bf16[64,128]{1,0:T(8,128)(2,1)}, bf16[64,128]{1,0:T(8,128)(2,1)S(1)}, u32[]{:S(2)}, u32[]{:S(2)}) collective-permute-start(bf16[64,128]{1,0:T(8,128)(2,1)} %bitcast.36), channel_id=1, source_target_pairs={{0,3},{1,0},{2,1},{3,2},{4,7},{5,4},{6,5},{7,6},{8,11},{9,8},{10,9... | collective-permute-start | bytes 49160 | tf_op jit(solution)/shard_map/ppermute | solution.py:260
  5.5 0.5 collective-permute-start.2
  6.0 0.9 %fetch.1 = (bf16[64,128]{1,0:T(8,128)(2,1)S(1)}, bf16[128,512]{1,0:T(8,128)(2,1)S(1)}) custom-call(bf16[64,128]{1,0:T(8,128)(2,1)} %bitcast.39, bf16[128,512]{1,0:T(8,128)(2,1)} %cond_hbm.1), custom_call_target="tpu_custom_call" | custom-call | bytes 262144 | tf_op jit(solution)/shard_map/fetch/pallas_call | solution.py:245
  6.9 2.3 %collective-permute-done.1 = bf16[64,128]{1,0:T(8,128)(2,1)S(1)} collective-permute-done((bf16[64,128]{1,0:T(8,128)(2,1)}, bf16[64,128]{1,0:T(8,128)(2,1)S(1)}, u32[]{:S(2)}, u32[]{:S(2)}) %collective-permute-start.1) | collective-permute-done | bytes 16416 | tf_op jit(solution)/shard_map/ppermute | solution.py:260
  9.2 1.0 %collective-permute-done.2 = bf16[64,128]{1,0:T(8,128)(2,1)S(1)} collective-permute-done((bf16[64,128]{1,0:T(8,128)(2,1)}, bf16[64,128]{1,0:T(8,128)(2,1)S(1)}, u32[]{:S(2)}, u32[]{:S(2)}) %collective-permute-start.2) | collective-permute-done | bytes 16416 | tf_op jit(solution)/shard_map/ppermute | solution.py:260
  10.2 2.2 %collective-permute-start.5 = (bf16[256,128]{1,0:T(8,128)(2,1)S(1)}, bf16[256,128]{1,0:T(8,128)(2,1)S(1)}, u32[]{:S(2)}, u32[]{:S(2)}) collective-permute-start(bf16[256,128]{1,0:T(8,128)(2,1)S(1)} %get-tuple-element.21), channel_id=1, source_target_pairs={{0,24},{4,28},{8,16},{12,20},{16,8},{20,12},{24,0},{28,4},{1,25},{... | collective-permute-start | bytes 196616 | tf_op jit(solution)/shard_map/ppermute | solution.py:20
  12.5 0.2 collective-permute-start.4
  12.7 1.2 %collective-permute-start.8 = (bf16[128,512]{1,0:T(8,128)(2,1)}, bf16[128,512]{1,0:T(8,128)(2,1)S(1)}, u32[]{:S(2)}, u32[]{:S(2)}) collective-permute-start(bf16[128,512]{1,0:T(8,128)(2,1)} %cond_hbm.1), channel_id=1, source_target_pairs={{0,24},{4,28},{8,16},{12,20},{16,8},{20,12},{24,0},{28,4},{1,25},{... | collective-permute-start | bytes 393224 | tf_op jit(solution)/shard_map/ppermute | solution.py:20
  14.1 1.5 %load.1 = (bf16[1024,512]{1,0:T(8,128)(2,1)S(1)}, s32[2,1024]{1,0:T(2,128)S(1)}, f32[1,512]{1,0:T(1,128)S(1)}) custom-call(s32[1]{0:T(128)} %bitcast.refs_0_.me_ref, s32[64,128]{1,0:T(8,128)} %bitcast.20, bf16[1024,512]{1,0:T(8,128)(2,1)} %val_ref.1, f32[1,512]{1,0:T(1,128)} %bitcast.23), custom_call_target="tpu_custom_call" | custom-call | flops 524288 | bytes 2097152 | tf_op jit(solution)/shard_map/load/pallas_call | solution.py:271
  15.7 1.3 %collective-permute-start.6 = (bf16[128,512]{1,0:T(8,128)(2,1)}, bf16[128,512]{1,0:T(8,128)(2,1)S(1)}, u32[]{:S(2)}, u32[]{:S(2)}) collective-permute-start(bf16[128,512]{1,0:T(8,128)(2,1)} %cond_hbm.1), channel_id=1, source_target_pairs={{0,8},{4,12},{8,0},{12,4},{16,24},{20,28},{24,16},{28,20},{1,9},{5... | collective-permute-start | bytes 393224 | tf_op jit(solution)/shard_map/ppermute | solution.py:20
  17.0 0.3 collective-permute-start.3
  17.2 1.3 %sent0.1.refs_3_ = bf16[1024,512]{1,0:T(8,128)(2,1)S(1)} custom-call(s32[2,1024]{1,0:T(2,128)S(1)} %get-tuple-element.15.order_ref.refs_1_, bf16[1024,512]{1,0:T(8,128)(2,1)S(1)} %get-tuple-element.16.scaled_ref), custom_call_target="tpu_custom_call" | custom-call | flops 1073741824 | bytes 2097152 | tf_op jit(solution)/shard_map/sent0/pallas_call | solution.py:292
  18.5 4.0 %collective-permute-done.3 = bf16[256,128]{1,0:T(8,128)(2,1)S(1)} collective-permute-done((bf16[256,128]{1,0:T(8,128)(2,1)S(1)}, bf16[256,128]{1,0:T(8,128)(2,1)S(1)}, u32[]{:S(2)}, u32[]{:S(2)}) %collective-permute-start.3) | collective-permute-done | bytes 65568 | tf_op jit(solution)/shard_map/ppermute | solution.py:20
  22.7 0.3 mixed.1
  23.0 2.7 %collective-permute-start.9 = (bf16[128,512]{1,0:T(8,128)(2,1)S(1)}, bf16[128,512]{1,0:T(8,128)(2,1)S(1)}, u32[]{:S(2)}, u32[]{:S(2)}) collective-permute-start(bf16[128,512]{1,0:T(8,128)(2,1)S(1)} %get-tuple-element.14), channel_id=1, source_target_pairs={{0,4},{4,0},{8,12},{12,8},{16,20},{20,16},{24,28},{28,24},{1,5},{5... | collective-permute-start | bytes 393224 | tf_op jit(solution)/shard_map/ppermute | solution.py:20
  25.7 1.3 %shard_map.113.refs_4_ = bf16[1024,512]{1,0:T(8,128)(2,1)S(1)} custom-call(s32[1]{0:T(128)} %bitcast.refs_0_.me_ref, s32[2,1024]{1,0:T(2,128)S(1)} %get-tuple-element.15.order_ref.refs_1_, f32[1,512]{1,0:T(1,128)S(1)} %get-tuple-element.17.refs_2_, bf16[1024,512]{1,0:T(8,128)(2,1)S(1)} %collective-permute-done.10.refs_3_), custom_call_target="tpu_custom_call" | custom-call | flops 1073741824 | bytes 2097152 | tf_op jit(solution)/shard_map/pallas_call | solution.py:303
  27.1 1.5 %apply.1 = bf16[32,32,256]{2,1,0:T(8,128)(2,1)} custom-call(s32[1]{0:T(128)} %bitcast.refs_0_.me_ref, f32[128,512]{1,0:T(8,128)S(1)} %get-tuple-element.13.refs_1_, bf16[128,512]{1,0:T(8,128)(2,1)S(1)} %collective-permute-done.9.refs_2_, bf16[1024,512]{1,0:T(8,128)(2,1)S(1)} %sent0.1.refs_3_, bf16[1024,512]{1,0:T(8,128)(2,1)S(1)} %shard_map.114.refs_4_), custom_call_target="tpu_custom_call" | custom-call | flops 268435456 | bytes 2097152 | tf_op jit(solution)/shard_map/apply/pallas_call | solution.py:329
  28.7 2.4 %all-to-all-start = ((bf16[32,32,256]{2,1,0:T(8,128)(2,1)}), bf16[32,32,256]{2,1,0:T(8,128)(2,1)S(1)}, u32[]{:S(2)}, u32[]{:S(2)}) async-start(bf16[32,32,256]{2,1,0:T(8,128)(2,1)} %apply.1), calls=%async_computation | async-start | bytes 1048576 | tf_op jit(solution)/shard_map/all_to_all | solution.py:348
  31.1 0.3 collective-permute-start.11
  31.4 1.1 %place.1 = (f32[1024,128]{1,0:T(8,128)S(1)}, f32[8,128]{1,0:T(8,128)S(1)}) custom-call(s32[1]{0:T(128)} %bitcast.refs_0_.me_ref, s32[64,128]{1,0:T(8,128)S(1)} %bitcast.21, s32[8,128]{1,0:T(8,128)S(1)} %bitcast.25, s32[8,128]{1,0:T(8,128)S(1)} %bitcast.26, f32[2,128]{1,0:T(2,128)S(1)} %bitcast.27, f32[1,128]{1,0:T(1,128)S(1)} %bitcast.28), custom_call_target="tpu_custom_call" | custom-call | flops 8388608 | bytes 2097152 | tf_op jit(solution)/shard_map/place/pallas_call | solution.py:371
  32.6 0.5 %collective-permute-done.11.theirs_ref = bf16[4,128,512]{2,1,0:T(8,128)(2,1)S(1)} collective-permute-done((bf16[4,128,512]{2,1,0:T(8,128)(2,1)S(1)}, bf16[4,128,512]{2,1,0:T(8,128)(2,1)S(1)}, u32[]{:S(2)}, u32[]{:S(2)}) %collective-permute-start.11) | collective-permute-done | bytes 524320 | tf_op jit(solution)/shard_map/ppermute | solution.py:20
  33.1 3.9 %tiles.1 = bf16[1,1024,1024]{2,1,0:T(8,128)(2,1)} custom-call(s32[1]{0:T(128)} %bitcast.refs_0_.me_ref, bf16[1024,512]{1,0:T(8,128)(2,1)S(1)} %copy-done, f32[1,512]{1,0:T(1,128)S(1)} %bitcast.24, bf16[4,128,512]{2,1,0:T(8,128)(2,1)S(1)} %pad_maximum_fusion.refs_2_.mine_ref, bf16[4,128,512]{2,1,0:T(8,128)(2,1)S(1)} %collective-permute-done.11.theirs_ref), custom_call_target="tpu_custom_call" | custom-call | flops 1073741824 | bytes 3145728 | tf_op jit(solution)/shard_map/tiles/pallas_call | solution.py:351
  36.9 9.4 %all-to-all-done.refs_0_ = bf16[32,32,256]{2,1,0:T(8,128)(2,1)S(1)} async-done(((bf16[32,32,256]{2,1,0:T(8,128)(2,1)}), bf16[32,32,256]{2,1,0:T(8,128)(2,1)S(1)}, u32[]{:S(2)}, u32[]{:S(2)}) %all-to-all-start) | async-done | bytes 524320 | tf_op jit(solution)/shard_map/all_to_all | solution.py:348
  46.4 1.2 %final.1 = bf16[64,1024]{1,0:T(8,128)(2,1)} custom-call(bf16[32,32,256]{2,1,0:T(8,128)(2,1)S(1)} %all-to-all-done.refs_0_, f32[1024,128]{1,0:T(8,128)S(1)} %get-tuple-element.18.refs_1_, f32[8,128]{1,0:T(8,128)S(1)} %get-tuple-element.19.refs_2_, bf16[64,1024]{1,0:T(8,128)(2,1)S(1)} %bitcast.19), custom_call_target="tpu_custom_call" | custom-call | flops 134217728 | bytes 2097152 | tf_op jit(solution)/shard_map/final/pallas_call | solution.py:396
  (32 shorter events, 0.5 us)
Async XLA Ops:
  0.6 25.1 %collective-permute-start.10 = (bf16[1024,512]{1,0:T(8,128)(2,1)}, bf16[1024,512]{1,0:T(8,128)(2,1)S(1)}, u32[]{:S(2)}, u32[]{:S(2)}) collective-permute-start(bf16[1024,512]{1,0:T(8,128)(2,1)} %val_ref.1), channel_id=1, source_target_pairs={{0,4},{4,0},{8,12},{12,8},{16,20},{20,16},{24,28},{28,24},{1,5},{5... | collective-permute-start | bytes 3145736 | tf_op jit(solution)/shard_map/ppermute | solution.py:20
  0.7 6.2 %collective-permute-start = (bf16[64,128]{1,0:T(8,128)(2,1)}, bf16[64,128]{1,0:T(8,128)(2,1)S(1)}, u32[]{:S(2)}, u32[]{:S(2)}) collective-permute-start(bf16[64,128]{1,0:T(8,128)(2,1)} %bitcast.36), channel_id=1, source_target_pairs={{0,3},{1,0},{2,1},{3,2},{4,7},{5,4},{6,5},{7,6},{8,11},{9,8},{10,9... | collective-permute-start | bytes 49160 | tf_op jit(solution)/shard_map/ppermute | solution.py:260
  5.5 3.7 %collective-permute-start.1 = (bf16[64,128]{1,0:T(8,128)(2,1)}, bf16[64,128]{1,0:T(8,128)(2,1)S(1)}, u32[]{:S(2)}, u32[]{:S(2)}) collective-permute-start(bf16[64,128]{1,0:T(8,128)(2,1)} %bitcast.37), channel_id=1, source_target_pairs={{0,2},{1,3},{2,0},{3,1},{4,6},{5,7},{6,4},{7,5},{8,10},{9,11},{10,... | collective-permute-start | bytes 49160 | tf_op jit(solution)/shard_map/ppermute | solution.py:260
  5.5 4.7 %collective-permute-start.2 = (bf16[64,128]{1,0:T(8,128)(2,1)}, bf16[64,128]{1,0:T(8,128)(2,1)S(1)}, u32[]{:S(2)}, u32[]{:S(2)}) collective-permute-start(bf16[64,128]{1,0:T(8,128)(2,1)} %bitcast.38), channel_id=1, source_target_pairs={{0,1},{1,2},{2,3},{3,0},{4,5},{5,6},{6,7},{7,4},{8,9},{9,10},{10,1... | collective-permute-start | bytes 49160 | tf_op jit(solution)/shard_map/ppermute | solution.py:260
  10.2 5.4 %collective-permute-start.5 = (bf16[256,128]{1,0:T(8,128)(2,1)S(1)}, bf16[256,128]{1,0:T(8,128)(2,1)S(1)}, u32[]{:S(2)}, u32[]{:S(2)}) collective-permute-start(bf16[256,128]{1,0:T(8,128)(2,1)S(1)} %get-tuple-element.21), channel_id=1, source_target_pairs={{0,24},{4,28},{8,16},{12,20},{16,8},{20,12},{24,0},{28,4},{1,25},{... | collective-permute-start | bytes 196616 | tf_op jit(solution)/shard_map/ppermute | solution.py:20
  12.5 4.5 %collective-permute-start.4 = (bf16[256,128]{1,0:T(8,128)(2,1)S(1)}, bf16[256,128]{1,0:T(8,128)(2,1)S(1)}, u32[]{:S(2)}, u32[]{:S(2)}) collective-permute-start(bf16[256,128]{1,0:T(8,128)(2,1)S(1)} %get-tuple-element.21), channel_id=1, source_target_pairs={{0,16},{4,20},{8,24},{12,28},{16,0},{20,4},{24,8},{28,12},{1,17},{... | collective-permute-start | bytes 196616 | tf_op jit(solution)/shard_map/ppermute | solution.py:20
  12.7 9.9 %collective-permute-start.8 = (bf16[128,512]{1,0:T(8,128)(2,1)}, bf16[128,512]{1,0:T(8,128)(2,1)S(1)}, u32[]{:S(2)}, u32[]{:S(2)}) collective-permute-start(bf16[128,512]{1,0:T(8,128)(2,1)} %cond_hbm.1), channel_id=1, source_target_pairs={{0,24},{4,28},{8,16},{12,20},{16,8},{20,12},{24,0},{28,4},{1,25},{... | collective-permute-start | bytes 393224 | tf_op jit(solution)/shard_map/ppermute | solution.py:20
  13.9 8.7 %collective-permute-start.7 = (bf16[128,512]{1,0:T(8,128)(2,1)}, bf16[128,512]{1,0:T(8,128)(2,1)S(1)}, u32[]{:S(2)}, u32[]{:S(2)}) collective-permute-start(bf16[128,512]{1,0:T(8,128)(2,1)} %cond_hbm.1), channel_id=1, source_target_pairs={{0,16},{4,20},{8,24},{12,28},{16,0},{20,4},{24,8},{28,12},{1,17},{... | collective-permute-start | bytes 393224 | tf_op jit(solution)/shard_map/ppermute | solution.py:20
  15.7 6.9 %collective-permute-start.6 = (bf16[128,512]{1,0:T(8,128)(2,1)}, bf16[128,512]{1,0:T(8,128)(2,1)S(1)}, u32[]{:S(2)}, u32[]{:S(2)}) collective-permute-start(bf16[128,512]{1,0:T(8,128)(2,1)} %cond_hbm.1), channel_id=1, source_target_pairs={{0,8},{4,12},{8,0},{12,4},{16,24},{20,28},{24,16},{28,20},{1,9},{5... | collective-permute-start | bytes 393224 | tf_op jit(solution)/shard_map/ppermute | solution.py:20
  17.0 5.6 %collective-permute-start.3 = (bf16[256,128]{1,0:T(8,128)(2,1)S(1)}, bf16[256,128]{1,0:T(8,128)(2,1)S(1)}, u32[]{:S(2)}, u32[]{:S(2)}) collective-permute-start(bf16[256,128]{1,0:T(8,128)(2,1)S(1)} %get-tuple-element.21), channel_id=1, source_target_pairs={{0,8},{4,12},{8,0},{12,4},{16,24},{20,28},{24,16},{28,20},{1,9},{5... | collective-permute-start | bytes 196616 | tf_op jit(solution)/shard_map/ppermute | solution.py:20
  23.0 4.1 %collective-permute-start.9 = (bf16[128,512]{1,0:T(8,128)(2,1)S(1)}, bf16[128,512]{1,0:T(8,128)(2,1)S(1)}, u32[]{:S(2)}, u32[]{:S(2)}) collective-permute-start(bf16[128,512]{1,0:T(8,128)(2,1)S(1)} %get-tuple-element.14), channel_id=1, source_target_pairs={{0,4},{4,0},{8,12},{12,8},{16,20},{20,16},{24,28},{28,24},{1,5},{5... | collective-permute-start | bytes 393224 | tf_op jit(solution)/shard_map/ppermute | solution.py:20
  27.0 4.4 %copy-start.2 = (s32[8192]{0:T(1024)S(1)}, s32[8192]{0:T(1024)}, u32[]{:S(2)}) copy-start(s32[8192]{0:T(1024)} %param.15) | copy-start | bytes 98308
  27.0 4.4 %copy-start.4 = (s32[1024]{0:T(1024)S(1)}, s32[1024]{0:T(1024)}, u32[]{:S(2)}) copy-start(s32[1024]{0:T(1024)} %param.17) | copy-start | bytes 12292
  27.1 4.4 %copy-start.5 = (s32[1024]{0:T(1024)S(1)}, s32[1024]{0:T(1024)}, u32[]{:S(2)}) copy-start(s32[1024]{0:T(1024)} %param.16) | copy-start | bytes 12292
  27.1 4.4 %copy-start.6 = (f32[256]{0:T(256)S(1)}, f32[256]{0:T(256)}, u32[]{:S(2)}) copy-start(f32[256]{0:T(256)} %param.19) | copy-start | bytes 3076
  27.1 4.4 %copy-start.7 = (f32[128]{0:T(128)S(1)}, f32[128]{0:T(128)}, u32[]{:S(2)}) copy-start(f32[128]{0:T(128)} %param.18) | copy-start | bytes 1540
  27.1 6.0 %copy-start = (bf16[1024,512]{1,0:T(8,128)(2,1)S(1)}, bf16[1024,512]{1,0:T(8,128)(2,1)}, u32[]{:S(2)}) copy-start(bf16[1024,512]{1,0:T(8,128)(2,1)} %val_ref.1) | copy-start | bytes 3145732
  27.1 6.0 %copy-start.3 = (f32[512]{0:T(512)S(1)}, f32[512]{0:T(512)}, u32[]{:S(2)}) copy-start(f32[512]{0:T(512)} %param.12) | copy-start | bytes 6148
  28.7 17.7 %all-to-all-start = ((bf16[32,32,256]{2,1,0:T(8,128)(2,1)}), bf16[32,32,256]{2,1,0:T(8,128)(2,1)S(1)}, u32[]{:S(2)}, u32[]{:S(2)}) async-start(bf16[32,32,256]{2,1,0:T(8,128)(2,1)} %apply.1), calls=%async_computation | async-start | bytes 1048576 | tf_op jit(solution)/shard_map/all_to_all | solution.py:348
  31.1 2.0 %collective-permute-start.11 = (bf16[4,128,512]{2,1,0:T(8,128)(2,1)S(1)}, bf16[4,128,512]{2,1,0:T(8,128)(2,1)S(1)}, u32[]{:S(2)}, u32[]{:S(2)}) collective-permute-start(bf16[4,128,512]{2,1,0:T(8,128)(2,1)S(1)} %pad_maximum_fusion.refs_2_.mine_ref), channel_id=1, source_target_pairs={{0,4},{4,0},{8,12},{12,8},{16,20},{20,16},{24,28},{28,24},{1,5},{5... | collective-permute-start | bytes 1572872 | tf_op jit(solution)/shard_map/ppermute | solution.py:20
  32.6 13.8 %copy-start.1 = (bf16[1024,64]{0,1:T(8,128)(2,1)S(1)}, bf16[1024,64]{0,1:T(8,128)(2,1)}, u32[]{:S(2)}) copy-start(bf16[1024,64]{0,1:T(8,128)(2,1)} %param.14) | copy-start | bytes 393220

commit v4 on v3

--- a/solution.py
+++ b/solution.py
@@ -18,6 +18,11 @@
 def exchange(x, mask):
     size = lax.axis_size("pairs")
     return lax.ppermute(x, "pairs", [(i, i ^ mask) for i in range(size)])
+
+
+def split_exchange(x, even_mask, odd_mask):
+    size = lax.axis_size("pairs")
+    return lax.ppermute(x, "pairs", [(i, i ^ (odd_mask if i & 1 else even_mask)) for i in range(size)])
 
 
 def in_order(odd, own, partner):
@@ -266,7 +271,12 @@
         wide.append(block)
     wide = jnp.concatenate(wide)
     vec_all = jnp.stack([wide] + [exchange(wide, k) for k in range(2, n, 2)])
-    mine = jnp.stack([cond_own] + [exchange(mat_cond, k) for k in range(2, n, 2)])
+    if n == 8:
+        near = split_exchange(mat_cond, 2, 4)
+        far = split_exchange(jnp.stack([cond_own, near]), 4, 2)
+        mine = jnp.stack([cond_own, jnp.where(odd, far[0], near), jnp.where(odd, near, far[0]), far[1]])
+    else:
+        mine = jnp.stack([cond_own] + [exchange(mat_cond, k) for k in range(2, n, 2)])
     theirs = exchange(mine, 1)
     scaled, order, screen_near = pl.pallas_call(
         lambda *refs: load_kernel(n, *refs),

time: 48 us -> 45.9 us (0.956)
  waiting for transfers between devices: 17.3 us -> 13.5 us
  starting transfers between devices: 16.2 us -> 17.8 us
    ppermute x3, waiting for transfers between devices: 3.27 us -> 0.01 us  [per_device(): lax.ppermute(trial_cols.T, 'rep', [(i, (i + k) % m) for i in range(m)])]
    all_to_all x1, starting transfers between devices: 2.4 us -> 4.22 us  [per_device(): lax.all_to_all(outgoing, ('pairs', 'rep'), split_axis=0, concat_axis=0, t...]
    ppermute x0 -> x2, starting transfers between devices: none -> 1.56 us  [split_exchange(): lax.ppermute(x, 'pairs', [(i, i ^ (odd_mask if i & 1 else even_mask)) for...]
    ppermute x9 -> x6, starting transfers between devices: 8.54 us -> 7.33 us  [exchange(): return lax.ppermute(x, 'pairs', [(i, i ^ mask) for i in range(size)])]
    ppermute x3, starting transfers between devices: 5.25 us -> 4.65 us  [per_device(): lax.ppermute(trial_cols.T, 'rep', [(i, (i + k) % m) for i in range(m)])]
    ppermute x9 -> x6, waiting for transfers between devices: 4.56 us -> 4.08 us  [exchange(): return lax.ppermute(x, 'pairs', [(i, i ^ mask) for i in range(size)])]
  transfers between devices with their start and end apart: 13 -> 12, of which waited for: 5 -> 4; matrix products, arithmetic and copies ran while one was open for 0% -> 0% of each run, Pallas kernels for 22% -> 23%
where the time goes in v4:
time: 45.9 us; the launch traced here: 45.5 us
  starting transfers between devices  17.8 us (39%)
  waiting for transfers between devices  13.5 us (29%)
  Pallas kernels  13.1 us (29%)
  between operations  0.9 us (2%)
    all_to_all x1, waiting for transfers between devices, per_device(): lax.all_to_all(outgoing, ('pairs', 'rep'), split_axis=0, concat_axis=0, t...  9.41 us
    ppermute x6, starting transfers between devices, exchange(): return lax.ppermute(x, 'pairs', [(i, i ^ mask) for i in range(size)])  7.33 us
    ppermute x3, starting transfers between devices, per_device(): lax.ppermute(trial_cols.T, 'rep', [(i, (i + k) % m) for i in range(m)])  4.65 us
    all_to_all x1, starting transfers between devices, per_device(): lax.all_to_all(outgoing, ('pairs', 'rep'), split_axis=0, concat_axis=0, t...  4.22 us
    ppermute x6, waiting for transfers between devices, exchange(): return lax.ppermute(x, 'pairs', [(i, i ^ mask) for i in range(size)])  4.08 us
    pallas_call x1, Pallas kernels, per_device(): pl.pallas_call(tile_kernel, grid_spec=pltpu.PrefetchScalarGridSpec(num_sc...  3.88 us
    ppermute x2, starting transfers between devices, split_exchange(): lax.ppermute(x, 'pairs', [(i, i ^ (odd_mask if i & 1 else even_mask)) for...  1.56 us
    pallas_call x1, Pallas kernels, per_device(): pl.pallas_call(lambda *refs: apply_kernel(m, n, *refs), in_specs=[SCALAR]...  1.54 us
  transfers between devices with their start and end apart: 12, of which 4 were waited for; matrix products, arithmetic and copies ran while one was open for 0% of the time, Pallas kernels for 23%

profile of v4, /device:TPU:1, one launch (start us, length us, event | category | flops | bytes accessed | tf_op | source)
XLA Modules:
  0.0 45.5 jit_solution(16130847424615928145)
XLA Ops:
  0.6 4.2 %collective-permute-start = (bf16[64,128]{1,0:T(8,128)(2,1)}, bf16[64,128]{1,0:T(8,128)(2,1)S(1)}, u32[]{:S(2)}, u32[]{:S(2)}) collective-permute-start(bf16[64,128]{1,0:T(8,128)(2,1)} %bitcast.43), channel_id=1, source_target_pairs={{0,3},{1,0},{2,1},{3,2},{4,7},{5,4},{6,5},{7,6},{8,11},{9,8},{10,9... | collective-permute-start | bytes 49160 | tf_op jit(solution)/shard_map/ppermute | solution.py:265
  4.8 0.5 collective-permute-start.2
  5.3 1.2 %collective-permute-start.6 = (bf16[128,512]{1,0:T(8,128)(2,1)}, bf16[128,512]{1,0:T(8,128)(2,1)S(1)}, u32[]{:S(2)}, u32[]{:S(2)}) collective-permute-start(bf16[128,512]{1,0:T(8,128)(2,1)} %cond_hbm.1), channel_id=1, source_target_pairs={{0,8},{4,20},{8,0},{12,28},{16,24},{20,4},{24,16},{28,12},{1,9},{5... | collective-permute-start | bytes 393224 | tf_op jit(solution)/shard_map/ppermute | solution.py:25
  6.5 1.8 %collective-permute-start.9 = (bf16[1024,512]{1,0:T(8,128)(2,1)}, bf16[1024,512]{1,0:T(8,128)(2,1)S(1)}, u32[]{:S(2)}, u32[]{:S(2)}) collective-permute-start(bf16[1024,512]{1,0:T(8,128)(2,1)} %val_ref.1), channel_id=1, source_target_pairs={{0,4},{4,0},{8,12},{12,8},{16,20},{20,16},{24,28},{28,24},{1,5},{5... | collective-permute-start | bytes 3145736 | tf_op jit(solution)/shard_map/ppermute | solution.py:20
  8.3 0.9 %fetch.1 = (bf16[64,128]{1,0:T(8,128)(2,1)S(1)}, bf16[128,512]{1,0:T(8,128)(2,1)S(1)}) custom-call(bf16[64,128]{1,0:T(8,128)(2,1)} %bitcast.46, bf16[128,512]{1,0:T(8,128)(2,1)} %cond_hbm.1), custom_call_target="tpu_custom_call" | custom-call | bytes 262144 | tf_op jit(solution)/shard_map/fetch/pallas_call | solution.py:250
  9.3 1.5 %load.1 = (bf16[1024,512]{1,0:T(8,128)(2,1)S(1)}, s32[2,1024]{1,0:T(2,128)S(1)}, f32[1,512]{1,0:T(1,128)S(1)}) custom-call(s32[1]{0:T(128)} %bitcast.refs_0_.me_ref, s32[64,128]{1,0:T(8,128)} %bitcast.30, bf16[1024,512]{1,0:T(8,128)(2,1)} %val_ref.1, f32[1,512]{1,0:T(1,128)} %bitcast.32), custom_call_target="tpu_custom_call" | custom-call | flops 524288 | bytes 2097152 | tf_op jit(solution)/shard_map/load/pallas_call | solution.py:281
  10.9 0.3 collective-permute-start.7
  11.2 2.2 %collective-permute-start.5 = (bf16[256,128]{1,0:T(8,128)(2,1)S(1)}, bf16[256,128]{1,0:T(8,128)(2,1)S(1)}, u32[]{:S(2)}, u32[]{:S(2)}) collective-permute-start(bf16[256,128]{1,0:T(8,128)(2,1)S(1)} %get-tuple-element.23), channel_id=1, source_target_pairs={{0,24},{4,28},{8,16},{12,20},{16,8},{20,12},{24,0},{28,4},{1,25},{... | collective-permute-start | bytes 196616 | tf_op jit(solution)/shard_map/ppermute | solution.py:20
  13.5 0.2 collective-permute-start.4
  13.7 0.3 collective-permute-start.3
  14.0 1.3 %sent0.1.refs_3_ = bf16[1024,512]{1,0:T(8,128)(2,1)S(1)} custom-call(s32[2,1024]{1,0:T(2,128)S(1)} %get-tuple-element.15.order_ref.refs_1_, bf16[1024,512]{1,0:T(8,128)(2,1)S(1)} %get-tuple-element.16.scaled_ref), custom_call_target="tpu_custom_call" | custom-call | flops 1073741824 | bytes 2097152 | tf_op jit(solution)/shard_map/sent0/pallas_call | solution.py:302
  15.2 3.4 %collective-permute-done.5 = bf16[256,128]{1,0:T(8,128)(2,1)S(1)} collective-permute-done((bf16[256,128]{1,0:T(8,128)(2,1)S(1)}, bf16[256,128]{1,0:T(8,128)(2,1)S(1)}, u32[]{:S(2)}, u32[]{:S(2)}) %collective-permute-start.5) | collective-permute-done | bytes 65568 | tf_op jit(solution)/shard_map/ppermute | solution.py:20
  18.6 0.2 collective-permute-done.4
  19.0 0.3 mixed.1
  19.3 2.5 %collective-permute-start.8 = (bf16[128,512]{1,0:T(8,128)(2,1)S(1)}, bf16[128,512]{1,0:T(8,128)(2,1)S(1)}, u32[]{:S(2)}, u32[]{:S(2)}) collective-permute-start(bf16[128,512]{1,0:T(8,128)(2,1)S(1)} %get-tuple-element.14), channel_id=1, source_target_pairs={{0,4},{4,0},{8,12},{12,8},{16,20},{20,16},{24,28},{28,24},{1,5},{5... | collective-permute-start | bytes 393224 | tf_op jit(solution)/shard_map/ppermute | solution.py:20
  21.8 1.3 %shard_map.113.refs_4_ = bf16[1024,512]{1,0:T(8,128)(2,1)S(1)} custom-call(s32[1]{0:T(128)} %bitcast.refs_0_.me_ref, s32[2,1024]{1,0:T(2,128)S(1)} %get-tuple-element.15.order_ref.refs_1_, f32[1,512]{1,0:T(1,128)S(1)} %get-tuple-element.17.refs_2_, bf16[1024,512]{1,0:T(8,128)(2,1)S(1)} %collective-permute-done.9.refs_3_), custom_call_target="tpu_custom_call" | custom-call | flops 1073741824 | bytes 2097152 | tf_op jit(solution)/shard_map/pallas_call | solution.py:313
  23.3 1.5 %apply.1 = bf16[32,32,256]{2,1,0:T(8,128)(2,1)} custom-call(s32[1]{0:T(128)} %bitcast.refs_0_.me_ref, f32[128,512]{1,0:T(8,128)S(1)} %get-tuple-element.13.refs_1_, bf16[128,512]{1,0:T(8,128)(2,1)S(1)} %collective-permute-done.8.refs_2_, bf16[1024,512]{1,0:T(8,128)(2,1)S(1)} %sent0.1.refs_3_, bf16[1024,512]{1,0:T(8,128)(2,1)S(1)} %shard_map.114.refs_4_), custom_call_target="tpu_custom_call" | custom-call | flops 268435456 | bytes 2097152 | tf_op jit(solution)/shard_map/apply/pallas_call | solution.py:339
  24.8 4.2 %all-to-all-start = ((bf16[32,32,256]{2,1,0:T(8,128)(2,1)}), bf16[32,32,256]{2,1,0:T(8,128)(2,1)S(1)}, u32[]{:S(2)}, u32[]{:S(2)}) async-start(bf16[32,32,256]{2,1,0:T(8,128)(2,1)} %apply.1), calls=%async_computation | async-start | bytes 1048576 | tf_op jit(solution)/shard_map/all_to_all | solution.py:358
  29.1 0.3 collective-permute-start.10
  29.4 1.1 %place.1 = (f32[1024,128]{1,0:T(8,128)S(1)}, f32[8,128]{1,0:T(8,128)S(1)}) custom-call(s32[1]{0:T(128)} %bitcast.refs_0_.me_ref, s32[64,128]{1,0:T(8,128)S(1)} %bitcast.31, s32[8,128]{1,0:T(8,128)S(1)} %bitcast.34, s32[8,128]{1,0:T(8,128)S(1)} %bitcast.35, f32[2,128]{1,0:T(2,128)S(1)} %bitcast.36, f32[1,128]{1,0:T(1,128)S(1)} %bitcast.37), custom_call_target="tpu_custom_call" | custom-call | flops 8388608 | bytes 2097152 | tf_op jit(solution)/shard_map/place/pallas_call | solution.py:381
  30.5 0.5 %collective-permute-done.10.theirs_ref = bf16[4,128,512]{2,1,0:T(8,128)(2,1)S(1)} collective-permute-done((bf16[4,128,512]{2,1,0:T(8,128)(2,1)S(1)}, bf16[4,128,512]{2,1,0:T(8,128)(2,1)S(1)}, u32[]{:S(2)}, u32[]{:S(2)}) %collective-permute-start.10) | collective-permute-done | bytes 524320 | tf_op jit(solution)/shard_map/ppermute | solution.py:20
  31.0 3.9 %tiles.1 = bf16[1,1024,1024]{2,1,0:T(8,128)(2,1)} custom-call(s32[1]{0:T(128)} %bitcast.refs_0_.me_ref, bf16[1024,512]{1,0:T(8,128)(2,1)S(1)} %copy-done, f32[1,512]{1,0:T(1,128)S(1)} %bitcast.33, bf16[4,128,512]{2,1,0:T(8,128)(2,1)S(1)} %pad_maximum_fusion.refs_2_.mine_ref, bf16[4,128,512]{2,1,0:T(8,128)(2,1)S(1)} %collective-permute-done.10.theirs_ref), custom_call_target="tpu_custom_call" | custom-call | flops 1073741824 | bytes 3145728 | tf_op jit(solution)/shard_map/tiles/pallas_call | solution.py:361
  34.9 9.4 %all-to-all-done.refs_0_ = bf16[32,32,256]{2,1,0:T(8,128)(2,1)S(1)} async-done(((bf16[32,32,256]{2,1,0:T(8,128)(2,1)}), bf16[32,32,256]{2,1,0:T(8,128)(2,1)S(1)}, u32[]{:S(2)}, u32[]{:S(2)}) %all-to-all-start) | async-done | bytes 524320 | tf_op jit(solution)/shard_map/all_to_all | solution.py:358
  44.3 1.2 %final.1 = bf16[64,1024]{1,0:T(8,128)(2,1)} custom-call(bf16[32,32,256]{2,1,0:T(8,128)(2,1)S(1)} %all-to-all-done.refs_0_, f32[1024,128]{1,0:T(8,128)S(1)} %get-tuple-element.18.refs_1_, f32[8,128]{1,0:T(8,128)S(1)} %get-tuple-element.19.refs_2_, bf16[64,1024]{1,0:T(8,128)(2,1)S(1)} %bitcast.29), custom_call_target="tpu_custom_call" | custom-call | flops 134217728 | bytes 2097152 | tf_op jit(solution)/shard_map/final/pallas_call | solution.py:406
  (33 shorter events, 0.3 us)
Async XLA Ops:
  0.6 10.2 %collective-permute-start = (bf16[64,128]{1,0:T(8,128)(2,1)}, bf16[64,128]{1,0:T(8,128)(2,1)S(1)}, u32[]{:S(2)}, u32[]{:S(2)}) collective-permute-start(bf16[64,128]{1,0:T(8,128)(2,1)} %bitcast.43), channel_id=1, source_target_pairs={{0,3},{1,0},{2,1},{3,2},{4,7},{5,4},{6,5},{7,6},{8,11},{9,8},{10,9... | collective-permute-start | bytes 49160 | tf_op jit(solution)/shard_map/ppermute | solution.py:265
  4.8 6.0 %collective-permute-start.1 = (bf16[64,128]{1,0:T(8,128)(2,1)}, bf16[64,128]{1,0:T(8,128)(2,1)S(1)}, u32[]{:S(2)}, u32[]{:S(2)}) collective-permute-start(bf16[64,128]{1,0:T(8,128)(2,1)} %bitcast.44), channel_id=1, source_target_pairs={{0,2},{1,3},{2,0},{3,1},{4,6},{5,7},{6,4},{7,5},{8,10},{9,11},{10,... | collective-permute-start | bytes 49160 | tf_op jit(solution)/shard_map/ppermute | solution.py:265
  4.8 6.0 %collective-permute-start.2 = (bf16[64,128]{1,0:T(8,128)(2,1)}, bf16[64,128]{1,0:T(8,128)(2,1)S(1)}, u32[]{:S(2)}, u32[]{:S(2)}) collective-permute-start(bf16[64,128]{1,0:T(8,128)(2,1)} %bitcast.45), channel_id=1, source_target_pairs={{0,1},{1,2},{2,3},{3,0},{4,5},{5,6},{6,7},{7,4},{8,9},{9,10},{10,1... | collective-permute-start | bytes 49160 | tf_op jit(solution)/shard_map/ppermute | solution.py:265
  5.3 5.6 %collective-permute-start.6 = (bf16[128,512]{1,0:T(8,128)(2,1)}, bf16[128,512]{1,0:T(8,128)(2,1)S(1)}, u32[]{:S(2)}, u32[]{:S(2)}) collective-permute-start(bf16[128,512]{1,0:T(8,128)(2,1)} %cond_hbm.1), channel_id=1, source_target_pairs={{0,8},{4,20},{8,0},{12,28},{16,24},{20,4},{24,16},{28,12},{1,9},{5... | collective-permute-start | bytes 393224 | tf_op jit(solution)/shard_map/ppermute | solution.py:25
  6.5 15.3 %collective-permute-start.9 = (bf16[1024,512]{1,0:T(8,128)(2,1)}, bf16[1024,512]{1,0:T(8,128)(2,1)S(1)}, u32[]{:S(2)}, u32[]{:S(2)}) collective-permute-start(bf16[1024,512]{1,0:T(8,128)(2,1)} %val_ref.1), channel_id=1, source_target_pairs={{0,4},{4,0},{8,12},{12,8},{16,20},{20,16},{24,28},{28,24},{1,5},{5... | collective-permute-start | bytes 3145736 | tf_op jit(solution)/shard_map/ppermute | solution.py:20
  10.9 7.9 %collective-permute-start.7 = (bf16[2,128,512]{2,1,0:T(8,128)(2,1)S(1)}, bf16[2,128,512]{2,1,0:T(8,128)(2,1)S(1)}, u32[]{:S(2)}, u32[]{:S(2)}) collective-permute-start(bf16[2,128,512]{2,1,0:T(8,128)(2,1)S(1)} %pad_maximum_fusion.2), channel_id=1, source_target_pairs={{0,16},{4,12},{8,24},{12,4},{16,0},{20,28},{24,8},{28,20},{1,17},{... | collective-permute-start | bytes 786440 | tf_op jit(solution)/shard_map/ppermute | solution.py:25
  11.2 7.4 %collective-permute-start.5 = (bf16[256,128]{1,0:T(8,128)(2,1)S(1)}, bf16[256,128]{1,0:T(8,128)(2,1)S(1)}, u32[]{:S(2)}, u32[]{:S(2)}) collective-permute-start(bf16[256,128]{1,0:T(8,128)(2,1)S(1)} %get-tuple-element.23), channel_id=1, source_target_pairs={{0,24},{4,28},{8,16},{12,20},{16,8},{20,12},{24,0},{28,4},{1,25},{... | collective-permute-start | bytes 196616 | tf_op jit(solution)/shard_map/ppermute | solution.py:20
  13.5 5.3 %collective-permute-start.4 = (bf16[256,128]{1,0:T(8,128)(2,1)S(1)}, bf16[256,128]{1,0:T(8,128)(2,1)S(1)}, u32[]{:S(2)}, u32[]{:S(2)}) collective-permute-start(bf16[256,128]{1,0:T(8,128)(2,1)S(1)} %get-tuple-element.23), channel_id=1, source_target_pairs={{0,16},{4,20},{8,24},{12,28},{16,0},{20,4},{24,8},{28,12},{1,17},{... | collective-permute-start | bytes 196616 | tf_op jit(solution)/shard_map/ppermute | solution.py:20
  13.7 5.1 %collective-permute-start.3 = (bf16[256,128]{1,0:T(8,128)(2,1)S(1)}, bf16[256,128]{1,0:T(8,128)(2,1)S(1)}, u32[]{:S(2)}, u32[]{:S(2)}) collective-permute-start(bf16[256,128]{1,0:T(8,128)(2,1)S(1)} %get-tuple-element.23), channel_id=1, source_target_pairs={{0,8},{4,12},{8,0},{12,4},{16,24},{20,28},{24,16},{28,20},{1,9},{5... | collective-permute-start | bytes 196616 | tf_op jit(solution)/shard_map/ppermute | solution.py:20
  19.3 4.0 %collective-permute-start.8 = (bf16[128,512]{1,0:T(8,128)(2,1)S(1)}, bf16[128,512]{1,0:T(8,128)(2,1)S(1)}, u32[]{:S(2)}, u32[]{:S(2)}) collective-permute-start(bf16[128,512]{1,0:T(8,128)(2,1)S(1)} %get-tuple-element.14), channel_id=1, source_target_pairs={{0,4},{4,0},{8,12},{12,8},{16,20},{20,16},{24,28},{28,24},{1,5},{5... | collective-permute-start | bytes 393224 | tf_op jit(solution)/shard_map/ppermute | solution.py:20
  23.2 6.2 %copy-start.2 = (s32[8192]{0:T(1024)S(1)}, s32[8192]{0:T(1024)}, u32[]{:S(2)}) copy-start(s32[8192]{0:T(1024)} %param.15) | copy-start | bytes 98308
  23.2 6.2 %copy-start.4 = (s32[1024]{0:T(1024)S(1)}, s32[1024]{0:T(1024)}, u32[]{:S(2)}) copy-start(s32[1024]{0:T(1024)} %param.17) | copy-start | bytes 12292
  23.2 6.2 %copy-start.5 = (s32[1024]{0:T(1024)S(1)}, s32[1024]{0:T(1024)}, u32[]{:S(2)}) copy-start(s32[1024]{0:T(1024)} %param.16) | copy-start | bytes 12292
  23.2 6.2 %copy-start.6 = (f32[256]{0:T(256)S(1)}, f32[256]{0:T(256)}, u32[]{:S(2)}) copy-start(f32[256]{0:T(256)} %param.19) | copy-start | bytes 3076
  23.2 6.2 %copy-start.7 = (f32[128]{0:T(128)S(1)}, f32[128]{0:T(128)}, u32[]{:S(2)}) copy-start(f32[128]{0:T(128)} %param.18) | copy-start | bytes 1540
  23.2 7.8 %copy-start = (bf16[1024,512]{1,0:T(8,128)(2,1)S(1)}, bf16[1024,512]{1,0:T(8,128)(2,1)}, u32[]{:S(2)}) copy-start(bf16[1024,512]{1,0:T(8,128)(2,1)} %val_ref.1) | copy-start | bytes 3145732
  23.2 7.8 %copy-start.3 = (f32[512]{0:T(512)S(1)}, f32[512]{0:T(512)}, u32[]{:S(2)}) copy-start(f32[512]{0:T(512)} %param.12) | copy-start | bytes 6148
  24.8 19.5 %all-to-all-start = ((bf16[32,32,256]{2,1,0:T(8,128)(2,1)}), bf16[32,32,256]{2,1,0:T(8,128)(2,1)S(1)}, u32[]{:S(2)}, u32[]{:S(2)}) async-start(bf16[32,32,256]{2,1,0:T(8,128)(2,1)} %apply.1), calls=%async_computation | async-start | bytes 1048576 | tf_op jit(solution)/shard_map/all_to_all | solution.py:358
  29.1 2.0 %collective-permute-start.10 = (bf16[4,128,512]{2,1,0:T(8,128)(2,1)S(1)}, bf16[4,128,512]{2,1,0:T(8,128)(2,1)S(1)}, u32[]{:S(2)}, u32[]{:S(2)}) collective-permute-start(bf16[4,128,512]{2,1,0:T(8,128)(2,1)S(1)} %pad_maximum_fusion.refs_2_.mine_ref), channel_id=1, source_target_pairs={{0,4},{4,0},{8,12},{12,8},{16,20},{20,16},{24,28},{28,24},{1,5},{5... | collective-permute-start | bytes 1572872 | tf_op jit(solution)/shard_map/ppermute | solution.py:20
  30.5 13.8 %copy-start.1 = (bf16[1024,64]{0,1:T(8,128)(2,1)S(1)}, bf16[1024,64]{0,1:T(8,128)(2,1)}, u32[]{:S(2)}) copy-start(bf16[1024,64]{0,1:T(8,128)(2,1)} %param.14) | copy-start | bytes 393220

commit v5 on v4

--- a/solution.py
+++ b/solution.py
@@ -118,10 +118,13 @@
         send_order(order_ref[1:2, :], scaled, refs[-1])
 
 
-def place_kernel(n, rows, me_ref, map_ref, ci_ref, vi_ref, ce_ref, ve_ref, slot_ref, gap_ref):
+def place_kernel(n, rows, me_ref, map_ref, ci_ref, vi_ref, ce_ref, ve_ref, trial_ref, slot_ref, base_ref):
     per_peer = rows // n
     lanes = rows // 128
-    gap_ref[...] = lookup(ce_ref, ci_ref[...]) - lookup(ve_ref, vi_ref[...])
+    gap = lookup(ce_ref, ci_ref[...]) - lookup(ve_ref, vi_ref[...])
+    for c in range(lanes):
+        part = slice(c * 128, (c + 1) * 128)
+        base_ref[:, part] = gap[c : c + 1, :] * trial_ref[:, part].astype(F32)
     grid = jnp.concatenate([map_ref[pl.ds(c, n, stride=lanes), :] for c in range(lanes)], axis=1)
     slots = grid - me_ref[0] * rows
     lands = (slots >= 0) & (slots < rows)
@@ -192,7 +195,7 @@
         copy.wait()
 
 
-def final_kernel(n, m, arrived_ref, slot_ref, gap_ref, trial_ref, out_ref, row_ref):
+def final_kernel(n, m, arrived_ref, slot_ref, base_ref, out_hbm, row_ref, out_ref, sems):
     width = out_ref.shape[1]
     half, pair = arrived_ref.shape[1:]
     for q in range(n):
@@ -201,18 +204,19 @@
             total = total + arrived_ref[q * m + k].astype(F32)
         at = (q & 1) * half
         row_ref[at : at + half, (q // 2) * pair : (q // 2 + 1) * pair] = total.astype(BF16)
+    copies = []
     slot = slot_ref[...]
     lane = lax.broadcasted_iota(jnp.int32, slot.shape, 1).astype(F32)
     for c in range(0, width // 128, 2):
         lands = jnp.concatenate(
             [jnp.where(slot == lane + 128.0 * (c + k), 1.0, 0.0).astype(BF16) for k in range(2)], axis=1)
         moved = jnp.dot(row_ref[...], lands, preferred_element_type=F32)
-        for k in range(2):
-            part = slice((c + k) * 128, (c + k + 1) * 128)
-            gap = gap_ref[c + k : c + k + 1, :]
-            out_ref[:, part] = (
-                gap * trial_ref[:, part].astype(F32) + moved[:, k * 128 : (k + 1) * 128]
-            ).astype(BF16)
+        part = pl.ds(c * 128, 256)
+        out_ref[:, part] = (base_ref[:, part] + moved).astype(BF16)
+        copies.append(pltpu.make_async_copy(out_ref.at[:, part], out_hbm.at[:, part], sems.at[c // 2]))
+        copies[-1].start()
+    for copy in copies:
+        copy.wait()
 
 
 def per_device(
@@ -378,13 +382,13 @@
         name="tiles",
     )(me, mat_val, screen, mine, theirs)
 
-    slot, gap = pl.pallas_call(
+    slot, base = pl.pallas_call(
         lambda *refs: place_kernel(n, rows, *refs),
-        in_specs=[SCALAR] + [WHOLE] * 5,
+        in_specs=[SCALAR] + [WHOLE] * 6,
         out_specs=(WHOLE, WHOLE),
         out_shape=(
             jax.ShapeDtypeStruct((rows, 128), F32),
-            jax.ShapeDtypeStruct((rows // 128, 128), F32),
+            jax.ShapeDtypeStruct((vecs, rows), F32),
         ),
         cost_estimate=pl.CostEstimate(
             flops=8 * rows * rows, bytes_accessed=2 * rows * rows, transcendentals=0),
@@ -397,6 +401,7 @@
         val_index.reshape(-1, 128),
         cond_energy.reshape(-1, 128),
         val_energy.reshape(-1, 128),
+        trial_rows.T,
     )
 
     if per_peer % 128 != 0:
@@ -405,15 +410,19 @@
     parts, layers = (n, m) if per_peer % 128 == 0 else (2, 1)
     response = pl.pallas_call(
         lambda *refs: final_kernel(parts, layers, *refs),
-        in_specs=[WHOLE] * 4,
-        out_specs=WHOLE,
+        in_specs=[WHOLE] * 3,
+        out_specs=pl.BlockSpec(memory_space=pltpu.HBM),
         compiler_params=roomy(8),
         out_shape=jax.ShapeDtypeStruct((vecs, rows), BF16),
-        scratch_shapes=[pltpu.VMEM((vecs, rows), BF16)],
+        scratch_shapes=[
+            pltpu.VMEM((vecs, rows), BF16),
+            pltpu.VMEM((vecs, rows), BF16),
+            pltpu.SemaphoreType.DMA((rows // 256,)),
+        ],
         cost_estimate=pl.CostEstimate(
             flops=2 * rows * rows * vecs, bytes_accessed=2 * rows * rows, transcendentals=0),
         name="final",
-    )(arrived, slot, gap, trial_rows.T)
+    )(arrived, slot, base)
     return (response.T, tiles)
 
 

time: 45.9 us -> 45.9 us (level)
  no operation moved by 1% of the time
where the time goes in v5:
time: 45.9 us; the launch traced here: 45.5 us
  starting transfers between devices  17.8 us (39%)
  waiting for transfers between devices  13.5 us (29%)
  Pallas kernels  13.1 us (29%)
  between operations  0.92 us (2%)
    all_to_all x1, waiting for transfers between devices, per_device(): lax.all_to_all(outgoing, ('pairs', 'rep'), split_axis=0, concat_axis=0, t...  9.41 us
    ppermute x6, starting transfers between devices, exchange(): return lax.ppermute(x, 'pairs', [(i, i ^ mask) for i in range(size)])  7.33 us
    ppermute x3, starting transfers between devices, per_device(): lax.ppermute(trial_cols.T, 'rep', [(i, (i + k) % m) for i in range(m)])  4.65 us
    all_to_all x1, starting transfers between devices, per_device(): lax.all_to_all(outgoing, ('pairs', 'rep'), split_axis=0, concat_axis=0, t...  4.22 us
    ppermute x6, waiting for transfers between devices, exchange(): return lax.ppermute(x, 'pairs', [(i, i ^ mask) for i in range(size)])  4.07 us
    pallas_call x1, Pallas kernels, per_device(): pl.pallas_call(tile_kernel, grid_spec=pltpu.PrefetchScalarGridSpec(num_sc...  3.87 us
    ppermute x2, starting transfers between devices, split_exchange(): lax.ppermute(x, 'pairs', [(i, i ^ (odd_mask if i & 1 else even_mask)) for...  1.56 us
    pallas_call x1, Pallas kernels, per_device(): pl.pallas_call(lambda *refs: apply_kernel(m, n, *refs), in_specs=[SCALAR]...  1.55 us
  transfers between devices with their start and end apart: 12, of which 4 were waited for; matrix products, arithmetic and copies ran while one was open for 0% of the time, Pallas kernels for 23%

profile of v5, /device:TPU:1, one launch (start us, length us, event | category | flops | bytes accessed | tf_op | source)
XLA Modules:
  0.0 45.5 jit_solution(9824731590859749143)
XLA Ops:
  0.6 4.2 %collective-permute-start = (bf16[64,128]{1,0:T(8,128)(2,1)}, bf16[64,128]{1,0:T(8,128)(2,1)S(1)}, u32[]{:S(2)}, u32[]{:S(2)}) collective-permute-start(bf16[64,128]{1,0:T(8,128)(2,1)} %bitcast.43), channel_id=1, source_target_pairs={{0,3},{1,0},{2,1},{3,2},{4,7},{5,4},{6,5},{7,6},{8,11},{9,8},{10,9... | collective-permute-start | bytes 49160 | tf_op jit(solution)/shard_map/ppermute | solution.py:269
  4.8 0.5 collective-permute-start.2
  5.3 1.2 %collective-permute-start.6 = (bf16[128,512]{1,0:T(8,128)(2,1)}, bf16[128,512]{1,0:T(8,128)(2,1)S(1)}, u32[]{:S(2)}, u32[]{:S(2)}) collective-permute-start(bf16[128,512]{1,0:T(8,128)(2,1)} %cond_hbm.1), channel_id=1, source_target_pairs={{0,8},{4,20},{8,0},{12,28},{16,24},{20,4},{24,16},{28,12},{1,9},{5... | collective-permute-start | bytes 393224 | tf_op jit(solution)/shard_map/ppermute | solution.py:25
  6.5 1.8 %collective-permute-start.9 = (bf16[1024,512]{1,0:T(8,128)(2,1)}, bf16[1024,512]{1,0:T(8,128)(2,1)S(1)}, u32[]{:S(2)}, u32[]{:S(2)}) collective-permute-start(bf16[1024,512]{1,0:T(8,128)(2,1)} %val_ref.1), channel_id=1, source_target_pairs={{0,4},{4,0},{8,12},{12,8},{16,20},{20,16},{24,28},{28,24},{1,5},{5... | collective-permute-start | bytes 3145736 | tf_op jit(solution)/shard_map/ppermute | solution.py:20
  8.3 0.9 %fetch.1 = (bf16[64,128]{1,0:T(8,128)(2,1)S(1)}, bf16[128,512]{1,0:T(8,128)(2,1)S(1)}) custom-call(bf16[64,128]{1,0:T(8,128)(2,1)} %bitcast.46, bf16[128,512]{1,0:T(8,128)(2,1)} %cond_hbm.1), custom_call_target="tpu_custom_call" | custom-call | bytes 262144 | tf_op jit(solution)/shard_map/fetch/pallas_call | solution.py:254
  9.3 1.5 %load.1 = (bf16[1024,512]{1,0:T(8,128)(2,1)S(1)}, s32[2,1024]{1,0:T(2,128)S(1)}, f32[1,512]{1,0:T(1,128)S(1)}) custom-call(s32[1]{0:T(128)} %bitcast.refs_0_.me_ref, s32[64,128]{1,0:T(8,128)} %bitcast.30, bf16[1024,512]{1,0:T(8,128)(2,1)} %val_ref.1, f32[1,512]{1,0:T(1,128)} %bitcast.32), custom_call_target="tpu_custom_call" | custom-call | flops 524288 | bytes 2097152 | tf_op jit(solution)/shard_map/load/pallas_call | solution.py:285
  10.9 0.3 collective-permute-start.7
  11.2 2.2 %collective-permute-start.5 = (bf16[256,128]{1,0:T(8,128)(2,1)S(1)}, bf16[256,128]{1,0:T(8,128)(2,1)S(1)}, u32[]{:S(2)}, u32[]{:S(2)}) collective-permute-start(bf16[256,128]{1,0:T(8,128)(2,1)S(1)} %get-tuple-element.23), channel_id=1, source_target_pairs={{0,24},{4,28},{8,16},{12,20},{16,8},{20,12},{24,0},{28,4},{1,25},{... | collective-permute-start | bytes 196616 | tf_op jit(solution)/shard_map/ppermute | solution.py:20
  13.5 0.2 collective-permute-start.4
  13.7 0.3 collective-permute-start.3
  14.0 1.3 %sent0.1.refs_3_ = bf16[1024,512]{1,0:T(8,128)(2,1)S(1)} custom-call(s32[2,1024]{1,0:T(2,128)S(1)} %get-tuple-element.15.order_ref.refs_1_, bf16[1024,512]{1,0:T(8,128)(2,1)S(1)} %get-tuple-element.16.scaled_ref), custom_call_target="tpu_custom_call" | custom-call | flops 1073741824 | bytes 2097152 | tf_op jit(solution)/shard_map/sent0/pallas_call | solution.py:306
  15.2 3.4 %collective-permute-done.5 = bf16[256,128]{1,0:T(8,128)(2,1)S(1)} collective-permute-done((bf16[256,128]{1,0:T(8,128)(2,1)S(1)}, bf16[256,128]{1,0:T(8,128)(2,1)S(1)}, u32[]{:S(2)}, u32[]{:S(2)}) %collective-permute-start.5) | collective-permute-done | bytes 65568 | tf_op jit(solution)/shard_map/ppermute | solution.py:20
  18.6 0.2 collective-permute-done.4
  19.0 0.3 mixed.1
  19.3 2.5 %collective-permute-start.8 = (bf16[128,512]{1,0:T(8,128)(2,1)S(1)}, bf16[128,512]{1,0:T(8,128)(2,1)S(1)}, u32[]{:S(2)}, u32[]{:S(2)}) collective-permute-start(bf16[128,512]{1,0:T(8,128)(2,1)S(1)} %get-tuple-element.14), channel_id=1, source_target_pairs={{0,4},{4,0},{8,12},{12,8},{16,20},{20,16},{24,28},{28,24},{1,5},{5... | collective-permute-start | bytes 393224 | tf_op jit(solution)/shard_map/ppermute | solution.py:20
  21.8 1.3 %shard_map.113.refs_4_ = bf16[1024,512]{1,0:T(8,128)(2,1)S(1)} custom-call(s32[1]{0:T(128)} %bitcast.refs_0_.me_ref, s32[2,1024]{1,0:T(2,128)S(1)} %get-tuple-element.15.order_ref.refs_1_, f32[1,512]{1,0:T(1,128)S(1)} %get-tuple-element.17.refs_2_, bf16[1024,512]{1,0:T(8,128)(2,1)S(1)} %collective-permute-done.9.refs_3_), custom_call_target="tpu_custom_call" | custom-call | flops 1073741824 | bytes 2097152 | tf_op jit(solution)/shard_map/pallas_call | solution.py:317
  23.3 1.5 %apply.1 = bf16[32,32,256]{2,1,0:T(8,128)(2,1)} custom-call(s32[1]{0:T(128)} %bitcast.refs_0_.me_ref, f32[128,512]{1,0:T(8,128)S(1)} %get-tuple-element.13.refs_1_, bf16[128,512]{1,0:T(8,128)(2,1)S(1)} %collective-permute-done.8.refs_2_, bf16[1024,512]{1,0:T(8,128)(2,1)S(1)} %sent0.1.refs_3_, bf16[1024,512]{1,0:T(8,128)(2,1)S(1)} %shard_map.114.refs_4_), custom_call_target="tpu_custom_call" | custom-call | flops 268435456 | bytes 2097152 | tf_op jit(solution)/shard_map/apply/pallas_call | solution.py:343
  24.8 4.2 %all-to-all-start = ((bf16[32,32,256]{2,1,0:T(8,128)(2,1)}), bf16[32,32,256]{2,1,0:T(8,128)(2,1)S(1)}, u32[]{:S(2)}, u32[]{:S(2)}) async-start(bf16[32,32,256]{2,1,0:T(8,128)(2,1)} %apply.1), calls=%async_computation | async-start | bytes 1048576 | tf_op jit(solution)/shard_map/all_to_all | solution.py:362
  29.1 0.3 collective-permute-start.10
  29.4 1.1 %place.1 = (f32[1024,128]{1,0:T(8,128)S(1)}, f32[64,1024]{1,0:T(8,128)S(1)}) custom-call(s32[1]{0:T(128)} %bitcast.refs_0_.me_ref, s32[64,128]{1,0:T(8,128)S(1)} %bitcast.31, s32[8,128]{1,0:T(8,128)S(1)} %bitcast.34, s32[8,128]{1,0:T(8,128)S(1)} %bitcast.35, f32[2,128]{1,0:T(2,128)S(1)} %bitcast.36, f32[1,128]{1,0:T(1,128)S(1)} %bitcast.37, ...), custom_call_target="tpu_custom_call" | custom-call | flops 8388608 | bytes 2097152 | tf_op jit(solution)/shard_map/place/pallas_call | solution.py:385
  30.5 0.5 %collective-permute-done.10.theirs_ref = bf16[4,128,512]{2,1,0:T(8,128)(2,1)S(1)} collective-permute-done((bf16[4,128,512]{2,1,0:T(8,128)(2,1)S(1)}, bf16[4,128,512]{2,1,0:T(8,128)(2,1)S(1)}, u32[]{:S(2)}, u32[]{:S(2)}) %collective-permute-start.10) | collective-permute-done | bytes 524320 | tf_op jit(solution)/shard_map/ppermute | solution.py:20
  31.1 3.9 %tiles.1 = bf16[1,1024,1024]{2,1,0:T(8,128)(2,1)} custom-call(s32[1]{0:T(128)} %bitcast.refs_0_.me_ref, bf16[1024,512]{1,0:T(8,128)(2,1)S(1)} %copy-done, f32[1,512]{1,0:T(1,128)S(1)} %bitcast.33, bf16[4,128,512]{2,1,0:T(8,128)(2,1)S(1)} %pad_maximum_fusion.refs_2_.mine_ref, bf16[4,128,512]{2,1,0:T(8,128)(2,1)S(1)} %collective-permute-done.10.theirs_ref), custom_call_target="tpu_custom_call" | custom-call | flops 1073741824 | bytes 3145728 | tf_op jit(solution)/shard_map/tiles/pallas_call | solution.py:365
  34.9 9.4 %all-to-all-done.refs_0_ = bf16[32,32,256]{2,1,0:T(8,128)(2,1)S(1)} async-done(((bf16[32,32,256]{2,1,0:T(8,128)(2,1)}), bf16[32,32,256]{2,1,0:T(8,128)(2,1)S(1)}, u32[]{:S(2)}, u32[]{:S(2)}) %all-to-all-start) | async-done | bytes 524320 | tf_op jit(solution)/shard_map/all_to_all | solution.py:362
  44.3 1.2 %final.1 = bf16[64,1024]{1,0:T(8,128)(2,1)} custom-call(bf16[32,32,256]{2,1,0:T(8,128)(2,1)S(1)} %all-to-all-done.refs_0_, f32[1024,128]{1,0:T(8,128)S(1)} %get-tuple-element.18.refs_1_, f32[64,1024]{1,0:T(8,128)S(1)} %get-tuple-element.19.refs_2_), custom_call_target="tpu_custom_call" | custom-call | flops 134217728 | bytes 2097152 | tf_op jit(solution)/shard_map/final/pallas_call | solution.py:411
  (33 shorter events, 0.3 us)
Async XLA Ops:
  0.6 10.2 %collective-permute-start = (bf16[64,128]{1,0:T(8,128)(2,1)}, bf16[64,128]{1,0:T(8,128)(2,1)S(1)}, u32[]{:S(2)}, u32[]{:S(2)}) collective-permute-start(bf16[64,128]{1,0:T(8,128)(2,1)} %bitcast.43), channel_id=1, source_target_pairs={{0,3},{1,0},{2,1},{3,2},{4,7},{5,4},{6,5},{7,6},{8,11},{9,8},{10,9... | collective-permute-start | bytes 49160 | tf_op jit(solution)/shard_map/ppermute | solution.py:269
  4.8 6.0 %collective-permute-start.1 = (bf16[64,128]{1,0:T(8,128)(2,1)}, bf16[64,128]{1,0:T(8,128)(2,1)S(1)}, u32[]{:S(2)}, u32[]{:S(2)}) collective-permute-start(bf16[64,128]{1,0:T(8,128)(2,1)} %bitcast.44), channel_id=1, source_target_pairs={{0,2},{1,3},{2,0},{3,1},{4,6},{5,7},{6,4},{7,5},{8,10},{9,11},{10,... | collective-permute-start | bytes 49160 | tf_op jit(solution)/shard_map/ppermute | solution.py:269
  4.8 6.0 %collective-permute-start.2 = (bf16[64,128]{1,0:T(8,128)(2,1)}, bf16[64,128]{1,0:T(8,128)(2,1)S(1)}, u32[]{:S(2)}, u32[]{:S(2)}) collective-permute-start(bf16[64,128]{1,0:T(8,128)(2,1)} %bitcast.45), channel_id=1, source_target_pairs={{0,1},{1,2},{2,3},{3,0},{4,5},{5,6},{6,7},{7,4},{8,9},{9,10},{10,1... | collective-permute-start | bytes 49160 | tf_op jit(solution)/shard_map/ppermute | solution.py:269
  5.3 5.6 %collective-permute-start.6 = (bf16[128,512]{1,0:T(8,128)(2,1)}, bf16[128,512]{1,0:T(8,128)(2,1)S(1)}, u32[]{:S(2)}, u32[]{:S(2)}) collective-permute-start(bf16[128,512]{1,0:T(8,128)(2,1)} %cond_hbm.1), channel_id=1, source_target_pairs={{0,8},{4,20},{8,0},{12,28},{16,24},{20,4},{24,16},{28,12},{1,9},{5... | collective-permute-start | bytes 393224 | tf_op jit(solution)/shard_map/ppermute | solution.py:25
  6.5 15.3 %collective-permute-start.9 = (bf16[1024,512]{1,0:T(8,128)(2,1)}, bf16[1024,512]{1,0:T(8,128)(2,1)S(1)}, u32[]{:S(2)}, u32[]{:S(2)}) collective-permute-start(bf16[1024,512]{1,0:T(8,128)(2,1)} %val_ref.1), channel_id=1, source_target_pairs={{0,4},{4,0},{8,12},{12,8},{16,20},{20,16},{24,28},{28,24},{1,5},{5... | collective-permute-start | bytes 3145736 | tf_op jit(solution)/shard_map/ppermute | solution.py:20
  10.9 7.9 %collective-permute-start.7 = (bf16[2,128,512]{2,1,0:T(8,128)(2,1)S(1)}, bf16[2,128,512]{2,1,0:T(8,128)(2,1)S(1)}, u32[]{:S(2)}, u32[]{:S(2)}) collective-permute-start(bf16[2,128,512]{2,1,0:T(8,128)(2,1)S(1)} %pad_maximum_fusion.2), channel_id=1, source_target_pairs={{0,16},{4,12},{8,24},{12,4},{16,0},{20,28},{24,8},{28,20},{1,17},{... | collective-permute-start | bytes 786440 | tf_op jit(solution)/shard_map/ppermute | solution.py:25
  11.2 7.4 %collective-permute-start.5 = (bf16[256,128]{1,0:T(8,128)(2,1)S(1)}, bf16[256,128]{1,0:T(8,128)(2,1)S(1)}, u32[]{:S(2)}, u32[]{:S(2)}) collective-permute-start(bf16[256,128]{1,0:T(8,128)(2,1)S(1)} %get-tuple-element.23), channel_id=1, source_target_pairs={{0,24},{4,28},{8,16},{12,20},{16,8},{20,12},{24,0},{28,4},{1,25},{... | collective-permute-start | bytes 196616 | tf_op jit(solution)/shard_map/ppermute | solution.py:20
  13.5 5.3 %collective-permute-start.4 = (bf16[256,128]{1,0:T(8,128)(2,1)S(1)}, bf16[256,128]{1,0:T(8,128)(2,1)S(1)}, u32[]{:S(2)}, u32[]{:S(2)}) collective-permute-start(bf16[256,128]{1,0:T(8,128)(2,1)S(1)} %get-tuple-element.23), channel_id=1, source_target_pairs={{0,16},{4,20},{8,24},{12,28},{16,0},{20,4},{24,8},{28,12},{1,17},{... | collective-permute-start | bytes 196616 | tf_op jit(solution)/shard_map/ppermute | solution.py:20
  13.7 5.1 %collective-permute-start.3 = (bf16[256,128]{1,0:T(8,128)(2,1)S(1)}, bf16[256,128]{1,0:T(8,128)(2,1)S(1)}, u32[]{:S(2)}, u32[]{:S(2)}) collective-permute-start(bf16[256,128]{1,0:T(8,128)(2,1)S(1)} %get-tuple-element.23), channel_id=1, source_target_pairs={{0,8},{4,12},{8,0},{12,4},{16,24},{20,28},{24,16},{28,20},{1,9},{5... | collective-permute-start | bytes 196616 | tf_op jit(solution)/shard_map/ppermute | solution.py:20
  19.3 4.0 %collective-permute-start.8 = (bf16[128,512]{1,0:T(8,128)(2,1)S(1)}, bf16[128,512]{1,0:T(8,128)(2,1)S(1)}, u32[]{:S(2)}, u32[]{:S(2)}) collective-permute-start(bf16[128,512]{1,0:T(8,128)(2,1)S(1)} %get-tuple-element.14), channel_id=1, source_target_pairs={{0,4},{4,0},{8,12},{12,8},{16,20},{20,16},{24,28},{28,24},{1,5},{5... | collective-permute-start | bytes 393224 | tf_op jit(solution)/shard_map/ppermute | solution.py:20
  23.2 6.2 %copy-start.1 = (bf16[1024,64]{0,1:T(8,128)(2,1)S(1)}, bf16[1024,64]{0,1:T(8,128)(2,1)}, u32[]{:S(2)}) copy-start(bf16[1024,64]{0,1:T(8,128)(2,1)} %param.14) | copy-start | bytes 393220
  23.2 6.2 %copy-start.2 = (s32[8192]{0:T(1024)S(1)}, s32[8192]{0:T(1024)}, u32[]{:S(2)}) copy-start(s32[8192]{0:T(1024)} %param.15) | copy-start | bytes 98308
  23.2 6.2 %copy-start.4 = (s32[1024]{0:T(1024)S(1)}, s32[1024]{0:T(1024)}, u32[]{:S(2)}) copy-start(s32[1024]{0:T(1024)} %param.17) | copy-start | bytes 12292
  23.2 6.2 %copy-start.5 = (s32[1024]{0:T(1024)S(1)}, s32[1024]{0:T(1024)}, u32[]{:S(2)}) copy-start(s32[1024]{0:T(1024)} %param.16) | copy-start | bytes 12292
  23.2 6.2 %copy-start.6 = (f32[256]{0:T(256)S(1)}, f32[256]{0:T(256)}, u32[]{:S(2)}) copy-start(f32[256]{0:T(256)} %param.19) | copy-start | bytes 3076
  23.2 6.2 %copy-start.7 = (f32[128]{0:T(128)S(1)}, f32[128]{0:T(128)}, u32[]{:S(2)}) copy-start(f32[128]{0:T(128)} %param.18) | copy-start | bytes 1540
  23.3 7.8 %copy-start = (bf16[1024,512]{1,0:T(8,128)(2,1)S(1)}, bf16[1024,512]{1,0:T(8,128)(2,1)}, u32[]{:S(2)}) copy-start(bf16[1024,512]{1,0:T(8,128)(2,1)} %val_ref.1) | copy-start | bytes 3145732
  23.3 7.8 %copy-start.3 = (f32[512]{0:T(512)S(1)}, f32[512]{0:T(512)}, u32[]{:S(2)}) copy-start(f32[512]{0:T(512)} %param.12) | copy-start | bytes 6148
  24.8 19.5 %all-to-all-start = ((bf16[32,32,256]{2,1,0:T(8,128)(2,1)}), bf16[32,32,256]{2,1,0:T(8,128)(2,1)S(1)}, u32[]{:S(2)}, u32[]{:S(2)}) async-start(bf16[32,32,256]{2,1,0:T(8,128)(2,1)} %apply.1), calls=%async_computation | async-start | bytes 1048576 | tf_op jit(solution)/shard_map/all_to_all | solution.py:362
  29.1 2.0 %collective-permute-start.10 = (bf16[4,128,512]{2,1,0:T(8,128)(2,1)S(1)}, bf16[4,128,512]{2,1,0:T(8,128)(2,1)S(1)}, u32[]{:S(2)}, u32[]{:S(2)}) collective-permute-start(bf16[4,128,512]{2,1,0:T(8,128)(2,1)S(1)} %pad_maximum_fusion.refs_2_.mine_ref), channel_id=1, source_target_pairs={{0,4},{4,0},{8,12},{12,8},{16,20},{20,16},{24,28},{28,24},{1,5},{5... | collective-permute-start | bytes 1572872 | tf_op jit(solution)/shard_map/ppermute | solution.py:20
